TPU v7x, 32 devices: a whole 2x2x4 slice. The times are simulated.
32 devices in a mesh: step: 8 (over y, x, core), rows: 4 (over z).
Axes of the slice: x: 2, y: 2, z: 4, core: 2. Of those that a mesh axis runs over, the one named last changes fastest.
Arguments:
- init_states: float32 [8, 1, 2, 77, 384], P('step', None, None, None, 'rows'), may hold values from -63 to 63
- forcing: float32 [8, 1, 4, 384], P('step', None, None, 'rows'), may hold values from -63 to 63
- history: int32 [8, 1], P('step'), may hold values from 1 to 2
- land_mask: int32 [384], P('rows'), may hold values 0 or 1
- w_in: float32 [800, 158], replicated, may hold values from -0.5 to 0.5
- b_in: float32 [800], replicated, may hold values from -1.5 to 1.5
- w_dw: float32 [800, 7, 7], replicated, may hold values from -0.875 to 0.875
- bn_gain: float32 [800], replicated, may hold values from 0.5 to 1.5
- bn_bias: float32 [800], replicated, may hold values from -1.5 to 1.5
- w_up: float32 [3200, 800], replicated, may hold values from -0.21875 to 0.21875
- b_up: float32 [3200], replicated, may hold values from -1.5 to 1.5
- w_down: float32 [800, 3200], replicated, may hold values from -0.109375 to 0.109375
- b_down: float32 [800], replicated, may hold values from -1.5 to 1.5
- w_out: float32 [77, 800], replicated, may hold values from -0.21875 to 0.21875
- b_out: float32 [77], replicated, may hold values from -1.5 to 1.5
- cotangent: float32 [8, 8, 1, 77, 384], P('step', None, None, None, 'rows'), may hold values from -6 to 6
Outputs:
- predicted: float32 [8, 8, 1, 77, 384], P('step', None, None, None, 'rows')
- grad_init: float32 [8, 1, 2, 77, 384], P('step', None, None, None, 'rows')
- grad_forcing: float32 [8, 1, 4, 384], P('step', None, None, 'rows')
- grad_w_in: float32 [800, 158], replicated
- grad_b_in: float32 [800], replicated
- grad_w_dw: float32 [800, 7, 7], replicated
- grad_bn_gain: float32 [800], replicated
- grad_bn_bias: float32 [800], replicated
- grad_w_up: float32 [3200, 800], P('step', 'rows')
- grad_b_up: float32 [3200], replicated
- grad_w_down: float32 [800, 3200], P('rows', 'step')
- grad_b_down: float32 [800], replicated
- grad_w_out: float32 [77, 800], replicated
- grad_b_out: float32 [77], replicated
All inputs are finite; a program needn't handle non-finite values. No bound on the sum of `land_mask` on one device may be relied on, other than what follows from the above.
Results may differ from a plain program's by a relative error of at most 0.0003.
Values sent between devices are 32-bit elements; how exact they have to be, the bound alone decides.
No kernel may reach another device: no remote copies, remote signals or barrier semaphores. Data moves between devices by JAX's collectives and lax.ppermute only.
A program may use at most 448 MiB of HBM per device.

v0:
```python
import jax
import jax.numpy as jnp
from jax import lax
from jax.sharding import PartitionSpec as P

HALO = 3
ROLL = 8
COLS = 32


EPSILON = 1e-05
HIGHEST = lax.Precision.HIGHEST


def padded(cells, sides, width):
    for axis, dim in sides:
        count = lax.axis_size(axis)
        ends = count - 1
        head = lax.slice_in_dim(cells, 0, width, axis=dim)
        tail = lax.slice_in_dim(cells, cells.shape[dim] - width, cells.shape[dim], axis=dim)
        cells = jnp.concatenate(
            [
                lax.ppermute(tail, axis, [(i, (i + 1) % count) for i in range(ends)]),
                cells,
                lax.ppermute(head, axis, [((i + 1) % count, i) for i in range(ends)]),
            ],
            axis=dim,
        )
    return cells


def passed_along(x, axis, by):
    devices = lax.axis_size(axis)
    return lax.ppermute(x, axis, [(i, (i + by) % devices) for i in range(devices)])


def gelu_exact(values):
    return jax.nn.gelu(values, approximate=False)


def depthwise(extended, kernel):
    kernel_width = kernel.shape[-1]
    reach_rows = kernel_width // 2
    rows_out = extended.shape[-1] // COLS - 2 * reach_rows
    column = jnp.arange(extended.shape[-1]) % COLS
    accumulated = jnp.zeros(extended.shape[:-1] + (rows_out * COLS,), jnp.float32)
    for tap_col in range(kernel_width):
        offset = tap_col - reach_rows
        shifted = jnp.roll(extended, -offset, axis=-1)
        inside = (column + offset >= 0) & (column + offset < COLS)
        shifted = jnp.where(inside, shifted, jnp.zeros_like(shifted))
        for tap_row in range(kernel_width):
            piece = shifted[..., tap_row * COLS : (tap_row + rows_out) * COLS]
            accumulated = accumulated + kernel[:, tap_row, tap_col, None] * piece
    return accumulated


def contract(weights, values):
    return jnp.einsum("dc,bcp->bdp", weights, values, precision=HIGHEST)


def transposed(weights, values):
    return jnp.einsum("dc,bdp->bcp", weights, values, precision=HIGHEST)


def outer_sum(first_factor, second_factor):
    return jnp.einsum("bdp,bcp->dc", first_factor, second_factor, precision=HIGHEST)


def reduce_forces(grad_forces):
    accumulated = grad_forces[0]
    for grad_force in grad_forces[1:]:
        accumulated = accumulated + grad_force
    return accumulated


def per_device(
    init_states,
    forcing,
    history,
    land_mask,
    w_in,
    b_in,
    w_dw,
    bn_gain,
    bn_bias,
    w_up,
    b_up,
    w_down,
    b_down,
    w_out,
    b_out,
    cotangent,
):
    ocean_mask = land_mask.astype(jnp.float32)
    local_count = jnp.sum(ocean_mask)
    states = w_out.shape[0]
    rim_cells = HALO * COLS

    def backward_tick(grad_new, kept_tick, grad_list):
        inputs_all, lifted_ext, normalized, inverse_std, ocean_count, residual = kept_tick
        (
            grad_w_in,
            grad_b_in,
            grad_w_dw,
            grad_bn_gain,
            grad_bn_bias,
            grad_w_up,
            grad_b_up,
            grad_w_down,
            grad_b_down,
            grad_w_out,
            grad_b_out,
        ) = grad_list
        grad_masked = grad_new * ocean_mask
        grad_b_out = grad_b_out + jnp.sum(grad_masked, axis=(0, 2))
        grad_w_out = grad_w_out + outer_sum(grad_masked, residual)
        grad_branch = transposed(w_out, grad_masked) * ocean_mask
        normed = normalized * bn_gain[:, None] + bn_bias[:, None]
        hidden_pre = contract(w_up, normed) + b_up[:, None]
        activated, gelu_back = jax.vjp(gelu_exact, hidden_pre)
        grad_b_down = grad_b_down + jnp.sum(grad_branch, axis=(0, 2))
        grad_w_down = grad_w_down + outer_sum(grad_branch, activated)
        grad_hidden = gelu_back(transposed(w_down, grad_branch))[0]
        grad_b_up = grad_b_up + jnp.sum(grad_hidden, axis=(0, 2))
        grad_w_up = grad_w_up + outer_sum(grad_hidden, normed)
        grad_normed = transposed(w_up, grad_hidden)
        local_bias = jnp.sum(grad_normed, axis=-1)
        local_gain = jnp.sum(grad_normed * normalized, axis=-1)
        grad_bn_bias = grad_bn_bias + jnp.sum(local_bias, axis=0)
        grad_bn_gain = grad_bn_gain + jnp.sum(local_gain, axis=0)
        total_bias, total_gain = lax.psum((local_bias, local_gain), "rows")
        correction = (
            ocean_mask * (total_bias[..., None] + normalized * total_gain[..., None]) / ocean_count
        )
        grad_mixed = inverse_std[..., None] * bn_gain[:, None] * (grad_normed - correction)
        grad_ext = padded(grad_mixed, (("rows", 2),), rim_cells)
        grad_lifted = depthwise(grad_ext, w_dw[:, ::-1, ::-1]) + grad_branch
        unused_out, kernel_back = jax.vjp(lambda kernel: depthwise(lifted_ext, kernel), w_dw)
        grad_w_dw = grad_w_dw + kernel_back(grad_mixed)[0]
        grad_b_in = grad_b_in + jnp.sum(grad_lifted, axis=(0, 2))
        grad_w_in = grad_w_in + outer_sum(grad_lifted, inputs_all)
        grad_inputs = transposed(w_in, grad_lifted)
        grad_list = (
            grad_w_in,
            grad_b_in,
            grad_w_dw,
            grad_bn_gain,
            grad_bn_bias,
            grad_w_up,
            grad_b_up,
            grad_w_down,
            grad_b_down,
            grad_w_out,
            grad_b_out,
        )
        return (
            grad_inputs[:, :states],
            grad_inputs[:, states : 2 * states],
            grad_inputs[:, 2 * states :],
            grad_list,
        )

    forcings = [forcing[0] for rollout_step in range(ROLL)]
    cotangents = [cotangent[0, rollout_step] for rollout_step in range(ROLL)]
    current = init_states[0, :, 1]
    previous = jnp.where(
        (history[0] == 2)[:, None, None], init_states[0, :, 0], init_states[0, :, 1]
    )
    outputs = []
    kept_all = []
    for rollout_step in range(ROLL):
        if rollout_step > 0:
            current, previous = passed_along((outputs[-1], current), "step", 1)
        inputs_all = jnp.concatenate([previous, current, forcings[rollout_step]], axis=1)
        lifted = contract(w_in, inputs_all) + b_in[:, None]
        forward_lifted_ext = padded(lifted, (("rows", 2),), rim_cells)
        mixed_cells = depthwise(forward_lifted_ext, w_dw)
        first_sum = jnp.sum(mixed_cells * ocean_mask, axis=-1)
        second_sum = jnp.sum(mixed_cells * mixed_cells * ocean_mask, axis=-1)
        first_total, second_total, forward_ocean_count = lax.psum(
            (first_sum, second_sum, local_count), "rows"
        )
        forward_ocean_count = jnp.maximum(forward_ocean_count, 1.0)
        average = first_total / forward_ocean_count
        variance = second_total / forward_ocean_count - average * average
        forward_inverse_std = lax.rsqrt(variance + EPSILON)
        forward_normalized = (mixed_cells - average[..., None]) * forward_inverse_std[..., None]
        forward_normed = forward_normalized * bn_gain[:, None] + bn_bias[:, None]
        forward_hidden_pre = contract(w_up, forward_normed) + b_up[:, None]
        branch = contract(w_down, gelu_exact(forward_hidden_pre)) + b_down[:, None]
        forward_residual = (lifted + branch) * ocean_mask
        new_state = (contract(w_out, forward_residual) + b_out[:, None]) * ocean_mask
        new_state, kept_tick = (
            new_state,
            (
                inputs_all,
                forward_lifted_ext,
                forward_normalized,
                forward_inverse_std,
                forward_ocean_count,
                forward_residual,
            ),
        )
        outputs.append(new_state)
        kept_all.append(kept_tick)
    grad_list = (
        jnp.zeros_like(w_in),
        jnp.zeros_like(b_in),
        jnp.zeros_like(w_dw),
        jnp.zeros_like(bn_gain),
        jnp.zeros_like(bn_bias),
        jnp.zeros_like(w_up),
        jnp.zeros_like(b_up),
        jnp.zeros_like(w_down),
        jnp.zeros_like(b_down),
        jnp.zeros_like(w_out),
        jnp.zeros_like(b_out),
    )
    grad_forces = [None] * ROLL
    sent_cur = None
    sent_prev = None
    for rollout_step in reversed(range(ROLL)):
        grad_new = cotangents[rollout_step]
        if rollout_step < ROLL - 1:
            came_cur, came_prev = passed_along((sent_cur, sent_prev), "step", -1)
            grad_new = grad_new + came_cur
        grad_prev, grad_cur, grad_force, grad_list = backward_tick(
            grad_new, kept_all[rollout_step], grad_list
        )
        if rollout_step < ROLL - 1:
            grad_cur = grad_cur + came_prev
        sent_cur, sent_prev = (grad_cur, grad_prev)
        grad_forces[rollout_step] = grad_force
    single_history = (history[0] == 1)[:, None, None]
    double_history = (history[0] == 2)[:, None, None]
    grad_init_cur = sent_cur + jnp.where(single_history, sent_prev, jnp.zeros_like(sent_prev))
    grad_init_prev = jnp.where(double_history, sent_prev, jnp.zeros_like(sent_prev))
    grad_init = jnp.stack([grad_init_prev, grad_init_cur], axis=1)[None]
    predicted = jnp.stack(outputs, axis=0)[None]
    grad_forcing = reduce_forces(grad_forces)[None]
    (
        grad_w_in,
        grad_b_in,
        grad_w_dw,
        grad_bn_gain,
        grad_bn_bias,
        grad_w_up,
        grad_b_up,
        grad_w_down,
        grad_b_down,
        grad_w_out,
        grad_b_out,
    ) = grad_list
    small_totals = lax.psum(
        (
            grad_w_in,
            grad_b_in,
            grad_w_dw,
            grad_bn_gain,
            grad_bn_bias,
            grad_b_up,
            grad_b_down,
            grad_w_out,
            grad_b_out,
        ),
        ("step", "rows"),
    )
    shares = (
        lax.psum_scatter(grad_w_up, "step", scatter_dimension=0, tiled=True),
        lax.psum_scatter(grad_w_down, "step", scatter_dimension=1, tiled=True),
    )
    share_up, share_down = (
        lax.psum_scatter(shares[0], "rows", scatter_dimension=1, tiled=True),
        lax.psum_scatter(shares[1], "rows", scatter_dimension=0, tiled=True),
    )
    return (
        predicted,
        grad_init,
        grad_forcing,
        small_totals[0],
        small_totals[1],
        small_totals[2],
        small_totals[3],
        small_totals[4],
        share_up,
        small_totals[5],
        share_down,
        small_totals[6],
        small_totals[7],
        small_totals[8],
    )


def solution(mesh):
    in_specs = (
        P("step", None, None, None, "rows"),
        P("step", None, None, "rows"),
        P("step", None),
        P("rows"),
        P(),
        P(),
        P(),
        P(),
        P(),
        P(),
        P(),
        P(),
        P(),
        P(),
        P(),
        P("step", None, None, None, "rows"),
    )
    out_specs = (
        P("step", None, None, None, "rows"),
        P("step", None, None, None, "rows"),
        P("step", None, None, "rows"),
        P(),
        P(),
        P(),
        P(),
        P(),
        P("step", "rows"),
        P(),
        P("rows", "step"),
        P(),
        P(),
        P(),
    )
    return jax.shard_map(
        per_device, mesh=mesh, in_specs=in_specs, out_specs=out_specs, check_vma=False
    )
```

profile of v0, /device:TPU:9, one launch (start us, length us, event | category | flops | bytes accessed | tf_op | source)
XLA Modules:
  0.0 1746.8 jit_solution(15639221785140882595)
XLA Ops:
  54.6 16.4 fusion.392
  117.3 16.4 fusion.377
  182.7 16.4 fusion.362
  247.2 16.4 fusion.347
  311.2 16.4 fusion.332
  376.8 16.4 fusion.317
  442.6 16.4 fusion.302
  832.7 13.5 fusion.35
  909.6 13.5 fusion.27
  958.8 13.6 fusion.23
  987.4 14.4 fusion.19
  1013.9 28.3 %add_add_fusion.1 = f32[3200,800]{1,0:T(8,128)} fusion(f32[3200,800]{1,0:T(8,128)} %fusion.19, f32[3200,800]{1,0:T(8,128)} %fusion.23, f32[3200,800]{1,0:T(8,128)} %fusion.27, f32[3200,800]{1,0:T(8,128)} %fusion.31, f32[3200,800]{1,0:T(8,128)} %fusion.35, f32[3200,800]{1,0:T(8,128)S(1)} %bitcast.1892, f32[3200,800]{1,0:T(8,128)} %fusion.39, ...), kind=kOutput, calls=%fused_computation.1 | convolution fusion | flops 2967347200 | bytes 83468800 | tf_op jit(solution)/shard_map/bdp,bcp->dc/dot_general | solution.py:67
  1043.2 13.5 fusion.47
  1056.8 17.4 fusion.57
  1074.2 17.5 %fusion.67 = f32[800,3200]{0,1:T(8,128)} fusion(f32[1,96,3200]{2,1,0:T(8,128)S(1)} %copy-done.228, f32[1,96,800]{2,1,0:T(8,128)S(1)} %copy-done.183), kind=kOutput, calls=%fused_computation.112 | convolution fusion | flops 2968780800 | bytes 11776000 | tf_op jit(solution)/shard_map/bdp,bcp->dc/dot_general | solution.py:67
  1091.7 17.7 %fusion.77 = f32[800,3200]{0,1:T(8,128)} fusion(f32[1,96,3200]{2,1,0:T(8,128)S(1)} %copy-done.225, f32[1,96,800]{2,1,0:T(8,128)S(1)} %copy-done.186), kind=kOutput, calls=%fused_computation.128 | convolution fusion | flops 2968780800 | bytes 11776000 | tf_op jit(solution)/shard_map/bdp,bcp->dc/dot_general | solution.py:67
  1109.4 17.4 fusion.87
  1126.8 17.4 fusion.97
  1144.2 17.6 %fusion.107 = f32[800,3200]{0,1:T(8,128)} fusion(f32[1,96,3200]{2,1,0:T(8,128)S(1)} %copy-done.216, f32[1,96,800]{2,1,0:T(8,128)S(1)} %copy-done.193), kind=kOutput, calls=%fused_computation.176 | convolution fusion | flops 2968780800 | bytes 11776000 | tf_op jit(solution)/shard_map/bdp,bcp->dc/dot_general | solution.py:67
  1161.9 29.4 %add_add_fusion = f32[800,3200]{0,1:T(8,128)} fusion(f32[800,3200]{0,1:T(8,128)} %fusion.107, f32[800,3200]{0,1:T(8,128)} %fusion.97, f32[800,3200]{0,1:T(8,128)} %fusion.87, f32[800,3200]{0,1:T(8,128)} %fusion.77, f32[800,3200]{0,1:T(8,128)} %fusion.67, f32[800,3200]{0,1:T(8,128)S(1)} %fusion.47, f32[800,3200]{0,1:T(8,128)} %fusion.57, ...), kind=kOutput, calls=%fused_computation | convolution fusion | flops 2986700800 | bytes 83456000 | tf_op jit(solution)/shard_map/bdp,bcp->dc/dot_general | solution.py:67
  1224.4 16.7 fusion.287
  1449.8 105.7 %add_add_fusion.2 = f32[800,7,7]{0,2,1:T(8,128)} fusion(f32[800,1,1]{0,2,1:T(1,128)S(1)} %broadcast_in_dim.2494, f32[800,1,1]{0,2,1:T(1,128)S(1)} %broadcast_in_dim.2493, f32[800,1,1]{0,2,1:T(1,128)S(1)} %broadcast_in_dim.2492, f32[800,1,1]{0,2,1:T(1,128)S(1)} %broadcast_in_dim.2491, f32[800,1,1]{0,2,1:T(1,128)S(1)} %broadcast_in_dim.2490, ...), kind=kLoop, calls=%fused_computation.1873 | loop fusion | flops 13720000 | bytes 1587200 | tf_op jit(solution)/shard_map/add | solution.py:140
  1591.6 39.3 %all-reduce.392 = (f32[800]{0:T(1024)}, f32[800]{0:T(1024)}, f32[800]{0:T(1024)}, f32[3200]{0:T(1024)}, f32[800]{0:T(1024)}, /*index=5*/f32[77]{0:T(128)}) all-reduce(f32[800]{0:T(1024)S(1)} %add_add_fusion.8, f32[800]{0:T(1024)S(1)} %add_add_fusion.7, ...), channel_id=1, replica_groups=mesh['step'=8,'rows'=4] {'step','rows'}, use_global_device_ids=true, to_apply=%region_75.76 | all-reduce | flops 6477 | bytes 51816 | tf_op jit(solution)/shard_map/psum | solution.py:255
  1634.2 102.0 %all-reduce.412.cloned.1.call-done = (f32[800,158]{0,1:T(8,128)}, f32[800,7,7]{0,2,1:T(8,128)}, f32[77,800]{1,0:T(8,128)}) async-done(((f32[800,158]{0,1:T(8,128)}, f32[800,7,7]{0,2,1:T(8,128)}, f32[77,800]{1,0:T(8,128)}), (f32[800,158]{0,1:T(8,128)}, f32[800,7,7]{0,2,1:T(8,128)}, f32[77,800]{1,0:T(8,128)})) %all-reduce.412.cloned.1.call-update) | async-done | bytes 908816 | tf_op jit(solution)/shard_map/psum | solution.py:255
  (2062 shorter events, 1111.1 us)
Async XLA Ops:
  8.0 1554.2 %reduce-scatter.9.cloned.1.call-start = ((), (), s32[]{:S(2)}) async-start(), calls=%async_computation.4 | async-start | bytes 12902400 | tf_op jit(solution)/shard_map/reduce_scatter | solution.py:270
  9.2 66.8 %collective-permute-start.2 = (f32[1,77,96]{2,1,0:T(8,128)S(1)}, f32[1,77,96]{2,1,0:T(8,128)S(1)}, u32[]{:S(2)}, u32[]{:S(2)}) collective-permute-start(f32[1,77,96]{2,1,0:T(8,128)S(1)} %bitcast.1912), channel_id=1, source_target_pairs={{0,4},{4,8},{8,12},{12,16},{16,20},{20,24},{24,28},{28,0},{1,5},{5... | collective-permute-start | bytes 88712 | tf_op jit(solution)/shard_map/ppermute | solution.py:34
  82.9 58.6 %collective-permute-start.6 = (f32[1,77,96]{2,1,0:T(8,128)S(1)}, f32[1,77,96]{2,1,0:T(8,128)S(1)}, u32[]{:S(2)}, u32[]{:S(2)}) collective-permute-start(f32[1,77,96]{2,1,0:T(8,128)S(1)} %collective-permute-done.3), channel_id=1, source_target_pairs={{0,4},{4,8},{8,12},{12,16},{16,20},{20,24},{24,28},{28,0},{1,5},{5... | collective-permute-start | bytes 88712 | tf_op jit(solution)/shard_map/ppermute | solution.py:34
  148.5 58.3 %collective-permute-start.10 = (f32[1,77,96]{2,1,0:T(8,128)S(1)}, f32[1,77,96]{2,1,0:T(8,128)S(1)}, u32[]{:S(2)}, u32[]{:S(2)}) collective-permute-start(f32[1,77,96]{2,1,0:T(8,128)S(1)} %collective-permute-done.7), channel_id=1, source_target_pairs={{0,4},{4,8},{8,12},{12,16},{16,20},{20,24},{24,28},{28,0},{1,5},{5... | collective-permute-start | bytes 88712 | tf_op jit(solution)/shard_map/ppermute | solution.py:34
  213.8 57.3 %collective-permute-start.14 = (f32[1,77,96]{2,1,0:T(8,128)S(1)}, f32[1,77,96]{2,1,0:T(8,128)S(1)}, u32[]{:S(2)}, u32[]{:S(2)}) collective-permute-start(f32[1,77,96]{2,1,0:T(8,128)S(1)} %collective-permute-done.11), channel_id=1, source_target_pairs={{0,4},{4,8},{8,12},{12,16},{16,20},{20,24},{24,28},{28,0},{1,5},{5... | collective-permute-start | bytes 88712 | tf_op jit(solution)/shard_map/ppermute | solution.py:34
  278.0 58.1 %collective-permute-start.18 = (f32[1,77,96]{2,1,0:T(8,128)S(1)}, f32[1,77,96]{2,1,0:T(8,128)S(1)}, u32[]{:S(2)}, u32[]{:S(2)}) collective-permute-start(f32[1,77,96]{2,1,0:T(8,128)S(1)} %collective-permute-done.15), channel_id=1, source_target_pairs={{0,4},{4,8},{8,12},{12,16},{16,20},{20,24},{24,28},{28,0},{1,5},{5... | collective-permute-start | bytes 88712 | tf_op jit(solution)/shard_map/ppermute | solution.py:34
  343.1 58.1 %collective-permute-start.22 = (f32[1,77,96]{2,1,0:T(8,128)S(1)}, f32[1,77,96]{2,1,0:T(8,128)S(1)}, u32[]{:S(2)}, u32[]{:S(2)}) collective-permute-start(f32[1,77,96]{2,1,0:T(8,128)S(1)} %collective-permute-done.19), channel_id=1, source_target_pairs={{0,4},{4,8},{8,12},{12,16},{16,20},{20,24},{24,28},{28,0},{1,5},{5... | collective-permute-start | bytes 88712 | tf_op jit(solution)/shard_map/ppermute | solution.py:34
  408.2 59.1 %collective-permute-start.26 = (f32[1,77,96]{2,1,0:T(8,128)S(1)}, f32[1,77,96]{2,1,0:T(8,128)S(1)}, u32[]{:S(2)}, u32[]{:S(2)}) collective-permute-start(f32[1,77,96]{2,1,0:T(8,128)S(1)} %collective-permute-done.23), channel_id=1, source_target_pairs={{0,4},{4,8},{8,12},{12,16},{16,20},{20,24},{24,28},{28,0},{1,5},{5... | collective-permute-start | bytes 88712 | tf_op jit(solution)/shard_map/ppermute | solution.py:34
  615.9 18.1 %collective-permute-start.35 = (f32[1,77,96]{2,1,0:T(8,128)S(1)}, f32[1,77,96]{2,1,0:T(8,128)S(1)}, u32[]{:S(2)}, u32[]{:S(2)}) collective-permute-start(f32[1,77,96]{2,1,0:T(8,128)S(1)} %get-tuple-element.916), channel_id=1, source_target_pairs={{0,28},{4,0},{8,4},{12,8},{16,12},{20,16},{24,20},{28,24},{1,29},{... | collective-permute-start | bytes 88712 | tf_op jit(solution)/shard_map/ppermute | solution.py:34
  675.4 18.3 %collective-permute-start.39 = (f32[1,77,96]{2,1,0:T(8,128)S(1)}, f32[1,77,96]{2,1,0:T(8,128)S(1)}, u32[]{:S(2)}, u32[]{:S(2)}) collective-permute-start(f32[1,77,96]{2,1,0:T(8,128)S(1)} %get-tuple-element.913), channel_id=1, source_target_pairs={{0,28},{4,0},{8,4},{12,8},{16,12},{20,16},{24,20},{28,24},{1,29},{... | collective-permute-start | bytes 88712 | tf_op jit(solution)/shard_map/ppermute | solution.py:34
  735.5 17.8 %collective-permute-start.43 = (f32[1,77,96]{2,1,0:T(8,128)S(1)}, f32[1,77,96]{2,1,0:T(8,128)S(1)}, u32[]{:S(2)}, u32[]{:S(2)}) collective-permute-start(f32[1,77,96]{2,1,0:T(8,128)S(1)} %get-tuple-element.912), channel_id=1, source_target_pairs={{0,28},{4,0},{8,4},{12,8},{16,12},{20,16},{24,20},{28,24},{1,29},{... | collective-permute-start | bytes 88712 | tf_op jit(solution)/shard_map/ppermute | solution.py:34
  753.5 15.4 collective-permute-start.44
  800.5 21.3 %collective-permute-start.46 = (f32[1,800,96]{1,2,0:T(8,128)S(1)}, f32[1,800,96]{1,2,0:T(8,128)S(1)}, u32[]{:S(2)}, u32[]{:S(2)}) collective-permute-start(f32[1,800,96]{1,2,0:T(8,128)S(1)} %get-tuple-element.753), channel_id=1, source_target_pairs={{0,1},{1,2},{2,3},{4,5},{5,6},{6,7},{8,9},{9,10},{10,11},{12,13},{... | collective-permute-start | bytes 921608 | tf_op jit(solution)/shard_map/ppermute | solution.py:23
  802.4 19.4 %collective-permute-start.45 = (f32[1,800,96]{1,2,0:T(8,128)S(1)}, f32[1,800,96]{1,2,0:T(8,128)S(1)}, u32[]{:S(2)}, u32[]{:S(2)}) collective-permute-start(f32[1,800,96]{1,2,0:T(8,128)S(1)} %get-tuple-element.753), channel_id=1, source_target_pairs={{1,0},{2,1},{3,2},{5,4},{6,5},{7,6},{9,8},{10,9},{11,10},{13,12},{... | collective-permute-start | bytes 921608 | tf_op jit(solution)/shard_map/ppermute | solution.py:25
  876.3 22.4 %collective-permute-start.50 = (f32[1,800,96]{1,2,0:T(8,128)S(1)}, f32[1,800,96]{1,2,0:T(8,128)S(1)}, u32[]{:S(2)}, u32[]{:S(2)}) collective-permute-start(f32[1,800,96]{1,2,0:T(8,128)S(1)} %get-tuple-element.754), channel_id=1, source_target_pairs={{0,1},{1,2},{2,3},{4,5},{5,6},{6,7},{8,9},{9,10},{10,11},{12,13},{... | collective-permute-start | bytes 921608 | tf_op jit(solution)/shard_map/ppermute | solution.py:23
  878.5 20.2 %collective-permute-start.49 = (f32[1,800,96]{1,2,0:T(8,128)S(1)}, f32[1,800,96]{1,2,0:T(8,128)S(1)}, u32[]{:S(2)}, u32[]{:S(2)}) collective-permute-start(f32[1,800,96]{1,2,0:T(8,128)S(1)} %get-tuple-element.754), channel_id=1, source_target_pairs={{1,0},{2,1},{3,2},{5,4},{6,5},{7,6},{9,8},{10,9},{11,10},{13,12},{... | collective-permute-start | bytes 921608 | tf_op jit(solution)/shard_map/ppermute | solution.py:25
  953.3 22.7 %collective-permute-start.54 = (f32[1,800,96]{1,2,0:T(8,128)S(1)}, f32[1,800,96]{1,2,0:T(8,128)S(1)}, u32[]{:S(2)}, u32[]{:S(2)}) collective-permute-start(f32[1,800,96]{1,2,0:T(8,128)S(1)} %get-tuple-element.755), channel_id=1, source_target_pairs={{0,1},{1,2},{2,3},{4,5},{5,6},{6,7},{8,9},{9,10},{10,11},{12,13},{... | collective-permute-start | bytes 921608 | tf_op jit(solution)/shard_map/ppermute | solution.py:23
  955.6 20.3 %collective-permute-start.53 = (f32[1,800,96]{1,2,0:T(8,128)S(1)}, f32[1,800,96]{1,2,0:T(8,128)S(1)}, u32[]{:S(2)}, u32[]{:S(2)}) collective-permute-start(f32[1,800,96]{1,2,0:T(8,128)S(1)} %get-tuple-element.755), channel_id=1, source_target_pairs={{1,0},{2,1},{3,2},{5,4},{6,5},{7,6},{9,8},{10,9},{11,10},{13,12},{... | collective-permute-start | bytes 921608 | tf_op jit(solution)/shard_map/ppermute | solution.py:25
  1042.3 533.4 %reduce-scatter.11.cloned.1.call-start = ((), (), s32[]{:S(2)}) async-start(), calls=%async_computation.5 | async-start | bytes 12902400 | tf_op jit(solution)/shard_map/reduce_scatter | solution.py:271
  1191.3 440.9 %reduce-scatter.13.cloned.1.call-start = ((), (), s32[]{:S(2)}) async-start(), calls=%async_computation.6 | async-start | bytes 2048000
  1439.2 119.2 %collective-permute-start.58 = (f32[1,800,96]{1,2,0:T(8,128)S(1)}, f32[1,800,96]{1,2,0:T(8,128)S(1)}, u32[]{:S(2)}, u32[]{:S(2)}) collective-permute-start(f32[1,800,96]{1,2,0:T(8,128)S(1)} %get-tuple-element.756), channel_id=1, source_target_pairs={{0,1},{1,2},{2,3},{4,5},{5,6},{6,7},{8,9},{9,10},{10,11},{12,13},{... | collective-permute-start | bytes 921608 | tf_op jit(solution)/shard_map/ppermute | solution.py:23
  1441.7 116.8 %collective-permute-start.57 = (f32[1,800,96]{1,2,0:T(8,128)S(1)}, f32[1,800,96]{1,2,0:T(8,128)S(1)}, u32[]{:S(2)}, u32[]{:S(2)}) collective-permute-start(f32[1,800,96]{1,2,0:T(8,128)S(1)} %get-tuple-element.756), channel_id=1, source_target_pairs={{1,0},{2,1},{3,2},{5,4},{6,5},{7,6},{9,8},{10,9},{11,10},{13,12},{... | collective-permute-start | bytes 921608 | tf_op jit(solution)/shard_map/ppermute | solution.py:25
  1565.4 170.8 %all-reduce.412.cloned.1.call-start = ((), (), s32[]{:S(2)}) async-start(), calls=%async_computation.8 | async-start | bytes 2121728 | tf_op jit(solution)/shard_map/psum | solution.py:255
  1575.7 160.5 %reduce-scatter.15.cloned.1.call-start = ((), (), s32[]{:S(2)}) async-start(), calls=%async_computation.7 | async-start | bytes 2048000
  (567 other events, 7554.8 us)
Sparse Core Ops, SparseCore 0:
  1042.4 86.2 reduce-scatter.8
  1191.5 86.2 reduce-scatter.10
  1565.5 37.9 reduce-scatter.12
  1606.2 36.2 reduce-scatter.14
Sparse Core Ops, SparseCore 1:
  1575.8 160.3 all-reduce.411
where the time goes:
time: 1760 us; the launch traced here: 1750 us
  matrix products  693 us (39%)
  other arithmetic  298 us (17%)
  local copies, waits for them, and re-layouts  223 us (13%)
  starting transfers between devices  187 us (11%)
  blocking collectives  161 us (9%)
  waiting for transfers between devices  158 us (9%)
  between operations  26.1 us (1%)
    dot_general x32, matrix products, outer_sum(): jnp.einsum('bdp,bcp->dc', first_factor, second_factor, precision=HIGHEST)  288 us
    dot_general x32, matrix products, contract(): return jnp.einsum('dc,bcp->bdp', weights, values, precision=HIGHEST)  224 us
    dot_general x32, matrix products, transposed(): return jnp.einsum('dc,bdp->bcp', weights, values, precision=HIGHEST)  181 us
    broadcast_in_dim x392, local copies, waits for them, and re-layouts, depthwise(): accumulated = accumulated + kernel[:, tap_row, tap_col, None] * piece  178 us
    add x1, other arithmetic, backward_tick(): grad_w_dw = grad_w_dw + kernel_back(grad_mixed)[0]  106 us
    psum x1, waiting for transfers between devices, per_device(): lax.psum((grad_w_in, grad_b_in, grad_w_dw, grad_bn_gain, grad_bn_bias, gr...  102 us
    ppermute x28, starting transfers between devices, passed_along(): lax.ppermute(x, axis, [(i, (i + by) % devices) for i in range(devices)])  101 us
    select_n x109, other arithmetic, depthwise(): shifted = jnp.where(inside, shifted, jnp.zeros_like(shifted))  89.6 us
  transfers between devices with their start and end apart: 65, of which 34 were waited for; matrix products, arithmetic and copies ran while one was open for 54% of the time, Pallas kernels for 0%

commit v1 on v0

v1 whole, which is shorter than its diff:
```python
import functools

import jax
import jax.numpy as jnp
from jax import lax
from jax.experimental import pallas as pl
from jax.experimental.pallas import tpu as pltpu
from jax.sharding import PartitionSpec as P

F32 = jnp.float32
BF16 = jnp.bfloat16
HIGHEST = lax.Precision.HIGHEST
ROLL = 8
COLS = 32
KW = 7
HALO = 3
EPSILON = 1e-05
LANES = 128
CHUNK = 256
SEG = 80
FORCE_LANE = 80
MIB = 2**20

ERF_P = 0.39
ERF_C = (0.23532534, 0.09138764, 0.64956134, -0.63540268, 0.88666585, -0.22753749)


def round_up(value, multiple):
    return -(-value // multiple) * multiple


def split(values):
    high = values.astype(BF16)
    return high, (values - high.astype(F32)).astype(BF16)


def split_outside(values):
    rounded = lax.reduce_precision(values, 8, 7)
    return rounded.astype(BF16), (values - rounded).astype(BF16)


def dot(left, right):
    return jnp.dot(left, right, preferred_element_type=F32)


def dot_t(left, right):
    return lax.dot_general(left, right, (((1,), (1,)), ((), ())), preferred_element_type=F32)


def gelu_both(v):
    e = jnp.exp(v * v * (-0.5))
    t = 1.0 / (1.0 + (ERF_P * 0.7071067811865476) * jnp.abs(v))
    q = 0.5 * ERF_C[5]
    for coefficient in ERF_C[4::-1]:
        q = q * t + 0.5 * coefficient
    q = (q * t) * e
    phi = jnp.where(v >= 0.0, 1.0 - q, q)
    return v * phi, phi + v * (e * 0.3989422804014327)


def depthwise(ext, shifted, kernel, mixed, lanes, flip, rows):
    rows_in = rows + 2 * HALO
    for q in range(KW):
        for r in range(rows_in):
            shifted[q, r] = ext[r, 5 + q : 5 + q + COLS, lanes]
    for v in range(0, COLS, 8):
        total = [None] * rows
        for q in range(KW):
            taps = [
                kernel[(KW * KW - 1 - (p * KW + q)) if flip else (p * KW + q), :, lanes]
                for p in range(KW)
            ]
            for r in range(rows_in):
                cell = shifted[q, r, v : v + 8, :]
                for p in range(KW):
                    i = r - p
                    if 0 <= i < rows:
                        term = taps[p] * cell
                        total[i] = term if total[i] is None else total[i] + term
        for i in range(rows):
            mixed[i, v : v + 8, lanes] = total[i]


def group_lanes(group):
    return pl.ds(pl.multiple_of(group * LANES, LANES), LANES)


def mix_kernel(
    at, cur, cur_edge, prev, prev_edge, force, force_edge, w_in_hi, w_in_lo, b_in, w_oi_hi, w_oi_lo, b_new, taps, ocean,
    mixed_out, stats_out, window_out, x_out, base_out,
    ext, shifted, mixed,
):
    core, part = at[0], at[1]
    px = cur.shape[0]
    edge_px = cur_edge.shape[0]
    rows = px // COLS
    width = mixed_out.shape[1]
    own = jnp.concatenate([prev[...] + force[...], cur[...]], axis=1)
    edge = jnp.concatenate([prev_edge[...] + force_edge[...], cur_edge[...]], axis=1)
    own_hi, own_lo = split(own)
    edge_hi, edge_lo = split(edge)
    both = dot(jnp.concatenate([own_hi, edge_hi, own_lo, edge_lo], axis=0), w_in_hi[...])
    high = dot(jnp.concatenate([own_hi, edge_hi], axis=0), w_in_lo[...])
    lifted = (both[: px + edge_px] + both[px + edge_px :]) + (high + b_in[...])
    base_out[...] = dot(own_hi, w_oi_hi[...]) + dot(own_lo, w_oi_hi[...]) + dot(own_hi, w_oi_lo[...]) + b_new[...]
    zeros = jnp.zeros((rows + 2 * HALO, 8, width), F32)
    ext[:, :8, :] = zeros
    ext[:, 8 + COLS :, :] = zeros
    ext[HALO : HALO + rows, 8 : 8 + COLS, :] = lifted[:px].reshape(rows, COLS, width)
    ext[pl.ds((rows + HALO) * (1 - core), HALO), 8 : 8 + COLS, :] = lifted[px:].reshape(HALO, COLS, width)
    ext[pl.ds((rows + HALO) * core, HALO), 8 : 8 + COLS, :] = jnp.zeros((HALO, COLS, width), F32)
    part_rows = window_out.shape[0] - 2 * HALO
    for i in range(window_out.shape[0]):
        window_out[i] = ext[part * part_rows + i, 8 : 8 + COLS, :]
    part_px = x_out.shape[0]
    first = part == 0
    x_out[...] = jnp.where(first, own[:part_px], own[part_px:])
    mask = ocean[...]

    def group(g, _):
        lanes = group_lanes(g)
        depthwise(ext, shifted, taps, mixed, lanes, False, rows)
        cells = mixed[:, :, lanes].reshape(px, LANES)
        mixed_out[:, lanes] = cells
        masked = cells * mask
        stats_out[0:1, lanes] = jnp.sum(masked, axis=0, keepdims=True)
        stats_out[1:2, lanes] = jnp.sum(masked * cells, axis=0, keepdims=True)
        return 0

    lax.fori_loop(0, width // LANES, group, 0)


def feed_kernel(
    at, mixed, stats, stats_other, count, gain, bias, ocean, base, w_up, b_up, w_od,
    new_out, new_edge_out, norm_out, norm_edge_out, slope_out, act_out, inv_out,
    w_vmem, stack, rem, acc, acc_lo, hold_a, hold_b, hold_act, sems, *, width, k_main, k_rem,
):
    core, part = at[0], at[1]
    px = mixed.shape[0]
    chunks = w_vmem.shape[0] // CHUNK
    part_px = act_out.shape[0]

    def fetch(t):
        rows = pl.ds(pl.multiple_of(t * CHUNK, CHUNK), CHUNK)
        return pltpu.make_async_copy(w_up.at[rows], w_vmem.at[rows], sems.at[t])

    for t in range(chunks):
        fetch(t).start()
    total = count[...]

    for g in range(width // LANES):
        lanes = slice(g * LANES, (g + 1) * LANES)
        cells = mixed[:, lanes]
        average = (stats[0:1, lanes] + stats_other[0:1, lanes]) / total
        variance = (stats[1:2, lanes] + stats_other[1:2, lanes]) / total - average * average
        inverse = lax.rsqrt(variance + EPSILON)
        inv_out[:, lanes] = jnp.broadcast_to(inverse, (8, LANES))
        normalized = (cells - average) * inverse
        norm_out[:, lanes] = normalized
        normed = normalized * gain[:, lanes] + bias[:, lanes]
        high = normed.astype(BF16)
        high_f = high.astype(F32)
        low_f = normed - high_f
        if (g + 1) * LANES <= k_main:
            stack[:px, lanes] = high
            stack[px:, lanes] = low_f.astype(BF16)
        else:
            rem[...] = (high_f + pltpu.roll(low_f, k_rem, 1) + pltpu.roll(high_f, 2 * k_rem, 1)).astype(BF16)
    edge_px = norm_edge_out.shape[0]
    norm_edge_out[...] = norm_out[pl.ds(pl.multiple_of((1 - core) * (px - edge_px), 8), edge_px), :]

    def up(t, hold):
        fetch(t).wait()
        rows = pl.ds(pl.multiple_of(t * CHUNK, CHUNK), CHUNK)
        both = dot_t(stack[...], w_vmem[rows, :k_main])
        high = dot_t(stack[:px], w_vmem[rows, k_main : 2 * k_main])
        rest = dot_t(rem[...], w_vmem[rows, 2 * k_main :])
        hold[...] = (both[:px] + both[px:]) + (high + rest)

    def act(t, hold):
        cols = pl.ds(pl.multiple_of(t * CHUNK, CHUNK), CHUNK)
        activated, slope = gelu_both(hold[...] + b_up[:, cols])
        slope_out[:, cols] = slope
        hold_act[...] = activated
        high, low = split(activated)
        acc[...] += dot(high, w_od[cols, :])
        acc_lo[...] += dot(low, w_od[cols, :LANES])
        act_out[:, cols] = hold_act[pl.ds(pl.multiple_of(part * part_px, 8), part_px), :]

    acc[...] = jnp.zeros_like(acc)
    acc_lo[...] = base[...]
    up(0, hold_a)

    def pair(i, _):
        up(2 * i + 1, hold_b)
        act(2 * i, hold_a)
        up(2 * i + 2, hold_a)
        act(2 * i + 1, hold_b)
        return 0

    lax.fori_loop(0, chunks // 2, pair, 0)
    act(chunks - 1, hold_a)
    new_out[...] = (acc[:, :LANES] + acc[:, LANES:] + acc_lo[...]) * ocean[...]
    new_edge_out[...] = new_out[pl.ds(pl.multiple_of((1 - core) * (px - edge_px), 8), edge_px), :]


def back_kernel(*refs, finish, begin, width, k_main, k_rem, states):
    refs = list(refs)

    def take(count):
        out = refs[:count]
        del refs[:count]
        return out

    (at, ocean, pending_in) = take(3)
    if finish:
        (grad_n, sent, came, norm, norm_edge, inv, gain, ocean_edge, count, grad_branch, window, taps, w_in_hi, w_in_lo) = take(14)
    if begin:
        (cot, slope, norm_now, w_out, w_od, w_up) = take(6)
    if finish:
        (carry_out, pending_out, lift_out, taps_out) = take(4)
    if begin:
        (masked_out, branch_out, hidden_out, grad_n_out, send_out) = take(5)
    if finish:
        (ext, shifted, mixed, grad_lift) = take(4)
    if begin:
        (w_vmem, sems) = take(2)
    core, part = at[0], at[1]
    px = ocean.shape[0]
    rows = px // COLS
    if begin:
        blocks = sems.shape[0]
        block = w_vmem.shape[0] // blocks

        def fetch(t):
            here = pl.ds(t * block, block)
            return pltpu.make_async_copy(w_up.at[here], w_vmem.at[here], sems.at[t])

        for t in range(blocks):
            fetch(t).start()
    if finish:
        edge_px = norm_edge.shape[0]
        total = count[...]
        zeros = jnp.zeros((rows + 2 * HALO, 8, width), F32)
        ext[:, :8, :] = zeros
        ext[:, 8 + COLS :, :] = zeros
        ext[pl.ds((rows + HALO) * core, HALO), 8 : 8 + COLS, :] = jnp.zeros((HALO, COLS, width), F32)
        part_rows = window.shape[0] - 2 * HALO
        for g in range(width // LANES):
            lanes = slice(g * LANES, (g + 1) * LANES)
            bias_sum = (sent[edge_px : edge_px + 1, lanes] + came[edge_px : edge_px + 1, lanes]) / total
            gain_sum = (sent[edge_px + 1 : edge_px + 2, lanes] + came[edge_px + 1 : edge_px + 2, lanes]) / total
            scale = inv[0:1, lanes] * gain[:, lanes]
            mix = scale * (grad_n[:, lanes] - ocean[...] * (bias_sum + norm[:, lanes] * gain_sum))
            mix_edge = scale * (came[:edge_px, lanes] - ocean_edge[...] * (bias_sum + norm_edge[:, lanes] * gain_sum))
            ext[HALO : HALO + rows, 8 : 8 + COLS, lanes] = mix.reshape(rows, COLS, LANES)
            ext[pl.ds((rows + HALO) * (1 - core), HALO), 8 : 8 + COLS, lanes] = mix_edge.reshape(HALO, COLS, LANES)

        def group(g, _):
            lanes = group_lanes(g)
            depthwise(ext, shifted, taps, mixed, lanes, True, rows)
            grad_lift[:, lanes] = mixed[:, :, lanes].reshape(px, LANES) + grad_branch[:, lanes]
            for q in range(KW):
                sums = [None] * KW
                for i in range(part_rows):
                    for v in range(0, COLS, 8):
                        grad = shifted[KW - 1 - q, HALO + part * part_rows + i, v : v + 8, :]
                        for p in range(KW):
                            term = grad * window[i + p, v : v + 8, lanes]
                            sums[p] = term if sums[p] is None else sums[p] + term
                for p in range(KW):
                    taps_out[p * KW + q : p * KW + q + 1, lanes] = jnp.sum(sums[p], axis=0, keepdims=True)
            return 0

        lax.fori_loop(0, width // LANES, group, 0)
        part_px = lift_out.shape[0]
        lift_out[...] = grad_lift[pl.ds(pl.multiple_of(part * part_px, 8), part_px), :]
        high, low = split(grad_lift[...])
        both = dot_t(jnp.concatenate([high, low], axis=0), w_in_hi[...])
        grad_x = (both[:px] + both[px:]) + dot_t(high, w_in_lo[...])
        carry = grad_x[:, LANES:] + pending_in[...]
        carry_out[...] = carry
        pending_out[...] = grad_x[:, :LANES]
    if begin:
        grad_new = cot[...] + carry if finish else cot[...]
        lane = lax.broadcasted_iota(jnp.int32, (px, LANES), 1)
        masked = jnp.where(lane < states, grad_new * ocean[...], 0.0)
        masked_out[...] = masked
        high_f = masked.astype(BF16).astype(F32)
        nothing = jnp.zeros((px, LANES), F32)
        high_w = jnp.concatenate([high_f, nothing], axis=1)
        low_w = jnp.concatenate([masked - high_f, nothing], axis=1)
        left = (high_w + pltpu.roll(low_w, SEG, 1) + pltpu.roll(high_w, 2 * SEG, 1)).astype(BF16)
        branch_out[...] = dot(left, w_out[...])
        chunks = w_od.shape[1] // CHUNK

        def chunk(t, _):
            cols = pl.ds(pl.multiple_of(t * CHUNK, CHUNK), CHUNK)
            high, low = split(dot(left, w_od[:, cols]) * slope[:, cols])
            hidden_out[:px, cols] = high
            hidden_out[px:, cols] = low
            return 0

        lax.fori_loop(0, chunks, chunk, 0)
        for t in range(blocks):
            fetch(t).wait()
        both = dot(hidden_out[...], w_vmem[:, :k_main])
        grad_n_out[:, :k_main] = (both[:px] + both[px:]) + dot(hidden_out[:px], w_vmem[:, k_main : 2 * k_main])
        rest = dot(hidden_out[...], w_vmem[:, 2 * k_main :])
        tail = rest[:px] + rest[px:] + pltpu.roll(rest[:px], LANES - 2 * k_rem, 1)
        grad_n_out[:, k_main:] = jnp.where(lane < k_rem, tail, 0.0)
        edge_px = send_out.shape[0] - 8
        for g in range(width // LANES):
            lanes = slice(g * LANES, (g + 1) * LANES)
            cells = grad_n_out[:, lanes]
            send_out[edge_px : edge_px + 1, lanes] = jnp.sum(cells, axis=0, keepdims=True)
            send_out[edge_px + 1 : edge_px + 2, lanes] = jnp.sum(cells * norm_now[:, lanes], axis=0, keepdims=True)
        send_out[:edge_px, :] = grad_n_out[pl.ds(pl.multiple_of((1 - core) * (px - edge_px), 8), edge_px), :]


def weight_kernel(n_pair, n_low, hidden, acc_in, acc_out):
    px = n_low.shape[1]

    def chunk(t, _):
        cols = pl.ds(pl.multiple_of(t * CHUNK, CHUNK), CHUNK)
        acc_out[:, cols] = acc_in[:, cols] + (dot(n_pair[...], hidden[:, cols]) + dot(n_low[...], hidden[:px, cols]))
        return 0

    lax.fori_loop(0, hidden.shape[1] // CHUNK, chunk, 0)


VMEM_SPEC = pl.BlockSpec(memory_space=pltpu.VMEM)
SMEM_SPEC = pl.BlockSpec(memory_space=pltpu.SMEM)
ANY_SPEC = pl.BlockSpec(memory_space=pl.ANY)


def out(*shape, dtype=F32):
    return jax.ShapeDtypeStruct(shape, dtype)


def call(kernel, name, args, specs, outs, scratch, limit, aliases=None):
    return pl.pallas_call(
        kernel,
        in_specs=specs,
        out_specs=[VMEM_SPEC] * len(outs),
        out_shape=outs,
        scratch_shapes=scratch,
        input_output_aliases=aliases or {},
        compiler_params=pltpu.CompilerParams(vmem_limit_bytes=limit * MIB),
        name=name,
    )(*args)


def pad_to(values, shape):
    return jnp.pad(values, [(0, size - have) for size, have in zip(shape, values.shape)])


def per_device(
    init_states, forcing, history, land_mask, w_in, b_in, w_dw, bn_gain, bn_bias, w_up, b_up, w_down, b_down, w_out, b_out, cotangent
):
    steps = lax.axis_size("step")
    devices_z = lax.axis_size("rows")
    step = lax.axis_index("step")
    depth = lax.axis_index("rows")
    core, pair = step % 2, step // 2
    side, part = depth % 2, depth // 2
    both_axes = ("step", "rows")
    block = land_mask.shape[0]
    px = 2 * block
    rows = px // COLS
    states = w_out.shape[0]
    forces = forcing.shape[2]
    channels = w_up.shape[1]
    hidden = w_up.shape[0]
    width = round_up(channels, LANES)
    wide = round_up(hidden, CHUNK)
    k_main = channels // CHUNK * CHUNK
    k_rem = channels - k_main
    col_block = channels // devices_z
    ff_block = hidden // steps

    def place(s, z):
        return s * devices_z + z

    cells = [(k, c, h, q) for k in range(steps // 2) for c in range(2) for h in range(2) for q in range(2)]
    fetch_perms = [
        [(place(2 * k + q, 2 * c + (b ^ h)), place(2 * k + c, 2 * h + q)) for k, c, h, q in cells] for b in range(2)
    ]

    def home_perm(j):
        return [(place(2 * k + c, 2 * h + q), place((2 * k + q + j) % steps, 2 * c + h)) for k, c, h, q in cells]

    siblings = [(s, s ^ 1) for s in range(steps)]

    def to_sibling(values):
        return lax.ppermute(values, "step", siblings)

    def shift_back(values, j):
        return values if j == 0 else lax.ppermute(values, "step", [((s + j) % steps, s) for s in range(steps)])

    def fetch_own(values):
        got = [lax.ppermute(values, both_axes, perm) for perm in fetch_perms]
        swap = part == 1
        return jnp.concatenate([jnp.where(swap, got[1], got[0]), jnp.where(swap, got[0], got[1])], axis=-1)

    def my_part(values, axis):
        return lax.dynamic_slice_in_dim(values, part * (values.shape[axis] // 2), values.shape[axis] // 2, axis)

    mask_row = land_mask.astype(F32)[None]
    current = init_states[0, 0, 1]
    previous = jnp.where(history[0, 0] == 2, init_states[0, 0, 0], current)
    forced = [shift_back(forcing[0, 0], j) for j in range(ROLL)]
    payload = fetch_own(jnp.concatenate([previous, current, mask_row] + forced, axis=0))
    local_count = jnp.sum(payload[2 * states])
    edge = jnp.where(core == 0, payload[:, block:], payload[:, :block])
    edge = to_sibling(jnp.concatenate([edge, jnp.full((1, block), local_count)], axis=0))
    count = jnp.full((1, LANES), jnp.maximum(local_count + edge[-1, 0], 1.0))

    def state_lanes(values):
        return pad_to(values.T, (values.shape[1], LANES))

    def force_lanes(values):
        return jnp.pad(values.T, ((0, 0), (FORCE_LANE, LANES - FORCE_LANE - forces)))

    def mask_lanes(values):
        return jnp.broadcast_to(values[:, None], (values.shape[0], LANES))

    prev, cur = state_lanes(payload[:states]), state_lanes(payload[states : 2 * states])
    prev_edge, cur_edge = state_lanes(edge[:states]), state_lanes(edge[states : 2 * states])
    ocean, ocean_edge = mask_lanes(payload[2 * states]), mask_lanes(edge[2 * states])
    base_row = 2 * states + 1
    force = [force_lanes(payload[base_row + forces * j : base_row + forces * (j + 1)]) for j in range(ROLL)]
    force_edge = [force_lanes(edge[base_row + forces * j : base_row + forces * (j + 1)]) for j in range(ROLL)]

    def in_rows(values):
        rest = LANES - FORCE_LANE - forces
        top = jnp.pad(values[:states], ((0, FORCE_LANE - states), (0, 0)))
        force_rows = jnp.pad(values[2 * states :], ((0, rest), (0, 0)))
        bottom = jnp.pad(values[states : 2 * states], ((0, LANES - states), (0, 0)))
        return jnp.concatenate([top, force_rows, bottom], axis=0)

    def row(values, size):
        return jnp.pad(values, (0, size - values.shape[0]))[None]

    w_in_hi, w_in_lo = split_outside(pad_to(in_rows(w_in.T), (2 * LANES, width)))
    w_oi = pad_to(in_rows(jnp.dot(w_out, w_in, precision=HIGHEST).T), (2 * LANES, LANES))
    w_oi_hi, w_oi_lo = split_outside(w_oi)
    b_new = row(jnp.dot(w_out, b_in + b_down, precision=HIGHEST) + b_out, LANES)
    taps = jnp.broadcast_to(
        pad_to(w_dw.reshape(channels, KW * KW).T, (KW * KW, width))[:, None], (KW * KW, 8, width)
    )
    gain, bias = row(bn_gain, width), row(bn_bias, width)
    up_hi, up_lo = split_outside(w_up)
    w_up_all = pad_to(
        jnp.concatenate(
            [up_hi[:, :k_main], up_lo[:, :k_main], up_hi[:, k_main:], up_hi[:, k_main:], up_lo[:, k_main:]], axis=1
        ),
        (wide, 2 * k_main + LANES),
    )
    w_od = jnp.dot(w_out, w_down, precision=HIGHEST)
    od_hi, od_lo = split_outside(pad_to(w_od, (SEG, wide)))
    w_od_fwd = jnp.concatenate([pad_to(od_hi, (LANES, wide)).T, pad_to(od_lo, (LANES, wide)).T], axis=1)
    w_od_bwd = pad_to(jnp.concatenate([od_hi, od_hi, od_lo], axis=0), (2 * LANES, wide))
    out_hi, out_lo = split_outside(pad_to(w_out, (SEG, width)))
    w_out_bwd = pad_to(jnp.concatenate([out_hi, out_hi, out_lo], axis=0), (2 * LANES, width))
    b_in_row, b_up_row = row(b_in, width), row(b_up, wide)
    at = jnp.stack([core, part]).astype(jnp.int32)

    cots = fetch_own(jnp.stack([shift_back(cotangent[0, j, 0], j) for j in range(ROLL)]))
    cots = jnp.pad(jnp.swapaxes(cots, 1, 2), ((0, 0), (0, 0), (0, LANES - states)))

    kept, predicted = [], []
    for j in range(ROLL):
        mixed, stats, window, x_part, base = call(
            mix_kernel, "mix",
            (at, cur, cur_edge, prev, prev_edge, force[j], force_edge[j], w_in_hi, w_in_lo, b_in_row, w_oi_hi, w_oi_lo, b_new, taps, ocean),
            [SMEM_SPEC] + [VMEM_SPEC] * 14,
            [out(px, width), out(8, width), out(3 + 2 * HALO, COLS, width), out(block, 2 * LANES), out(px, LANES)],
            [pltpu.VMEM((rows + 2 * HALO, COLS + 16, width), F32), pltpu.VMEM((KW, rows + 2 * HALO, COLS, LANES), F32), pltpu.VMEM((rows, COLS, width), F32)],
            24,
        )
        stats_other = to_sibling(stats)
        new, new_edge, norm, norm_edge, slope, act, inv = call(
            functools.partial(feed_kernel, width=width, k_main=k_main, k_rem=k_rem), "feed",
            (at, mixed, stats, stats_other, count, gain, bias, ocean, base, w_up_all, b_up_row, w_od_fwd),
            [SMEM_SPEC] + [VMEM_SPEC] * 8 + [ANY_SPEC] + [VMEM_SPEC] * 2,
            [out(px, LANES), out(block, LANES), out(px, width), out(block, width), out(px, wide), out(block, wide), out(8, width)],
            [
                pltpu.VMEM(w_up_all.shape, BF16), pltpu.VMEM((2 * px, k_main), BF16), pltpu.VMEM((px, LANES), BF16),
                pltpu.VMEM((px, CHUNK), F32), pltpu.VMEM((px, LANES), F32), pltpu.VMEM((px, CHUNK), F32), pltpu.VMEM((px, CHUNK), F32),
                pltpu.VMEM((px, CHUNK), F32), pltpu.SemaphoreType.DMA((wide // CHUNK,)),
            ],
            36,
        )
        norm_edge = to_sibling(norm_edge)
        prev, prev_edge, cur = cur, cur_edge, new
        if j < ROLL - 1:
            cur_edge = to_sibling(new_edge)
        predicted.append(lax.ppermute(my_part(new, 0)[:, :states].T, both_axes, home_perm(j)))
        kept.append((window, x_part, norm, norm_edge, slope, act, inv))

    quarter = channels // 2
    gain_q = lax.dynamic_slice_in_dim(bn_gain, part * quarter, quarter)
    bias_q = lax.dynamic_slice_in_dim(bn_bias, part * quarter, quarter)
    acc_rows = round_up(quarter + 1, 8)
    acc = jnp.zeros((acc_rows, wide), F32)
    carry, pending = None, jnp.zeros((px, LANES), F32)
    previous_step = None
    masked_parts, lifts, tap_sums, stat_sums, force_grads = [], [], [], [], []
    begin_scratch = [pltpu.VMEM(w_up_all.shape, BF16), pltpu.SemaphoreType.DMA((4,))]
    finish_scratch = [
        pltpu.VMEM((rows + 2 * HALO, COLS + 16, width), F32), pltpu.VMEM((KW, rows + 2 * HALO, COLS, LANES), F32),
        pltpu.VMEM((rows, COLS, width), F32), pltpu.VMEM((px, width), F32),
    ]
    for j in range(ROLL - 1, -2, -1):
        finish, begin = j < ROLL - 1, j >= 0
        args, specs, outs, scratch = [at, ocean, pending], [SMEM_SPEC, VMEM_SPEC, VMEM_SPEC], [], []
        if finish:
            window, x_part, norm, norm_edge, slope, act, inv = kept[j + 1]
            grad_n, sent, came, grad_branch = previous_step
            args += [grad_n, sent, came, norm, norm_edge, inv, gain, ocean_edge, count, grad_branch, window, taps, w_in_hi, w_in_lo]
            specs += [VMEM_SPEC] * 14
            outs += [out(px, LANES), out(px, LANES), out(block, width), out(round_up(KW * KW, 8), width)]
            scratch += finish_scratch
        if begin:
            args += [cots[j], kept[j][4], kept[j][2], w_out_bwd, w_od_bwd, w_up_all]
            specs += [VMEM_SPEC] * 5 + [ANY_SPEC]
            outs += [out(px, LANES), out(px, width), out(2 * px, wide, dtype=BF16), out(px, width), out(block + 8, width)]
            scratch += begin_scratch
        results = list(
            call(
                functools.partial(
                    back_kernel, finish=finish, begin=begin, width=width, k_main=k_main, k_rem=k_rem, states=states
                ),
                "back", args, specs, outs, scratch, 48,
            )
        )
        if finish:
            carry, pending, lift, tap_sum = results[:4]
            results = results[4:]
            lifts.append(lift)
            tap_sums.append(tap_sum)
            gone = my_part(pending, 0)[:, FORCE_LANE : FORCE_LANE + forces].T
            if j + 1 > 0:
                force_grads.append(lax.ppermute(gone, both_axes, home_perm(j + 1)))
        if begin:
            masked, grad_branch, hidden_now, grad_n, sent = results
            came = to_sibling(sent)
            previous_step = (grad_n, sent, came, grad_branch)
            masked_parts.append(my_part(masked, 0))
            stat_sums.append(sent[block:])
            n_q = lax.dynamic_slice_in_dim(kept[j][2], part * quarter, quarter, axis=1) * gain_q + bias_q
            n_t = jnp.concatenate([n_q.T, jnp.ones((1, px), F32), jnp.zeros((acc_rows - quarter - 1, px), F32)], axis=0)
            n_hi, n_lo = split_outside(n_t)
            (acc,) = call(
                weight_kernel, "weight", (jnp.concatenate([n_hi, n_hi], axis=1), n_lo, hidden_now, acc),
                [VMEM_SPEC] * 4, [out(acc_rows, wide)], [], 24, aliases={3: 0},
            )

    def total(values):
        return functools.reduce(jnp.add, values)

    last = jnp.concatenate([my_part(pending, 0)[:, :states], my_part(carry, 0)[:, :states], gone.T], axis=1).T
    last = lax.ppermute(last, both_axes, home_perm(0))
    grad_prev, grad_cur, gone = last[:states], last[states : 2 * states], last[2 * states :]
    grad_forcing = total(force_grads + [gone])[None, None]
    grad_init_prev = jnp.where(history[0, 0] == 2, grad_prev, 0.0)
    grad_init_cur = grad_cur + jnp.where(history[0, 0] == 1, grad_prev, 0.0)
    grad_init = jnp.stack([grad_init_prev, grad_init_cur])[None, None]

    order = range(ROLL - 1, -1, -1)
    masked_all = jnp.concatenate([m[:, :states] for m in masked_parts], axis=0)
    act_all = jnp.concatenate([kept[j][5][:, :hidden] for j in order], axis=0)
    lift_in = jnp.concatenate(
        [kept[j][0][HALO : 2 * HALO, :, :channels].reshape(block, channels) for j in order], axis=0
    )
    x_all = jnp.concatenate([kept[j][1] for j in order], axis=0)
    lift_all = jnp.concatenate([g[:, :channels] for g in lifts], axis=0)

    def outer(a, b):
        return lax.dot_general(a, b, (((0,), (0,)), ((), ())), precision=lax.Precision.HIGH, preferred_element_type=F32)

    hidden_out = outer(masked_all, act_all)
    masked_sum = jnp.sum(masked_all, axis=0)
    g_out = (
        outer(masked_all, lift_in)
        + lax.dot_general(hidden_out, w_down, (((1,), (1,)), ((), ())), precision=lax.Precision.HIGH, preferred_element_type=F32)
        + masked_sum[:, None] * b_down
    )
    g_in = outer(lift_all, x_all)
    g_in = jnp.concatenate(
        [g_in[:, :states], g_in[:, LANES : LANES + states], g_in[:, FORCE_LANE : FORCE_LANE + forces]], axis=1
    )
    first = (part == 0).astype(F32)
    stats = total(stat_sums)[:2, :channels] * first
    small = [
        g_in, jnp.sum(lift_all, axis=0), total(tap_sums)[: KW * KW, :channels].T, stats[1], stats[0],
        acc[quarter, :hidden] * first, jnp.zeros((0,), F32), g_out, masked_sum,
    ]
    flat = lax.psum(jnp.concatenate([v.reshape(-1) for v in small]), both_axes)
    pieces, offset = [], 0
    for v in small:
        pieces.append(flat[offset : offset + v.size].reshape(v.shape))
        offset += v.size
    g_w_in, g_b_in, g_w_dw, g_gain, g_bias, g_b_up, _, g_w_out, g_b_out = pieces
    g_b_down = jnp.sum(w_out * g_b_out[:, None], axis=0)

    share = lax.psum_scatter(acc[:quarter, :hidden], "step", scatter_dimension=1, tiled=True)
    mine = lax.dynamic_slice_in_dim(share, side * col_block, col_block, axis=0)
    other = lax.dynamic_slice_in_dim(share, (1 - side) * col_block, col_block, axis=0)
    share_up = (mine + lax.ppermute(other, "rows", [(z, z ^ 1) for z in range(devices_z)])).T
    hidden_share = lax.psum(lax.psum_scatter(hidden_out, "step", scatter_dimension=1, tiled=True), "rows")
    w_out_block = lax.dynamic_slice_in_dim(w_out, depth * col_block, col_block, axis=1)
    share_down = outer(w_out_block, hidden_share)
    return (
        jnp.stack(predicted)[None, :, None],
        grad_init,
        grad_forcing,
        g_w_in,
        g_b_in,
        g_w_dw.reshape(channels, KW, KW),
        g_gain,
        g_bias,
        share_up,
        g_b_up,
        share_down,
        g_b_down,
        g_w_out,
        g_b_out,
    )


def solution(mesh):
    state_spec = P("step", None, None, None, "rows")
    force_spec = P("step", None, None, "rows")
    in_specs = (state_spec, force_spec, P("step", None), P("rows")) + (P(),) * 11 + (state_spec,)
    out_specs = (state_spec, state_spec, force_spec) + (P(),) * 5 + (P("step", "rows"), P(), P("rows", "step"), P(), P(), P())
    return jax.shard_map(per_device, mesh=mesh, in_specs=in_specs, out_specs=out_specs, check_vma=False)
```

time: 1760 us -> 956 us (0.54)
  matrix products: 693 us -> 33.2 us
  Pallas kernels: 0 us -> 323 us
  other arithmetic: 298 us -> 49 us
  blocking collectives: 161 us -> 0 us
  starting transfers between devices: 187 us -> 65.6 us
  local copies, waits for them, and re-layouts: 223 us -> 312 us
  waiting for transfers between devices: 158 us -> 135 us
    dot_general x96 -> x8, matrix products: 693 us -> 33.2 us  [the longest x4 13 us: outer(): lax.dot_general(a, b, (((0,), (0,)), ((), ())), precision=lax.Precision.H...]
    pallas_call x0 -> x33, Pallas kernels: none -> 323 us  [call(): pl.pallas_call(kernel, in_specs=specs, out_specs=[VMEM_SPEC] * len(outs),...]
    broadcast_in_dim x392 -> x12, local copies, waits for them, and re-layouts: 178 us -> 1.38 us  [the longest x5 0.67 us: row(): return jnp.pad(values, (0, size - values.shape[0]))[None]]
    psum x17 -> x0, blocking collectives: 161 us -> none  [the longest x8 63 us: per_device(): lax.psum((first_sum, second_sum, local_count), 'rows')]
    unnamed x1061 -> x748, local copies, waits for them, and re-layouts: 32.1 us -> 178 us
    ppermute x60 -> x67, starting transfers between devices: 186 us -> 65.4 us  [the longest x14 16.5 us: shift_back(): lax.ppermute(values, 'step', [((s + j) % steps, s) for s in range(steps)])]
    add x10 -> x3, other arithmetic: 108 us -> 3.16 us  [the longest x2 3.15 us: total(): return functools.reduce(jnp.add, values)]
    select_n x110 -> x3, other arithmetic: 89.6 us -> 1.78 us  [the longest x1 1.75 us: fetch_own(): jnp.where(swap, got[1], got[0])]
  transfers between devices with their start and end apart: 65 -> 71, of which waited for: 34 -> 19; matrix products, arithmetic and copies ran while one was open for 54% -> 27% of each run, Pallas kernels for 0% -> 34%
where the time goes in v1:
time: 956 us; the launch traced here: 939 us
  Pallas kernels  323 us (34%)
  local copies, waits for them, and re-layouts  312 us (33%)
  waiting for transfers between devices  135 us (14%)
  starting transfers between devices  65.6 us (7%)
  other arithmetic  49 us (5%)
  matrix products  33.2 us (3%)
  between operations  21.4 us (2%)
    pallas_call x33, Pallas kernels, call(): pl.pallas_call(kernel, in_specs=specs, out_specs=[VMEM_SPEC] * len(outs),...  323 us
    unnamed x748, local copies, waits for them, and re-layouts  178 us
    psum x1, waiting for transfers between devices, per_device(): flat = lax.psum(jnp.concatenate([v.reshape(-1) for v in small]), both_axes)  78.6 us
    psum x1, waiting for transfers between devices, per_device(): lax.psum(lax.psum_scatter(hidden_out, 'step', scatter_dimension=1, tiled=...  29.8 us
  transfers between devices with their start and end apart: 71, of which 19 were waited for; matrix products, arithmetic and copies ran while one was open for 27% of the time, Pallas kernels for 34%

profile of v1, /device:TPU:9, one launch (start us, length us, event | category | flops | bytes accessed | tf_op | source)
XLA Modules:
  0.0 939.4 jit_solution(9801906298962581925)
XLA Ops:
  21.4 9.2 fusion.70
  38.3 12.2 %copy.122 = f32[3200,800]{1,0:T(8,128)} copy(f32[3200,800]{0,1:T(8,128)} %param.25) | data formatting | bytes 20480000 | tf_op args[9]
  50.6 10.2 %fusion = (bf16[3200,800]{1,0:T(8,128)(2,1)}, bf16[3200,800]{1,0:T(8,128)(2,1)}) fusion(f32[3200,800]{1,0:T(8,128)} %copy.122), kind=kLoop, calls=%fused_computation.2 | loop fusion | flops 10240000 | bytes 20480000 | tf_op jit(solution)/shard_map/convert_element_type | solution.py:39
  112.4 16.4 %concatenate.107 = bf16[3200,1632]{1,0:T(8,128)(2,1)} concatenate(bf16[3200,768]{1,0:T(8,128)(2,1)} %slice.538, bf16[3200,768]{1,0:T(8,128)(2,1)} %slice.539, bf16[3200,32]{1,0:T(8,128)(2,1)} %slice.540, bf16[3200,32]{1,0:T(8,128)(2,1)} %slice.540, bf16[3200,32]{1,0:T(8,128)(2,1)} %slice.541), dimensions={1} | concatenate | bytes 20889600 | tf_op jit(solution)/shard_map/concatenate | solution.py:455
  128.9 9.7 %pad.169.w_up.refs_8_.refs_22_ = bf16[3328,1664]{1,0:T(8,128)(2,1)} pad(bf16[3200,1632]{1,0:T(8,128)(2,1)} %concatenate.107, bf16[]{:T(256)} %constant.61.clone.1), padding=0_128x0_32 | pad | bytes 21520386 | tf_op jit(solution)/shard_map/jit(_pad)/pad | solution.py:355
  152.2 14.9 %feed.8 = (f32[192,128]{1,0:T(8,128)S(1)}, f32[96,128]{1,0:T(8,128)}, f32[192,896]{1,0:T(8,128)S(1)}, f32[96,896]{1,0:T(8,128)}, f32[192,3328]{1,0:T(8,128)S(1)}...) custom-call(s32[2]{0:T(128)S(1)} %copy-done.153, f32[192,896]{1,0:T(8,128)S(1)} %copy-done.101, f32[8,896]{1,0:T(8,128)S(1)} %copy-done.256, ...), custom_call_target="tpu_custom_call" | custom-call | tf_op jit(solution)/shard_map/feed/pallas_call | solution.py:342
  198.0 14.3 %feed.9 = (f32[192,128]{1,0:T(8,128)S(1)}, f32[96,128]{1,0:T(8,128)S(1)}, f32[192,896]{1,0:T(8,128)S(1)}, f32[96,896]{1,0:T(8,128)S(1)}, f32[192,3328]{1,0:T(8,1...) custom-call(s32[2]{0:T(128)S(1)} %copy-done.155, f32[192,896]{1,0:T(8,128)S(1)} %get-tuple-element.179.mixed, ...), custom_call_target="tpu_custom_call" | custom-call | tf_op jit(solution)/shard_map/feed/pallas_call | solution.py:342
  225.9 14.9 %feed.10 = (f32[192,128]{1,0:T(8,128)S(1)}, f32[96,128]{1,0:T(8,128)S(1)}, f32[192,896]{1,0:T(8,128)S(1)}, f32[96,896]{1,0:T(8,128)}, f32[192,3328]{1,0:T(8,128)...) custom-call(s32[2]{0:T(128)S(1)} %copy-done.155, f32[192,896]{1,0:T(8,128)S(1)} %get-tuple-element.184.mixed, ...), custom_call_target="tpu_custom_call" | custom-call | tf_op jit(solution)/shard_map/feed/pallas_call | solution.py:342
  252.0 14.9 %feed.11 = (f32[192,128]{1,0:T(8,128)S(1)}, f32[96,128]{1,0:T(8,128)S(1)}, f32[192,896]{1,0:T(8,128)S(1)}, f32[96,896]{1,0:T(8,128)}, f32[192,3328]{1,0:T(8,128)...) custom-call(s32[2]{0:T(128)S(1)} %copy-done.155, f32[192,896]{1,0:T(8,128)S(1)} %get-tuple-element.189.mixed, ...), custom_call_target="tpu_custom_call" | custom-call | tf_op jit(solution)/shard_map/feed/pallas_call | solution.py:342
  282.8 14.9 %feed.12 = (f32[192,128]{1,0:T(8,128)S(1)}, f32[96,128]{1,0:T(8,128)}, f32[192,896]{1,0:T(8,128)S(1)}, f32[96,896]{1,0:T(8,128)}, f32[192,3328]{1,0:T(8,128)S(1)...) custom-call(s32[2]{0:T(128)S(1)} %copy-done.155, f32[192,896]{1,0:T(8,128)S(1)} %get-tuple-element.194.mixed, ...), custom_call_target="tpu_custom_call" | custom-call | tf_op jit(solution)/shard_map/feed/pallas_call | solution.py:342
  348.4 14.6 %feed.13 = (f32[192,128]{1,0:T(8,128)S(1)}, f32[96,128]{1,0:T(8,128)S(1)}, f32[192,896]{1,0:T(8,128)S(1)}, f32[96,896]{1,0:T(8,128)S(1)}, f32[192,3328]{1,0:T(8,...) custom-call(s32[2]{0:T(128)S(1)} %copy-done.157, f32[192,896]{1,0:T(8,128)S(1)} %copy-done.103, ...), custom_call_target="tpu_custom_call" | custom-call | tf_op jit(solution)/shard_map/feed/pallas_call | solution.py:342
  373.9 15.3 %feed.14 = (f32[192,128]{1,0:T(8,128)S(1)}, f32[96,128]{1,0:T(8,128)}, f32[192,896]{1,0:T(8,128)S(1)}, f32[96,896]{1,0:T(8,128)S(1)}, f32[192,3328]{1,0:T(8,128)...) custom-call(s32[2]{0:T(128)S(1)} %copy-done.157, f32[192,896]{1,0:T(8,128)S(1)} %get-tuple-element.204.mixed, ...), custom_call_target="tpu_custom_call" | custom-call | tf_op jit(solution)/shard_map/feed/pallas_call | solution.py:342
  436.9 14.9 %feed.15 = (f32[192,128]{1,0:T(8,128)S(1)}, f32[96,128]{1,0:T(8,128)}, f32[192,896]{1,0:T(8,128)S(1)}, f32[96,896]{1,0:T(8,128)S(1)}, f32[192,3328]{1,0:T(8,128)...) custom-call(s32[2]{0:T(128)S(1)} %copy-done.159, f32[192,896]{1,0:T(8,128)S(1)} %get-tuple-element.209.mixed, ...), custom_call_target="tpu_custom_call" | custom-call | tf_op jit(solution)/shard_map/feed/pallas_call | solution.py:342
  457.2 10.1 %back.9 = (f32[192,128]{1,0:T(8,128)S(1)}, f32[192,896]{1,0:T(8,128)S(1)}, bf16[384,3328]{1,0:T(8,128)(2,1)}, f32[192,896]{1,0:T(8,128)S(1)}, f32[104,896]{1,0:T(8,128)S(1)}) custom-call(s32[2]{0:T(128)S(1)} %copy-done.159, f32[192,128]{1,0:T(8,128)S(1)} %broadcast_in_dim.86.ocean.refs_1_, f32[192,128]{1,0:T(8,128)S(1)} %broadcast_in_dim.92.refs_2_, ...), custom_call_target="tpu_custom_call" | custom-call | tf_op jit(solution)/shard_map/back/pallas_call | solution.py:342
  482.1 15.7 %back.10 = (f32[192,128]{1,0:T(8,128)}, f32[192,128]{1,0:T(8,128)S(1)}, f32[96,896]{1,0:T(8,128)S(1)}, f32[56,896]{1,0:T(8,128)S(1)}, f32[192,128]{1,0:T(8,128)S...) custom-call(s32[2]{0:T(128)S(1)} %copy-done.159, ...), custom_call_target="tpu_custom_call" | custom-call | tf_op jit(solution)/shard_map/back/pallas_call | solution.py:342
  500.3 16.1 %back.11 = (f32[192,128]{1,0:T(8,128)}, f32[192,128]{1,0:T(8,128)S(1)}, f32[96,896]{1,0:T(8,128)S(1)}, f32[56,896]{1,0:T(8,128)S(1)}, f32[192,128]{1,0:T(8,128)S...) custom-call(s32[2]{0:T(128)S(1)} %copy-done.159, ...), custom_call_target="tpu_custom_call" | custom-call | tf_op jit(solution)/shard_map/back/pallas_call | solution.py:342
  534.4 15.8 %back.12 = (f32[192,128]{1,0:T(8,128)}, f32[192,128]{1,0:T(8,128)S(1)}, f32[96,896]{1,0:T(8,128)S(1)}, f32[56,896]{1,0:T(8,128)S(1)}, f32[192,128]{1,0:T(8,128)S...) custom-call(s32[2]{0:T(128)S(1)} %copy-done.159, ...), custom_call_target="tpu_custom_call" | custom-call | tf_op jit(solution)/shard_map/back/pallas_call | solution.py:342
  564.6 16.8 %back.13 = (f32[192,128]{1,0:T(8,128)}, f32[192,128]{1,0:T(8,128)S(1)}, f32[96,896]{1,0:T(8,128)S(1)}, f32[56,896]{1,0:T(8,128)S(1)}, f32[192,128]{1,0:T(8,128)S...) custom-call(s32[2]{0:T(128)S(1)} %copy-done.159, ...), custom_call_target="tpu_custom_call" | custom-call | tf_op jit(solution)/shard_map/back/pallas_call | solution.py:342
  601.4 16.0 %back.14 = (f32[192,128]{1,0:T(8,128)}, f32[192,128]{1,0:T(8,128)S(1)}, f32[96,896]{1,0:T(8,128)S(1)}, f32[56,896]{1,0:T(8,128)S(1)}, f32[192,128]{1,0:T(8,128)S...) custom-call(s32[2]{0:T(128)S(1)} %copy-done.159, ...), custom_call_target="tpu_custom_call" | custom-call | tf_op jit(solution)/shard_map/back/pallas_call | solution.py:342
  627.0 16.7 %back.15 = (f32[192,128]{1,0:T(8,128)}, f32[192,128]{1,0:T(8,128)S(1)}, f32[96,896]{1,0:T(8,128)S(1)}, f32[56,896]{1,0:T(8,128)S(1)}, f32[192,128]{1,0:T(8,128)S...) custom-call(s32[2]{0:T(128)S(1)} %copy-done.159, ...), custom_call_target="tpu_custom_call" | custom-call | tf_op jit(solution)/shard_map/back/pallas_call | solution.py:342
  658.0 17.1 %back.16 = (f32[192,128]{1,0:T(8,128)}, f32[192,128]{1,0:T(8,128)S(1)}, f32[96,896]{1,0:T(8,128)S(1)}, f32[56,896]{1,0:T(8,128)S(1)}, f32[192,128]{1,0:T(8,128)S...) custom-call(s32[2]{0:T(128)S(1)} %copy-done.159, ...), custom_call_target="tpu_custom_call" | custom-call | tf_op jit(solution)/shard_map/back/pallas_call | solution.py:342
  721.9 11.1 %concatenate.135 = f32[232877]{0:T(1024)} concatenate(f32[126400]{0:T(1024)S(1)} %reshape.107, f32[800]{0:T(1024)S(1)} %add_add_fusion, f32[39200]{0:T(1024)S(1)} %reshape.108, f32[800]{0:T(1024)S(1)} %copy-done.326, f32[800]{0:T(1024)S(1)} %copy-done.325, f32[3200]{0:T(1024)S(1)} %copy-done.313, f32[61600]{0:T(1024)} %reshape.117, f32[77]{0:T(128)S(1)} %copy-done.338), dimensions={0} | concatenate | bytes 1863016 | tf_op jit(solution)/shard_map/concatenate | solution.py:600
  800.8 78.6 %all-reduce.44.cloned.1.call-done = f32[232877]{0:T(1024)} async-done(((f32[232877]{0:T(1024)}), f32[232877]{0:T(1024)}) %all-reduce.44.cloned.1.call-update) | async-done | bytes 931524 | tf_op jit(solution)/shard_map/psum | solution.py:600
  898.5 29.8 %all-reduce.46.cloned.1.call-done = f32[77,400]{1,0:T(8,128)} async-done(((f32[77,400]{1,0:T(8,128)}), f32[77,400]{1,0:T(8,128)}) %all-reduce.46.cloned.1.call-update) | async-done | bytes 123216 | tf_op jit(solution)/shard_map/psum | solution.py:612
  (1103 shorter events, 497.8 us)
Async XLA Ops:
  8.0 871.3 %all-reduce.44.cloned.1.call-start = ((), (), s32[]{:S(2)}) async-start(), calls=%async_computation.2 | async-start | bytes 1867776 | tf_op jit(solution)/shard_map/psum | solution.py:600
  8.8 56.2 %collective-permute-start = (f32[4,96]{0,1:T(8,128)S(1)}, f32[4,96]{0,1:T(8,128)}, u32[]{:S(2)}, u32[]{:S(2)}) collective-permute-start(f32[4,96]{0,1:T(8,128)S(1)} %bitcast.232), channel_id=1, source_target_pairs={{4,0},{8,4},{12,8},{16,12},{20,16},{24,20},{28,24},{0,28},{5,1},{9... | collective-permute-start | bytes 4616 | tf_op jit(solution)/shard_map/ppermute | solution.py:399
  9.6 56.1 %collective-permute-start.1 = (f32[4,96]{0,1:T(8,128)S(1)}, f32[4,96]{0,1:T(8,128)}, u32[]{:S(2)}, u32[]{:S(2)}) collective-permute-start(f32[4,96]{0,1:T(8,128)S(1)} %bitcast.233), channel_id=1, source_target_pairs={{8,0},{12,4},{16,8},{20,12},{24,16},{28,20},{0,24},{4,28},{9,1},{1... | collective-permute-start | bytes 4616 | tf_op jit(solution)/shard_map/ppermute | solution.py:399
  11.7 60.1 %collective-permute-start.2 = (f32[4,96]{0,1:T(8,128)S(1)}, f32[4,96]{0,1:T(8,128)}, u32[]{:S(2)}, u32[]{:S(2)}) collective-permute-start(f32[4,96]{0,1:T(8,128)S(1)} %bitcast.234), channel_id=1, source_target_pairs={{12,0},{16,4},{20,8},{24,12},{28,16},{0,20},{4,24},{8,28},{13,1},{... | collective-permute-start | bytes 4616 | tf_op jit(solution)/shard_map/ppermute | solution.py:399
  13.0 58.8 %collective-permute-start.3 = (f32[4,96]{0,1:T(8,128)S(1)}, f32[4,96]{0,1:T(8,128)}, u32[]{:S(2)}, u32[]{:S(2)}) collective-permute-start(f32[4,96]{0,1:T(8,128)S(1)} %bitcast.235), channel_id=1, source_target_pairs={{16,0},{20,4},{24,8},{28,12},{0,16},{4,20},{8,24},{12,28},{17,1},{... | collective-permute-start | bytes 4616 | tf_op jit(solution)/shard_map/ppermute | solution.py:399
  14.3 59.6 %collective-permute-start.4 = (f32[4,96]{0,1:T(8,128)S(1)}, f32[4,96]{0,1:T(8,128)}, u32[]{:S(2)}, u32[]{:S(2)}) collective-permute-start(f32[4,96]{0,1:T(8,128)S(1)} %bitcast.236), channel_id=1, source_target_pairs={{20,0},{24,4},{28,8},{0,12},{4,16},{8,20},{12,24},{16,28},{21,1},{... | collective-permute-start | bytes 4616 | tf_op jit(solution)/shard_map/ppermute | solution.py:399
  71.8 117.9 %collective-permute-start.33 = (f32[77,96]{0,1:T(8,128)}, f32[77,96]{0,1:T(8,128)}, u32[]{:S(2)}, u32[]{:S(2)}) collective-permute-start(f32[77,96]{0,1:T(8,128)} %bitcast.52), channel_id=1, source_target_pairs={{4,0},{8,4},{12,8},{16,12},{20,16},{24,20},{28,24},{0,28},{5,1},{9... | collective-permute-start | bytes 88712 | tf_op jit(solution)/shard_map/ppermute | solution.py:399
  71.8 142.9 %collective-permute-start.34 = (f32[77,96]{0,1:T(8,128)}, f32[77,96]{0,1:T(8,128)}, u32[]{:S(2)}, u32[]{:S(2)}) collective-permute-start(f32[77,96]{0,1:T(8,128)} %bitcast.54), channel_id=1, source_target_pairs={{8,0},{12,4},{16,8},{20,12},{24,16},{28,20},{0,24},{4,28},{9,1},{1... | collective-permute-start | bytes 88712 | tf_op jit(solution)/shard_map/ppermute | solution.py:399
  73.8 150.6 %collective-permute-start.35 = (f32[77,96]{0,1:T(8,128)}, f32[77,96]{0,1:T(8,128)}, u32[]{:S(2)}, u32[]{:S(2)}) collective-permute-start(f32[77,96]{0,1:T(8,128)} %bitcast.56), channel_id=1, source_target_pairs={{12,0},{16,4},{20,8},{24,12},{28,16},{0,20},{4,24},{8,28},{13,1},{... | collective-permute-start | bytes 88712 | tf_op jit(solution)/shard_map/ppermute | solution.py:399
  84.0 159.6 %collective-permute-start.36 = (f32[77,96]{0,1:T(8,128)}, f32[77,96]{0,1:T(8,128)}, u32[]{:S(2)}, u32[]{:S(2)}) collective-permute-start(f32[77,96]{0,1:T(8,128)} %bitcast.58), channel_id=1, source_target_pairs={{16,0},{20,4},{24,8},{28,12},{0,16},{4,20},{8,24},{12,28},{17,1},{... | collective-permute-start | bytes 88712 | tf_op jit(solution)/shard_map/ppermute | solution.py:399
  98.7 42.4 %collective-permute-start.10 = (f32[8,896]{1,0:T(8,128)S(1)}, f32[8,896]{1,0:T(8,128)S(1)}, u32[]{:S(2)}, u32[]{:S(2)}) collective-permute-start(f32[8,896]{1,0:T(8,128)S(1)} %get-tuple-element.175.stats), channel_id=1, source_target_pairs={{0,4},{4,0},{8,12},{12,8},{16,20},{20,16},{24,28},{28,24},{1,5},{5... | collective-permute-start | bytes 86024 | tf_op jit(solution)/shard_map/ppermute | solution.py:396
  178.4 72.5 %collective-permute-start.37 = (f32[77,96]{0,1:T(8,128)}, f32[77,96]{0,1:T(8,128)S(1)}, u32[]{:S(2)}, u32[]{:S(2)}) collective-permute-start(f32[77,96]{0,1:T(8,128)} %bitcast.242), channel_id=1, source_target_pairs={{20,0},{24,4},{28,8},{0,12},{4,16},{8,20},{12,24},{16,28},{21,1},{... | collective-permute-start | bytes 88712 | tf_op jit(solution)/shard_map/ppermute | solution.py:399
  191.2 78.0 %collective-permute-start.38 = (f32[77,96]{0,1:T(8,128)S(1)}, f32[77,96]{0,1:T(8,128)S(1)}, u32[]{:S(2)}, u32[]{:S(2)}) collective-permute-start(f32[77,96]{0,1:T(8,128)S(1)} %bitcast.241), channel_id=1, source_target_pairs={{24,0},{28,4},{0,8},{4,12},{8,16},{12,20},{16,24},{20,28},{25,1},{... | collective-permute-start | bytes 88712 | tf_op jit(solution)/shard_map/ppermute | solution.py:399
  216.9 59.4 %collective-permute-start.39 = (f32[77,96]{0,1:T(8,128)S(1)}, f32[77,96]{0,1:T(8,128)S(1)}, u32[]{:S(2)}, u32[]{:S(2)}) collective-permute-start(f32[77,96]{0,1:T(8,128)S(1)} %bitcast.240), channel_id=1, source_target_pairs={{28,0},{0,4},{4,8},{8,12},{12,16},{16,20},{20,24},{24,28},{29,1},{... | collective-permute-start | bytes 88712 | tf_op jit(solution)/shard_map/ppermute | solution.py:399
  276.9 89.0 %collective-permute-start.40 = (f32[8,77,96]{1,2,0:T(8,128)}, f32[8,77,96]{1,2,0:T(8,128)}, u32[]{:S(2)}, u32[]{:S(2)}) collective-permute-start(f32[8,77,96]{1,2,0:T(8,128)} %constant_dynamic-update-slice_fusion.8), channel_id=1, source_target_pairs={{1,0},{5,1},{0,2},{4,3},{3,4},{7,5},{2,6},{6,7},{9,8},{13,9},{8,10... | collective-permute-start | bytes 709640 | tf_op jit(solution)/shard_map/ppermute | solution.py:402
  276.9 88.9 %collective-permute-start.41 = (f32[8,77,96]{1,2,0:T(8,128)}, f32[8,77,96]{1,2,0:T(8,128)}, u32[]{:S(2)}, u32[]{:S(2)}) collective-permute-start(f32[8,77,96]{1,2,0:T(8,128)} %constant_dynamic-update-slice_fusion.8), channel_id=1, source_target_pairs={{0,0},{4,1},{1,2},{5,3},{2,4},{6,5},{3,6},{7,7},{8,8},{12,9},{9,10... | collective-permute-start | bytes 709640 | tf_op jit(solution)/shard_map/ppermute | solution.py:402
  331.9 373.3 %collective-permute-start.57 = (f32[96,896]{1,0:T(8,128)}, f32[96,896]{1,0:T(8,128)}, u32[]{:S(2)}, u32[]{:S(2)}) collective-permute-start(f32[96,896]{1,0:T(8,128)} %get-tuple-element.280), channel_id=1, source_target_pairs={{0,4},{4,0},{8,12},{12,8},{16,20},{20,16},{24,28},{28,24},{1,5},{5... | collective-permute-start | bytes 1032200 | tf_op jit(solution)/shard_map/ppermute | solution.py:396
  335.9 320.3 %collective-permute-start.55 = (f32[96,896]{1,0:T(8,128)}, f32[96,896]{1,0:T(8,128)}, u32[]{:S(2)}, u32[]{:S(2)}) collective-permute-start(f32[96,896]{1,0:T(8,128)} %copy-done.269), channel_id=1, source_target_pairs={{0,4},{4,0},{8,12},{12,8},{16,20},{20,16},{24,28},{28,24},{1,5},{5... | collective-permute-start | bytes 1032200 | tf_op jit(solution)/shard_map/ppermute | solution.py:396
  397.3 229.6 %collective-permute-start.53 = (f32[96,896]{1,0:T(8,128)}, f32[96,896]{1,0:T(8,128)}, u32[]{:S(2)}, u32[]{:S(2)}) collective-permute-start(f32[96,896]{1,0:T(8,128)} %get-tuple-element.262), channel_id=1, source_target_pairs={{0,4},{4,0},{8,12},{12,8},{16,20},{20,16},{24,28},{28,24},{1,5},{5... | collective-permute-start | bytes 1032200 | tf_op jit(solution)/shard_map/ppermute | solution.py:396
  560.6 39.1 %collective-permute-start.51 = (f32[96,896]{1,0:T(8,128)}, f32[96,896]{1,0:T(8,128)}, u32[]{:S(2)}, u32[]{:S(2)}) collective-permute-start(f32[96,896]{1,0:T(8,128)} %get-tuple-element.253), channel_id=1, source_target_pairs={{0,4},{4,0},{8,12},{12,8},{16,20},{20,16},{24,28},{28,24},{1,5},{5... | collective-permute-start | bytes 1032200 | tf_op jit(solution)/shard_map/ppermute | solution.py:396
  733.0 159.8 %reduce-scatter.9.cloned.1.call-start = ((), (), s32[]{:S(2)}) async-start(), calls=%async_computation.5 | async-start | bytes 1843200
  734.8 159.8 %reduce-scatter.7.cloned.1.call-start = ((), (), s32[]{:S(2)}) async-start(), calls=%async_computation.4 | async-start | bytes 7372800
  747.6 180.6 %all-reduce.46.cloned.1.call-start = ((), (), s32[]{:S(2)}) async-start(), calls=%async_computation.3 | async-start | bytes 327680 | tf_op jit(solution)/shard_map/psum | solution.py:612
  896.4 34.2 %collective-permute-start.66 = (f32[200,400]{1,0:T(8,128)S(1)}, f32[200,400]{1,0:T(8,128)S(1)}, u32[]{:S(2)}, u32[]{:S(2)}) collective-permute-start(f32[200,400]{1,0:T(8,128)S(1)} %copy.171), channel_id=1, source_target_pairs={{0,1},{1,0},{2,3},{3,2},{4,5},{5,4},{6,7},{7,6},{8,9},{9,8},{10,11... | collective-permute-start | bytes 960008 | tf_op jit(solution)/shard_map/ppermute | solution.py:611
  (392 other events, 3561.4 us)
Sparse Core Ops, SparseCore 0:
  733.1 146.1 all-reduce.43
Sparse Core Ops, SparseCore 1:
  737.1 38.6 reduce-scatter.8
  779.5 63.9 reduce-scatter.6
  894.7 33.5 all-reduce.45

commit v2 on v1

v2 whole, which is shorter than its diff:
```python
import functools

import jax
import jax.numpy as jnp
from jax import lax
from jax.experimental import pallas as pl
from jax.experimental.pallas import tpu as pltpu
from jax.sharding import PartitionSpec as P

F32 = jnp.float32
BF16 = jnp.bfloat16
HIGHEST = lax.Precision.HIGHEST
ROLL = 8
COLS = 32
KW = 7
HALO = 3
EPSILON = 1e-05
LANES = 128
CHUNK = 256
SEG = 80
MIB = 2**20

ERF_P = 0.39
ERF_C = (0.23532534, 0.09138764, 0.64956134, -0.63540268, 0.88666585, -0.22753749)


def round_up(value, multiple):
    return -(-value // multiple) * multiple


def split(values):
    high = values.astype(BF16)
    return high, (values - high.astype(F32)).astype(BF16)


def split_outside(values):
    rounded = lax.reduce_precision(values, 8, 7)
    return rounded.astype(BF16), (values - rounded).astype(BF16)


def dot(left, right):
    return jnp.dot(left, right, preferred_element_type=F32)


def dot_t(left, right):
    return lax.dot_general(left, right, (((1,), (1,)), ((), ())), preferred_element_type=F32)


def gelu_both(v):
    e = jnp.exp(v * v * (-0.5))
    t = 1.0 / (1.0 + (ERF_P * 0.7071067811865476) * jnp.abs(v))
    q = 0.5 * ERF_C[5]
    for coefficient in ERF_C[4::-1]:
        q = q * t + 0.5 * coefficient
    q = (q * t) * e
    phi = jnp.where(v >= 0.0, 1.0 - q, q)
    return v * phi, phi + v * (e * 0.3989422804014327)


def depthwise(ext, shifted, kernel, mixed, lanes, flip, rows):
    rows_in = rows + 2 * HALO
    for q in range(KW):
        for r in range(rows_in):
            shifted[q, r] = ext[r, 5 + q : 5 + q + COLS, lanes]
    for v in range(0, COLS, 8):
        total = [None] * rows
        for q in range(KW):
            taps = [
                kernel[(KW * KW - 1 - (p * KW + q)) if flip else (p * KW + q), :, lanes]
                for p in range(KW)
            ]
            for r in range(rows_in):
                cell = shifted[q, r, v : v + 8, :]
                for p in range(KW):
                    i = r - p
                    if 0 <= i < rows:
                        term = taps[p] * cell
                        total[i] = term if total[i] is None else total[i] + term
        for i in range(rows):
            mixed[i, v : v + 8, lanes] = total[i]


def ocean_count(sent, came):
    last = sent.shape[0] - 1
    return jnp.maximum(sent[last:, :LANES] + came[last:, :LANES], 1.0)


def group_lanes(group):
    return pl.ds(pl.multiple_of(group * LANES, LANES), LANES)


def mix_kernel(
    at, cur, cur_edge, prev, prev_edge, force, force_edge, w_in_hi, w_in_lo, b_in, w_oi_hi, w_oi_lo, b_new, taps, ocean,
    mixed_out, stats_out, base_out, window_out, x_all, lifted_all,
    ext, shifted, mixed, x_part, sems, *, turn, cur_lanes, prev_lanes,
):
    core, part = at[0], at[1]
    px = cur.shape[0]
    edge_px = x_part.shape[0]
    rows = px // COLS
    width = mixed_out.shape[1]
    prev_now, prev_edge_now = prev[...], prev_edge[:edge_px, prev_lanes : prev_lanes + LANES]
    if turn:
        prev_now, prev_edge_now = prev_now + force[turn], prev_edge_now + force_edge[turn]
    own = jnp.concatenate([prev_now, cur[...]], axis=1)
    edge = jnp.concatenate([prev_edge_now, cur_edge[:edge_px, cur_lanes : cur_lanes + LANES]], axis=1)
    own_hi, own_lo = split(own)
    edge_hi, edge_lo = split(edge)
    both = dot(jnp.concatenate([own_hi, edge_hi, own_lo, edge_lo], axis=0), w_in_hi[...])
    high = dot(jnp.concatenate([own_hi, edge_hi], axis=0), w_in_lo[...])
    lifted = (both[: px + edge_px] + both[px + edge_px :]) + (high + b_in[...])
    base_out[...] = dot(own_hi, w_oi_hi[...]) + dot(own_lo, w_oi_hi[...]) + dot(own_hi, w_oi_lo[...]) + b_new[...]
    zeros = jnp.zeros((rows + 2 * HALO, 8, width), F32)
    ext[:, :8, :] = zeros
    ext[:, 8 + COLS :, :] = zeros
    ext[HALO : HALO + rows, 8 : 8 + COLS, :] = lifted[:px].reshape(rows, COLS, width)
    ext[pl.ds((rows + HALO) * (1 - core), HALO), 8 : 8 + COLS, :] = lifted[px:].reshape(HALO, COLS, width)
    ext[pl.ds((rows + HALO) * core, HALO), 8 : 8 + COLS, :] = jnp.zeros((HALO, COLS, width), F32)
    part_rows = window_out.shape[0] - 2 * HALO
    part_px = x_part.shape[0]
    x_part[...] = jnp.where(part == 0, own[:part_px], own[part_px:])
    here = pl.ds(turn * part_rows, part_rows)
    keeps = [
        pltpu.make_async_copy(ext.at[pl.ds(part * part_rows, window_out.shape[0]), 8 : 8 + COLS, :], window_out, sems.at[0]),
        pltpu.make_async_copy(ext.at[pl.ds(part * part_rows + HALO, part_rows), 8 : 8 + COLS, :], lifted_all.at[here], sems.at[1]),
        pltpu.make_async_copy(x_part, x_all.at[pl.ds(turn * part_px, part_px)], sems.at[2]),
    ]
    for keep in keeps:
        keep.start()
    mask = ocean[...]

    def group(g, _):
        lanes = group_lanes(g)
        depthwise(ext, shifted, taps, mixed, lanes, False, rows)
        cells = mixed[:, :, lanes].reshape(px, LANES)
        mixed_out[:, lanes] = cells
        masked = cells * mask
        stats_out[0:1, lanes] = jnp.sum(masked, axis=0, keepdims=True)
        stats_out[1:2, lanes] = jnp.sum(masked * cells, axis=0, keepdims=True)
        return 0

    lax.fori_loop(0, width // LANES, group, 0)
    for keep in keeps:
        keep.wait()


def feed_kernel(
    at, mixed, stats, stats_other, sent, came, gain, bias, ocean, base, w_up, b_up, w_od,
    new_out, new_edge_out, state_out, norm_edge_out, inv_out, norm_out, slope_out, act_all,
    stack, rem, acc, acc_lo, hold_a, hold_b, hold_act, norm, slope, act_part, sems, *, turn, width, k_main, k_rem,
):
    core, part = at[0], at[1]
    px = mixed.shape[0]
    chunks = w_up.shape[1] // CHUNK
    part_px = act_part.shape[1]
    total = ocean_count(sent, came)
    keep_norm = pltpu.make_async_copy(norm, norm_out, sems.at[2 * chunks])

    for g in range(width // LANES):
        lanes = slice(g * LANES, (g + 1) * LANES)
        cells = mixed[:, lanes]
        average = (stats[0:1, lanes] + stats_other[0:1, lanes]) / total
        variance = (stats[1:2, lanes] + stats_other[1:2, lanes]) / total - average * average
        inverse = lax.rsqrt(variance + EPSILON)
        inv_out[:, lanes] = jnp.broadcast_to(inverse, (8, LANES))
        normalized = (cells - average) * inverse
        norm[:, lanes] = normalized
        normed = normalized * gain[:, lanes] + bias[:, lanes]
        high = normed.astype(BF16)
        high_f = high.astype(F32)
        low_f = normed - high_f
        if (g + 1) * LANES <= k_main:
            stack[:px, lanes] = high
            stack[px:, lanes] = low_f.astype(BF16)
        else:
            rem[...] = (high_f + pltpu.roll(low_f, k_rem, 1) + pltpu.roll(high_f, 2 * k_rem, 1)).astype(BF16)
    keep_norm.start()
    edge_px = norm_edge_out.shape[0]
    norm_edge_out[...] = norm[pl.ds(pl.multiple_of((1 - core) * (px - edge_px), 8), edge_px), :]

    def up(t, hold):
        cols = pl.ds(pl.multiple_of(t * CHUNK, CHUNK), CHUNK)
        both = dot(stack[...], w_up[:k_main, cols])
        high = dot(stack[:px], w_up[k_main : 2 * k_main, cols])
        rest = dot(rem[...], w_up[2 * k_main :, cols])
        hold[...] = (both[:px] + both[px:]) + (high + rest)

    def keep_slope(t):
        return pltpu.make_async_copy(slope.at[t], slope_out.at[t], sems.at[t])

    def keep_act(t):
        return pltpu.make_async_copy(act_part.at[t], act_all.at[t, pl.ds(turn * part_px, part_px)], sems.at[chunks + t])

    def act(t, hold):
        cols = pl.ds(pl.multiple_of(t * CHUNK, CHUNK), CHUNK)
        activated, slope[t] = gelu_both(hold[...] + b_up[:, cols])
        hold_act[...] = activated
        high, low = split(activated)
        acc[...] += dot(high, w_od[cols, :])
        acc_lo[...] += dot(low, w_od[cols, :LANES])
        act_part[t] = hold_act[pl.ds(pl.multiple_of(part * part_px, 8), part_px), :]
        keep_slope(t).start()
        keep_act(t).start()

    acc[...] = jnp.zeros_like(acc)
    acc_lo[...] = base[...]
    up(0, hold_a)

    def pair(i, _):
        up(2 * i + 1, hold_b)
        act(2 * i, hold_a)
        up(2 * i + 2, hold_a)
        act(2 * i + 1, hold_b)
        return 0

    lax.fori_loop(0, chunks // 2, pair, 0)
    act(chunks - 1, hold_a)
    new = (acc[:, :LANES] + acc[:, LANES:] + acc_lo[...]) * ocean[...]
    new_out[...] = new
    new_edge_out[...] = new_out[pl.ds(pl.multiple_of((1 - core) * (px - edge_px), 8), edge_px), :]
    mine = jnp.where(part == 0, new[:part_px], new[part_px:])
    state_out[...] = mine.T[: state_out.shape[0]]
    keep_norm.wait()
    for t in range(chunks):
        keep_slope(t).wait()
        keep_act(t).wait()


def back_kernel(*refs, finish, begin, turn, width, k_main, k_rem, states):
    refs = list(refs)

    def take(count):
        out = refs[:count]
        del refs[:count]
        return out

    (at, ocean, pending_in) = take(3)
    if finish:
        (grad_n, sent, came, norm, norm_edge, inv, gain, first_sent, first_came, grad_branch, window, taps, w_in_hi, w_in_lo) = take(14)
    if begin:
        (cots, slope_hbm, norm_now, w_out, w_od, w_up) = take(6)
    if finish:
        (carry_out, pending_out, taps_out, home_out, lift_all) = take(5)
    if begin:
        (branch_out, hidden_out, grad_n_out, send_out, masked_all) = take(5)
    if finish:
        (ext, shifted, mixed, grad_lift, lift_sem) = take(5)
    if begin:
        (cot, slope, masked_part, begin_sems) = take(4)
    core, part = at[0], at[1]
    px = ocean.shape[0]
    rows = px // COLS
    part_px = px // 2
    if begin:
        get_cot = pltpu.make_async_copy(cots.at[turn], cot, begin_sems.at[0])
        get_slope = pltpu.make_async_copy(slope_hbm, slope, begin_sems.at[1])
        get_cot.start()
        get_slope.start()
    if finish:
        edge_px = norm_edge.shape[0]
        total = ocean_count(first_sent, first_came)
        ocean_edge = first_came[:edge_px, 2 * LANES :]
        zeros = jnp.zeros((rows + 2 * HALO, 8, width), F32)
        ext[:, :8, :] = zeros
        ext[:, 8 + COLS :, :] = zeros
        ext[pl.ds((rows + HALO) * core, HALO), 8 : 8 + COLS, :] = jnp.zeros((HALO, COLS, width), F32)
        part_rows = window.shape[0] - 2 * HALO
        for g in range(width // LANES):
            lanes = slice(g * LANES, (g + 1) * LANES)
            bias_sum = (sent[edge_px : edge_px + 1, lanes] + came[edge_px : edge_px + 1, lanes]) / total
            gain_sum = (sent[edge_px + 1 : edge_px + 2, lanes] + came[edge_px + 1 : edge_px + 2, lanes]) / total
            scale = inv[0:1, lanes] * gain[:, lanes]
            mix = scale * (grad_n[:, lanes] - ocean[...] * (bias_sum + norm[:, lanes] * gain_sum))
            mix_edge = scale * (came[:edge_px, lanes] - ocean_edge * (bias_sum + norm_edge[:, lanes] * gain_sum))
            ext[HALO : HALO + rows, 8 : 8 + COLS, lanes] = mix.reshape(rows, COLS, LANES)
            ext[pl.ds((rows + HALO) * (1 - core), HALO), 8 : 8 + COLS, lanes] = mix_edge.reshape(HALO, COLS, LANES)

        def group(g, _):
            lanes = group_lanes(g)
            depthwise(ext, shifted, taps, mixed, lanes, True, rows)
            grad_lift[:, lanes] = mixed[:, :, lanes].reshape(px, LANES) + grad_branch[:, lanes]
            for q in range(KW):
                sums = [None] * KW
                for i in range(part_rows):
                    for v in range(0, COLS, 8):
                        grad = shifted[KW - 1 - q, HALO + part * part_rows + i, v : v + 8, :]
                        for p in range(KW):
                            term = grad * window[i + p, v : v + 8, lanes]
                            sums[p] = term if sums[p] is None else sums[p] + term
                for p in range(KW):
                    taps_out[p * KW + q : p * KW + q + 1, lanes] = jnp.sum(sums[p], axis=0, keepdims=True)
            return 0

        lax.fori_loop(0, width // LANES, group, 0)
        keep_lift = pltpu.make_async_copy(
            grad_lift.at[pl.ds(pl.multiple_of(part * part_px, 8), part_px)], lift_all.at[pl.ds((turn + 1) * part_px, part_px)], lift_sem
        )
        keep_lift.start()
        high, low = split(grad_lift[...])
        both = dot_t(jnp.concatenate([high, low], axis=0), w_in_hi[...])
        grad_x = (both[:px] + both[px:]) + dot_t(high, w_in_lo[...])
        carry = grad_x[:, LANES:] + pending_in[...]
        carry_out[...] = carry
        pending_out[...] = grad_x[:, :LANES]
        part_x = jnp.where(part == 0, grad_x[:part_px, :LANES], grad_x[part_px:, :LANES])
        part_c = jnp.where(part == 0, carry[:part_px], carry[part_px:])
        home_out[:LANES] = part_x.T
        home_out[LANES:] = part_c.T
    if begin:
        get_cot.wait()
        grad_new = cot[...] + carry if finish else cot[...]
        lane = lax.broadcasted_iota(jnp.int32, (px, LANES), 1)
        masked = jnp.where(lane < states, grad_new * ocean[...], 0.0)
        masked_part[...] = jnp.where(part == 0, masked[:part_px], masked[part_px:])
        keep_masked = pltpu.make_async_copy(masked_part, masked_all.at[pl.ds(turn * part_px, part_px)], begin_sems.at[2])
        keep_masked.start()
        high_f = masked.astype(BF16).astype(F32)
        nothing = jnp.zeros((px, LANES), F32)
        high_w = jnp.concatenate([high_f, nothing], axis=1)
        low_w = jnp.concatenate([masked - high_f, nothing], axis=1)
        left = (high_w + pltpu.roll(low_w, SEG, 1) + pltpu.roll(high_w, 2 * SEG, 1)).astype(BF16)
        branch_out[...] = dot(left, w_out[...])
        chunks = w_od.shape[1] // CHUNK
        get_slope.wait()

        def chunk(t, _):
            cols = pl.ds(pl.multiple_of(t * CHUNK, CHUNK), CHUNK)
            high, low = split(dot(left, w_od[:, cols]) * slope[t])
            hidden_out[:px, cols] = high
            hidden_out[px:, cols] = low
            return 0

        lax.fori_loop(0, chunks, chunk, 0)
        both = dot_t(hidden_out[...], w_up[:k_main])
        grad_n_out[:, :k_main] = (both[:px] + both[px:]) + dot_t(hidden_out[:px], w_up[k_main : 2 * k_main])
        rest = dot_t(hidden_out[...], w_up[2 * k_main :])
        tail = rest[:px] + rest[px:] + pltpu.roll(rest[:px], LANES - 2 * k_rem, 1)
        grad_n_out[:, k_main:] = jnp.where(lane < k_rem, tail, 0.0)
        edge_px = send_out.shape[0] - 8
        for g in range(width // LANES):
            lanes = slice(g * LANES, (g + 1) * LANES)
            cells = grad_n_out[:, lanes]
            send_out[edge_px : edge_px + 1, lanes] = jnp.sum(cells, axis=0, keepdims=True)
            send_out[edge_px + 1 : edge_px + 2, lanes] = jnp.sum(cells * norm_now[:, lanes], axis=0, keepdims=True)
        send_out[edge_px + 2 :, :] = jnp.zeros((6, width), F32)
        send_out[:edge_px, :] = grad_n_out[pl.ds(pl.multiple_of((1 - core) * (px - edge_px), 8), edge_px), :]
        keep_masked.wait()
    if finish:
        keep_lift.wait()


def weight_kernel(at, norm, gain, bias, hidden, send, *rest, quarter, finish):
    if finish:
        taps, keep_in, give_in, sums_in, keep_out, give_out, sums_out = rest
    else:
        keep_out, give_out, sums_out = rest
    core = at[0]
    part = at[1]
    px = norm.shape[0]
    tap_rows = sums_out.shape[0] - 8
    if finish:
        sums_out[:tap_rows] = sums_in[:tap_rows] + taps[...]
        sums_out[tap_rows:] = sums_in[tap_rows:] + send[send.shape[0] - 8 :]
    else:
        sums_out[:tap_rows] = jnp.zeros((tap_rows, sums_out.shape[1]), F32)
        sums_out[tap_rows:] = send[send.shape[0] - 8 :]
    window = round_up(quarter, LANES)
    base = (quarter // LANES) * LANES
    normed = norm[...] * gain[...] + bias[...]
    second = pltpu.roll(normed[:, base : base + window], window - (quarter - base), 1)
    mine = jnp.where(part == 0, normed[:, :window], second)
    lane = lax.broadcasted_iota(jnp.int32, (px, window), 1)
    mine = jnp.where(lane < quarter, mine, jnp.where(lane == quarter, 1.0, 0.0))
    high, low = split(mine.T[: keep_out.shape[0]])
    half = keep_out.shape[1]

    def chunk(side, start, size):
        acc_out = (keep_out, give_out)[side]
        here = pl.ds(start, size)
        actual = core if side == 0 else 1 - core
        cols = pl.ds(pl.multiple_of(actual * half + start, LANES), size)
        new = dot(high, hidden[:px, cols]) + dot(high, hidden[px:, cols]) + dot(low, hidden[:px, cols])
        acc_out[:, here] = (keep_in, give_in)[side][:, here] + new if finish else new

    for side in range(2):

        def step(t, _):
            chunk(side, pl.multiple_of(t * CHUNK, CHUNK), CHUNK)
            return 0

        lax.fori_loop(0, half // CHUNK, step, 0)
        if half % CHUNK:
            chunk(side, half // CHUNK * CHUNK, half % CHUNK)


VMEM_SPEC = pl.BlockSpec(memory_space=pltpu.VMEM)
SMEM_SPEC = pl.BlockSpec(memory_space=pltpu.SMEM)
HBM_SPEC = pl.BlockSpec(memory_space=pltpu.HBM)


def out(*shape, dtype=F32):
    return jax.ShapeDtypeStruct(shape, dtype)


def in_hbm(values):
    return pltpu.with_memory_space_constraint(values, pltpu.HBM)


def call(kernel, name, args, outs, scratch, limit, *, micros, smem=0, hbm=(), hbm_outs=(), vmem_outs=(), aliases=None, stacked=()):
    args = [in_hbm(a) if i in hbm else a for i, a in enumerate(args)]
    specs = [SMEM_SPEC if i < smem else HBM_SPEC if i in hbm else VMEM_SPEC for i in range(len(args))]
    hbm_outs = tuple(hbm_outs) + tuple(i for i, _ in stacked)
    aliases = dict(aliases or {})
    used = len(args)
    for i, buffer in stacked:
        if buffer is not None:
            aliases[len(args)] = i
            args.append(in_hbm(buffer))
            specs.append(HBM_SPEC)
    extra = len(args) - used

    def body(*refs):
        kernel(*refs[:used], *refs[used + extra :])

    return pl.pallas_call(
        body,
        in_specs=specs,
        out_specs=[HBM_SPEC if i in hbm_outs else VMEM_SPEC for i in range(len(outs))],
        out_shape=[
            pltpu.HBM(o.shape, o.dtype) if i in hbm_outs else pltpu.VMEM(o.shape, o.dtype) if i in vmem_outs else o
            for i, o in enumerate(outs)
        ],
        scratch_shapes=scratch,
        input_output_aliases=aliases,
        compiler_params=pltpu.CompilerParams(vmem_limit_bytes=limit * MIB),
        cost_estimate=pl.CostEstimate(flops=int(micros * 1.1e9), bytes_accessed=1024, transcendentals=0),
        name=name,
    )(*args)


def start_kernel(at, first, second, prev_out, cur_out, ocean_out, send_out, *, states, forces):
    core, part = at[0], at[1]
    block = first.shape[1]
    rows = first.shape[0]
    mask_row = 2 * states + forces

    def turn(values):
        prev = jnp.concatenate([values[: states + forces], jnp.zeros((LANES - states - forces, block), F32)], axis=0).T
        cur = jnp.concatenate([values[states + forces : mask_row], jnp.zeros((LANES - states, block), F32)], axis=0).T
        mask = jnp.broadcast_to(values[mask_row : mask_row + 1], (LANES, block)).T
        return prev, cur, mask

    zero, one = first[...], second[...]
    swap = part == 1
    top, low = jnp.where(swap, one, zero), jnp.where(swap, zero, one)
    count = jnp.sum(top[mask_row : mask_row + 1]) + jnp.sum(low[mask_row : mask_row + 1])
    for i, values in enumerate((top, low)):
        prev, cur, mask = turn(values)
        here = slice(i * block, (i + 1) * block)
        prev_out[here] = prev
        cur_out[here] = cur
        ocean_out[here] = mask
    at_edge = pl.ds(pl.multiple_of((1 - core) * block, 8), block)
    send_out[:block, :LANES] = prev_out[at_edge, :]
    send_out[:block, LANES : 2 * LANES] = cur_out[at_edge, :]
    send_out[:block, 2 * LANES :] = ocean_out[at_edge, :]
    send_out[block:] = jnp.full((8, 3 * LANES), count)


def pack_kernel(at, first, second, force_out, force_send, cot_out, *, states, forces):
    core, part = at[0], at[1]
    steps, rows, block = first.shape
    lane = lax.broadcasted_iota(jnp.int32, (block, LANES), 1)
    for j in range(steps):
        turned = [
            jnp.concatenate([values[j], jnp.zeros((LANES - rows, block), F32)], axis=0).T for values in (first, second)
        ]
        top, low = jnp.where(part == 1, turned[1], turned[0]), jnp.where(part == 1, turned[0], turned[1])
        for i, values in enumerate((top, low)):
            cot_out[j, i * block : (i + 1) * block] = jnp.where(lane < states, values, 0.0)
            force_out[j, i * block : (i + 1) * block] = jnp.where(lane < states, 0.0, values)
        force_send[j] = force_out[j, pl.ds(pl.multiple_of((1 - core) * block, 8), block), :]


def reorder(source, target, spans):
    for start, size, place in spans:
        target[:, place : place + size] = source[:, start : start + size]


def up_kernel(w_up_t, up_all, raw, turned, sems, *, k_main, k_rem, spans):
    slots, block = raw.shape[0], raw.shape[1]
    blocks = k_main // block

    def get(t, size):
        slot = lax.rem(t, slots)
        return pltpu.make_async_copy(
            w_up_t.at[pl.ds(pl.multiple_of(t * block, 8), size)], raw.at[slot, pl.ds(0, size)], sems.at[slot]
        )

    for t in range(slots):
        get(t, block).start()
    turned[...] = jnp.zeros_like(turned)

    def main(t, _):
        get(t, block).wait()
        reorder(raw.at[lax.rem(t, slots)], turned, spans)

        @pl.when(t + slots < blocks)
        def _():
            get(t + slots, block).start()

        @pl.when(t + slots == blocks)
        def _():
            get(t + slots, k_rem).start()

        high, low = split(turned[...])
        up_all[pl.ds(pl.multiple_of(t * block, block), block), :] = high
        up_all[pl.ds(pl.multiple_of(k_main + t * block, block), block), :] = low
        return 0

    lax.fori_loop(0, blocks, main, 0)
    get(blocks, k_rem).wait()
    reorder(raw.at[blocks % slots, pl.ds(0, k_rem)], turned.at[pl.ds(0, k_rem)], spans)
    high, low = split(turned[:k_rem])
    base = 2 * k_main
    up_all[base : base + k_rem] = high
    up_all[base + k_rem : base + 2 * k_rem] = high
    up_all[base + 2 * k_rem : base + 3 * k_rem] = low
    up_all[base + 3 * k_rem :] = jnp.zeros((LANES - 3 * k_rem, up_all.shape[1]), BF16)


def down_kernel(w_down, out_parts, od_fwd, od_bwd, down, product, ordered, sems, *, spans):
    pieces = sems.shape[0]
    piece = down.shape[1] // pieces

    def get(t):
        cols = pl.ds(pl.multiple_of(t * piece, LANES), piece)
        return pltpu.make_async_copy(w_down.at[:, cols], down.at[:, cols], sems.at[t])

    for t in range(pieces):
        get(t).start()
    ordered[...] = jnp.zeros_like(ordered)

    def multiply(t, _):
        cols = pl.ds(pl.multiple_of(t * piece, LANES), piece)
        get(t).wait()
        high, low = split(down[:, cols])
        both = dot(out_parts[...], high)
        product[:, cols] = (both[:SEG] + both[SEG:]) + dot(out_parts[:SEG], low)
        return 0

    lax.fori_loop(0, pieces, multiply, 0)
    reorder(product, ordered.at[pl.ds(0, SEG)], spans)

    def spread(t, _):
        cols = pl.ds(pl.multiple_of(t * CHUNK, CHUNK), CHUNK)
        values = ordered[:, cols]
        high, low = split(values)
        od_bwd[:SEG, cols] = high[:SEG]
        od_bwd[SEG : 2 * SEG, cols] = high[:SEG]
        od_bwd[2 * SEG : 3 * SEG, cols] = low[:SEG]
        od_bwd[3 * SEG :, cols] = jnp.zeros((od_bwd.shape[0] - 3 * SEG, CHUNK), BF16)
        high, low = split(values.T)
        od_fwd[cols, :LANES] = high
        od_fwd[cols, LANES:] = low
        return 0

    lax.fori_loop(0, ordered.shape[1] // CHUNK, spread, 0)


def last_kernel(
    at, masked_hbm, x_hbm, lifts_hbm, lifted_hbm, act_hbm, down_hbm, b_down, sums, taps, table, hidden_keep, hidden_give,
    masked, x_parts, lifts, lifted, act, down, masked_t, x_t, g_hidden, natural, g_parts, sems, *, spans, blocks,
):
    chunks = act.shape[0]
    half = hidden_keep.shape[1]
    width = table.shape[1]
    scale = (at[1] == 0).astype(F32)
    tap_rows = taps.shape[0]
    pairs = [(masked_hbm, masked), (x_hbm, x_parts), (lifts_hbm, lifts), (lifted_hbm, lifted)]
    firsts = [pltpu.make_async_copy(pair[0], pair[1], sems.at[i]) for i, pair in enumerate(pairs)]
    downs = [
        pltpu.make_async_copy(down_hbm.at[pl.ds(start, size)], down.at[pl.ds(start, size)], sems.at[4 + i])
        for i, (start, size) in enumerate(blocks)
    ]

    def get(t):
        return pltpu.make_async_copy(act_hbm.at[t], act.at[t], sems.at[4 + len(blocks) + t])

    firsts[0].start()
    for t in range(chunks):
        get(t).start()
    for copy in firsts[1:] + downs:
        copy.start()
    firsts[0].wait()
    turned = masked[...].T[:SEG]
    high = turned.astype(BF16)
    masked_t[:SEG] = high
    masked_t[SEG:] = (turned - high.astype(F32)).astype(BF16)
    total = jnp.sum(turned, axis=1, keepdims=True)

    def chunk(t, _):
        get(t).wait()
        high, low = split(act[t])
        both = dot(masked_t[...], high)
        sums_now = (both[:SEG] + both[SEG:]) + dot(masked_t[:SEG], low)
        g_hidden[:, pl.ds(pl.multiple_of(t * CHUNK, CHUNK), CHUNK)] = sums_now
        return 0

    lax.fori_loop(0, chunks, chunk, 0)
    hidden_keep[...] = g_hidden[:, pl.ds(pl.multiple_of(at[0] * half, LANES), half)]
    hidden_give[...] = g_hidden[:, pl.ds(pl.multiple_of((1 - at[0]) * half, LANES), half)]
    for start, size, place in spans:
        natural[:, start : start + size] = g_hidden[:, place : place + size]
    high, low = split(natural[...])
    g_parts[:SEG] = high
    g_parts[SEG:] = low
    for copy in firsts[1:]:
        copy.wait()
    high, low = split(x_parts[...].T)
    x_t[0] = high
    x_t[1] = low
    for start in range(0, width, CHUNK):
        size = min(CHUNK, width - start)
        lanes = slice(start, start + size)
        high, low = split(lifted[:, :, lanes].reshape(lifts.shape[0], size))
        both = dot(masked_t[...], high)
        lifted_sum = (both[:SEG] + both[SEG:]) + dot(masked_t[:SEG], low)
        grads = lifts[:, lanes]
        high, low = split(grads)
        g_in = dot(x_t[0], high) + dot(x_t[1], high) + dot(x_t[0], low)
        table[:88, lanes] = g_in[:88]
        table[88:168, lanes] = g_in[LANES : LANES + 80]
        table[168:224, lanes] = sums[:tap_rows, lanes] + taps[:, lanes]
        table[224:304, lanes] = lifted_sum + total * b_down[:, lanes]
        table[304:311, lanes] = sums[tap_rows : tap_rows + 7, lanes] * scale
        table[311:312, lanes] = jnp.sum(grads, axis=0, keepdims=True)
    for (start, size), copy in zip(blocks, downs):
        copy.wait()
        high, low = split(down[start : start + size])
        both = dot_t(g_parts[...], high)
        g_out = (both[:SEG] + both[SEG:]) + dot_t(g_parts[:SEG], low)
        table[224:304, start : start + size] += g_out


def pad_to(values, shape):
    return jnp.pad(values, [(0, size - have) for size, have in zip(shape, values.shape)])


def per_device(
    init_states, forcing, history, land_mask, w_in, b_in, w_dw, bn_gain, bn_bias, w_up, b_up, w_down, b_down, w_out, b_out, cotangent
):
    steps = lax.axis_size("step")
    devices_z = lax.axis_size("rows")
    step = lax.axis_index("step")
    depth = lax.axis_index("rows")
    core, pair = step % 2, step // 2
    side, part = depth % 2, depth // 2
    both_axes = ("step", "rows")
    block = land_mask.shape[0]
    px = 2 * block
    rows = px // COLS
    states = w_out.shape[0]
    forces = forcing.shape[2]
    channels = w_up.shape[1]
    hidden = w_up.shape[0]
    width = round_up(channels, LANES)
    ff_block = hidden // steps
    half = round_up(hidden // 2, LANES)
    wide = 2 * half
    spans = [(s * ff_block, ff_block, (s % 2) * half + (s // 2) * ff_block) for s in range(steps)]
    k_main = channels // CHUNK * CHUNK
    k_rem = channels - k_main
    col_block = channels // devices_z

    def place(s, z):
        return s * devices_z + z

    cells = [(k, c, h, q) for k in range(steps // 2) for c in range(2) for h in range(2) for q in range(2)]
    fetch_perms = [
        [(place(2 * k + q, 2 * c + (b ^ h)), place(2 * k + c, 2 * h + q)) for k, c, h, q in cells] for b in range(2)
    ]

    siblings = [(s, s ^ 1) for s in range(steps)]

    def to_sibling(values):
        return lax.ppermute(values, "step", siblings)

    def shift_back(values, j):
        return values if j == 0 else lax.ppermute(values, "step", [((s + j) % steps, s) for s in range(steps)])

    def fetch_own(values):
        got = [lax.ppermute(values, both_axes, perm) for perm in fetch_perms]
        return got

    def turn_round(values):
        doubled = jnp.flip(jnp.concatenate([values, values]), axis=0)
        return lax.dynamic_slice_in_dim(doubled, steps - 1 - step, steps, axis=0)

    def rotate(values, by):
        return lax.dynamic_slice_in_dim(jnp.concatenate([values, values]), by, steps, axis=0)

    def from_later(values):
        if steps == ROLL:
            return rotate(lax.all_to_all(turn_round(values), "step", 0, 0, tiled=True), step)
        return jnp.stack([shift_back(values[j], j) for j in range(ROLL)])

    def to_later(values):
        if steps == ROLL:
            return turn_round(lax.all_to_all(rotate(values, (steps - step) % steps), "step", 0, 0, tiled=True))
        return jnp.stack([lax.ppermute(values[j], "step", [(s, (s + j) % steps) for s in range(steps)]) for j in range(ROLL)])

    at = jnp.stack([core, part]).astype(jnp.int32)
    mask_row = land_mask.astype(F32)[None]
    current = init_states[0, 0, 1]
    previous = jnp.where(history[0, 0] == 2, init_states[0, 0, 0], current)
    payload = jnp.concatenate([previous, forcing[0, 0], current, mask_row], axis=0)
    timed = jnp.concatenate([cotangent[0, :, 0], jnp.broadcast_to(forcing[0], (ROLL,) + forcing.shape[2:])], axis=1)
    payload, timed = lax.optimization_barrier((payload, timed))
    payload = fetch_own(payload)
    timed = from_later(timed)

    def in_rows(values):
        top = jnp.concatenate([values[:states], values[2 * states :]], axis=0)
        bottom = values[states : 2 * states]
        return jnp.concatenate([jnp.pad(v, ((0, LANES - v.shape[0]), (0, 0))) for v in (top, bottom)], axis=0)

    def row(values, size):
        return jnp.pad(values, (0, size - values.shape[0]))[None]

    w_in_hi, w_in_lo = split_outside(pad_to(in_rows(w_in.T), (2 * LANES, width)))
    w_oi = pad_to(in_rows(jnp.dot(w_out, w_in, precision=HIGHEST).T), (2 * LANES, LANES))
    w_oi_hi, w_oi_lo = split_outside(w_oi)
    b_new = row(jnp.dot(w_out, b_in + b_down, precision=HIGHEST) + b_out, LANES)
    taps = jnp.broadcast_to(
        pad_to(w_dw.reshape(channels, KW * KW).T, (KW * KW, width))[:, None], (KW * KW, 8, width)
    )
    gain, bias = row(bn_gain, width), row(bn_bias, width)
    row_hi, row_lo = split_outside(pad_to(w_out, (SEG, channels)))
    out_parts = jnp.concatenate([row_hi, row_lo], axis=0)
    pieces = 5
    w_od_fwd, w_od_bwd = call(
        functools.partial(down_kernel, spans=spans), "down", (w_down, out_parts),
        [out(wide, 2 * LANES, dtype=BF16), out(2 * LANES, wide, dtype=BF16)],
        [pltpu.VMEM((channels, hidden), F32), pltpu.VMEM((SEG, hidden), F32), pltpu.VMEM((LANES, wide), F32), pltpu.SemaphoreType.DMA((pieces,))],
        20, micros=7, hbm=(0,), vmem_outs=(0, 1),
    )
    out_hi, out_lo = split_outside(pad_to(w_out, (SEG, width)))
    w_out_bwd = pad_to(jnp.concatenate([out_hi, out_hi, out_lo], axis=0), (2 * LANES, width))
    b_in_row = row(b_in, width)
    b_up_row = pad_to(b_up.reshape(steps // 2, 2, ff_block).swapaxes(0, 1).reshape(2, hidden // 2), (2, half)).reshape(1, wide)
    b_down_row = row(b_down, width)
    prev, cur, ocean, first_sent = call(
        functools.partial(start_kernel, states=states, forces=forces), "start", (at, *payload),
        [out(px, LANES), out(px, LANES), out(px, LANES), out(block + 8, 3 * LANES)], [], 4, micros=1, smem=1,
    )
    first_came = to_sibling(first_sent)
    ready = lax.optimization_barrier(
        (w_up.T, timed, w_in_hi, w_in_lo, w_oi_hi, w_oi_lo, b_new, taps, gain, bias, w_out_bwd, b_in_row, b_up_row, b_down_row, at, first_sent)
    )
    up_source, timed, w_in_hi, w_in_lo, w_oi_hi, w_oi_lo, b_new, taps, gain, bias, w_out_bwd, b_in_row, b_up_row, b_down_row, at, first_sent = ready
    timed = fetch_own(timed)
    (w_up_all,) = call(
        functools.partial(up_kernel, k_main=k_main, k_rem=k_rem, spans=spans), "up", (up_source,),
        [out(2 * k_main + LANES, wide, dtype=BF16)],
        [pltpu.VMEM((3, k_main // 8, hidden), F32), pltpu.VMEM((k_main // 8, wide), F32), pltpu.SemaphoreType.DMA((3,))],
        10, micros=7, hbm=(0,), vmem_outs=(0,),
    )
    first_came, w_up_all = lax.optimization_barrier((first_came, w_up_all))
    force, force_send, cots = call(
        functools.partial(pack_kernel, states=states, forces=forces), "pack", (at, *timed),
        [out(ROLL, px, LANES), out(ROLL, block, LANES), out(ROLL, px, LANES)], [], 6, micros=2, smem=1,
    )
    force_edge = to_sibling(force_send)

    chunks = wide // CHUNK
    x_all, lifted_all, act_all = None, None, None
    kept, predicted = [], []
    prev_edge, cur_edge, prev_lanes, cur_lanes = first_came, first_came, 0, LANES
    for j in range(ROLL):
        mixed, stats, base, window, x_all, lifted_all = call(
            functools.partial(mix_kernel, turn=j, cur_lanes=cur_lanes, prev_lanes=prev_lanes), "mix",
            (at, cur, cur_edge, prev, prev_edge) + ((force, force_edge) if j else (at, at)) + (w_in_hi, w_in_lo, b_in_row, w_oi_hi, w_oi_lo, b_new, taps, ocean),
            [
                out(px, width), out(8, width), out(px, LANES), out(HALO + 2 * HALO, COLS, width), out(ROLL * block, 2 * LANES),
                out(ROLL * HALO, COLS, width),
            ],
            [
                pltpu.VMEM((rows + 2 * HALO, COLS + 16, width), F32), pltpu.VMEM((KW, rows + 2 * HALO, COLS, LANES), F32),
                pltpu.VMEM((rows, COLS, width), F32), pltpu.VMEM((block, 2 * LANES), F32), pltpu.SemaphoreType.DMA((3,)),
            ],
            12, micros=4.5, smem=1, hbm_outs=(3,), stacked=((4, x_all), (5, lifted_all)),
        )
        stats_other = to_sibling(stats)
        new, new_edge, state, norm_edge, inv, norm, slope, act_all = call(
            functools.partial(feed_kernel, turn=j, width=width, k_main=k_main, k_rem=k_rem), "feed",
            (at, mixed, stats, stats_other, first_sent, first_came, gain, bias, ocean, base, w_up_all, b_up_row, w_od_fwd),
            [
                out(px, LANES), out(block, LANES), out(SEG, block), out(block, width), out(8, width), out(px, width),
                out(chunks, px, CHUNK), out(chunks, ROLL * block, CHUNK),
            ],
            [
                pltpu.VMEM((2 * px, k_main), BF16), pltpu.VMEM((px, LANES), BF16),
                pltpu.VMEM((px, CHUNK), F32), pltpu.VMEM((px, LANES), F32), pltpu.VMEM((px, CHUNK), F32), pltpu.VMEM((px, CHUNK), F32),
                pltpu.VMEM((px, CHUNK), F32), pltpu.VMEM((px, width), F32), pltpu.VMEM((chunks, px, CHUNK), F32),
                pltpu.VMEM((chunks, block, CHUNK), F32), pltpu.SemaphoreType.DMA((2 * chunks + 1,)),
            ],
            14, micros=8.5, smem=1, hbm_outs=(5, 6), stacked=((7, act_all),),
        )
        prev, prev_edge, prev_lanes, cur = cur, cur_edge, cur_lanes, new
        if j < ROLL - 1:
            cur_edge, cur_lanes = to_sibling(new_edge), 0
        norm_edge = to_sibling(norm_edge)
        predicted.append(state)
        kept.append((window, norm, norm_edge, slope, inv))

    quarter = channels // 2
    acc_rows = round_up(quarter + 1, 8)
    tap_rows = round_up(KW * KW, 8)
    carry, pending = None, jnp.zeros((px, LANES), F32)
    previous_step, keep_acc, give_acc, sums, lift_all, masked_all = None, None, None, None, None, None
    homes = []
    begin_scratch = [
        pltpu.VMEM((px, LANES), F32), pltpu.VMEM((chunks, px, CHUNK), F32), pltpu.VMEM((block, LANES), F32), pltpu.SemaphoreType.DMA((3,)),
    ]
    finish_scratch = [
        pltpu.VMEM((rows + 2 * HALO, COLS + 16, width), F32), pltpu.VMEM((KW, rows + 2 * HALO, COLS, LANES), F32),
        pltpu.VMEM((rows, COLS, width), F32), pltpu.VMEM((px, width), F32), pltpu.SemaphoreType.DMA,
    ]
    for j in range(ROLL - 1, -2, -1):
        finish, begin = j < ROLL - 1, j >= 0
        if finish:
            pending, keep_acc, give_acc = lax.optimization_barrier((pending, keep_acc, give_acc))
        args, outs, scratch, stacked, hbm = [at, ocean, pending], [], [], [], ()
        if finish:
            window, norm, norm_edge, slope, inv = kept[j + 1]
            grad_n, sent, came, grad_branch = previous_step
            args += [grad_n, sent, came, norm, norm_edge, inv, gain, first_sent, first_came, grad_branch, window, taps, w_in_hi, w_in_lo]
            outs += [out(px, LANES), out(px, LANES), out(tap_rows, width), out(2 * LANES, block), out(ROLL * block, width)]
            stacked.append((4, lift_all))
            scratch += finish_scratch
        if begin:
            hbm = (len(args), len(args) + 1)
            args += [cots, kept[j][3], kept[j][1], w_out_bwd, w_od_bwd, w_up_all]
            outs += [out(px, width), out(2 * px, wide, dtype=BF16), out(px, width), out(block + 8, width), out(ROLL * block, LANES)]
            stacked.append((len(outs) - 1, masked_all))
            scratch += begin_scratch
        kernel = functools.partial(
            back_kernel, finish=finish, begin=begin, turn=j, width=width, k_main=k_main, k_rem=k_rem, states=states
        )
        results = list(
            call(kernel, "back", args, outs, scratch, 18, micros=7 * finish + 7.5 * begin, smem=1, hbm=hbm, stacked=stacked)
        )
        if finish:
            carry, pending, tap_sum, home, lift_all = results[:5]
            results = results[5:]
            homes.append(home)
        if begin:
            grad_branch, hidden_now, grad_n, sent, masked_all = results
            came = to_sibling(sent)
            previous_step = (grad_n, sent, came, grad_branch)
            keep_acc, give_acc, sums = call(
                functools.partial(weight_kernel, quarter=quarter, finish=finish), "weight",
                (at, kept[j][1], gain, bias, hidden_now, sent) + ((tap_sum, keep_acc, give_acc, sums) if finish else ()),
                [out(acc_rows, half), out(acc_rows, half), out(tap_rows + 8, width)], [], 8, micros=5, smem=1,
                aliases=({7: 0, 8: 1, 9: 2} if j else {7: 0, 9: 2}) if finish else None, vmem_outs=(0, 1, 2) if j else (),
            )

    def trade(values, axis, flip):
        return lax.ppermute(values, axis, [(i, i ^ flip) for i in range(lax.axis_size(axis))])

    def pick(first, second, bit):
        return jnp.where(bit == 0, first, second), jnp.where(bit == 0, second, first)

    def at_index(values, index):
        return lax.dynamic_index_in_dim(values, index, keepdims=False)

    def cut(values, k):
        return values[..., k * ff_block : (k + 1) * ff_block]

    def sum_z(values):
        near = values + trade(values, "rows", 1)
        return near + trade(near, "rows", 2)

    direct = steps == 8 and devices_z == 4
    bit_x, bit_y = pair % 2, pair // 2
    mine_up = keep_acc + trade(give_acc, "step", 1)
    masked_all, mine_up, lift_all = lax.optimization_barrier((masked_all, mine_up, lift_all))
    if direct:
        rows_a, rows_b = mine_up[:col_block], mine_up[col_block : 2 * col_block]
        even = jnp.stack([cut(rows_a, 0), cut(rows_a, 2)])
        odd = jnp.stack([cut(rows_a, 1), cut(rows_a, 3)])
        keep_a, give_a = pick(even, odd, bit_x)
        low = jnp.stack([cut(rows_b, 0), cut(rows_b, 1)])
        top = jnp.stack([cut(rows_b, 2), cut(rows_b, 3)])
        keep_b, give_b = pick(low, top, bit_y)
        got_a = keep_a + trade(give_a, "step", 2)
        got_b = keep_b + trade(give_b, "step", 4)
    part_px = ROLL * block
    blocks = [(start, min(CHUNK, channels - start)) for start in range(0, channels, CHUNK)]
    table, hidden_keep, hidden_give = call(
        functools.partial(last_kernel, spans=spans, blocks=blocks), "last",
        (
            at, masked_all, x_all, lift_all, lifted_all, act_all, w_down, b_down_row, sums, tap_sum,
        ),
        [out(312, width), out(SEG, half), out(SEG, half)],
        [
            pltpu.VMEM((part_px, LANES), F32), pltpu.VMEM((part_px, 2 * LANES), F32), pltpu.VMEM((part_px, width), F32),
            pltpu.VMEM(lifted_all.shape, F32), pltpu.VMEM((chunks, part_px, CHUNK), F32), pltpu.VMEM((channels, hidden), F32),
            pltpu.VMEM((2 * SEG, part_px), BF16), pltpu.VMEM((2, 2 * LANES, part_px), BF16), pltpu.VMEM((SEG, wide), F32),
            pltpu.VMEM((SEG, hidden), F32), pltpu.VMEM((2 * SEG, hidden), BF16),
            pltpu.SemaphoreType.DMA((4 + len(blocks) + chunks,)),
        ],
        44, micros=12, smem=1, hbm=(1, 2, 3, 4, 5, 6),
    )
    if direct:
        table, got_a, got_b = lax.optimization_barrier((table, got_a, got_b))
    first_table = table
    up_row = jnp.stack(pick(keep_acc[quarter], give_acc[quarter], core)).reshape(wide) * (part == 0).astype(F32)
    masked_sum = jnp.sum(masked_all, axis=0)
    extra = jnp.concatenate([pad_to(up_row, (4 * width,)).reshape(4, width), row(masked_sum, width), jnp.zeros((3, width), F32)], axis=0)
    table = jnp.concatenate([table, extra], axis=0)
    mine_down = hidden_keep + trade(hidden_give, "step", 1)
    if direct:
        table = table.reshape(2, -1, width)
        own = at_index(table, core) + trade(at_index(table, 1 - core), "step", 1)
        own = own.reshape(4, -1, width)
        rest = [trade(at_index(own, pair ^ b), "step", 2 * b) for b in (1, 2, 3)]
        own = (at_index(own, pair) + rest[0]) + (rest[1] + rest[2])

        keep_a, give_a = pick(got_a[0], got_a[1], bit_y)
        keep_b, give_b = pick(got_b[0], got_b[1], bit_x)
        got_a = keep_a + trade(give_a, "step", 4)
        got_b = keep_b + trade(give_b, "step", 2)

        rest = [trade(own, "rows", b) for b in (1, 2, 3)]
        own = (own + rest[0]) + (rest[1] + rest[2])
        keep, give = pick(got_a, got_b, side)
        share_up = (keep + trade(give, "rows", 1)).T
        rest = jnp.stack([own] + [trade(own, "step", 2 * b) for b in (1, 2, 3)])
        own = jnp.concatenate([at_index(rest, pair ^ b) for b in range(4)], axis=0)
        other = trade(own, "step", 1)
        table = jnp.concatenate(pick(own, other, core), axis=0)

        pieces = jnp.stack([cut(mine_down, k) for k in range(4)])
        near = at_index(pieces, pair) + trade(at_index(pieces, pair ^ 1), "step", 2)
        far = trade(at_index(pieces, pair ^ 2), "step", 4) + trade(at_index(pieces, pair ^ 3), "step", 6)
        hidden_share = sum_z(near + far)
    else:
        units = steps // 2
        same_core = [[2 * k + c for k in range(units)] for c in range(2)]
        share = lax.psum_scatter(mine_up[:, : hidden // 2], "step", scatter_dimension=1, axis_index_groups=same_core, tiled=True)
        keep, give = pick(share[:col_block], share[col_block : 2 * col_block], side)
        share_up = (keep + trade(give, "rows", 1)).T
        hidden_share = lax.psum(
            lax.psum_scatter(mine_down[:, : hidden // 2], "step", scatter_dimension=1, axis_index_groups=same_core, tiled=True), "rows"
        )
        table = lax.psum(table, both_axes)

    g_w_in = jnp.concatenate([table[:states], table[88 : 88 + states], table[states : states + forces]], axis=0)[:, :channels].T
    g_w_dw = table[168 : 168 + KW * KW, :channels].T.reshape(channels, KW, KW)
    g_w_out = table[224 : 224 + states, :channels]
    g_bias, g_gain, g_b_in = table[304, :channels], table[305, :channels], table[311, :channels]
    g_b_up = table[312:316].reshape(-1)[:wide].reshape(2, half)[:, : hidden // 2].reshape(2, steps // 2, ff_block).swapaxes(0, 1).reshape(-1)
    g_b_out = table[316, :states]
    g_b_down = jnp.sum(w_out * g_b_out[:, None], axis=0)

    *late, _ = lax.optimization_barrier((*predicted, *homes, first_table))
    predicted, homes = late[:ROLL], late[ROLL:]
    going = jnp.stack([jnp.concatenate([predicted[j][:states], homes[ROLL - 1 - j][states : states + forces]], axis=0) for j in range(ROLL)])
    ending = jnp.concatenate([homes[-1][:states], homes[-1][LANES : LANES + states]], axis=0)
    flat = jnp.concatenate([going.reshape(-1, block), ending], axis=0)
    flat = lax.ppermute(flat, both_axes, [(place(2 * k + c, 2 * h + q), place(2 * k + q, 2 * c + h)) for k, c, h, q in cells])
    gone = to_later(flat[: going.shape[0] * going.shape[1]].reshape(going.shape))
    grad_prev, grad_cur = flat[-2 * states : -states], flat[-states:]
    grad_forcing = jnp.sum(gone[:, states:], axis=0)[None, None]
    grad_init_prev = jnp.where(history[0, 0] == 2, grad_prev, 0.0)
    grad_init_cur = grad_cur + jnp.where(history[0, 0] == 1, grad_prev, 0.0)
    grad_init = jnp.stack([grad_init_prev, grad_init_cur])[None, None]
    w_out_block = lax.dynamic_slice_in_dim(w_out, depth * col_block, col_block, axis=1)
    share_down = lax.dot_general(
        w_out_block, hidden_share[:states], (((0,), (0,)), ((), ())), precision=lax.Precision.HIGH, preferred_element_type=F32
    )
    return (
        gone[None, :, None, :states],
        grad_init,
        grad_forcing,
        g_w_in,
        g_b_in,
        g_w_dw,
        g_gain,
        g_bias,
        share_up,
        g_b_up,
        share_down,
        g_b_down,
        g_w_out,
        g_b_out,
    )


def solution(mesh):
    state_spec = P("step", None, None, None, "rows")
    force_spec = P("step", None, None, "rows")
    in_specs = (state_spec, force_spec, P("step", None), P("rows")) + (P(),) * 11 + (state_spec,)
    out_specs = (state_spec, state_spec, force_spec) + (P(),) * 5 + (P("step", "rows"), P(), P("rows", "step"), P(), P(), P())
    return jax.shard_map(per_device, mesh=mesh, in_specs=in_specs, out_specs=out_specs, check_vma=False)
```

time: 956 us -> 501 us (0.52)
  local copies, waits for them, and re-layouts: 312 us -> 47.1 us
  waiting for transfers between devices: 135 us -> 57.1 us
  matrix products: 33.2 us -> 2.1 us
  Pallas kernels: 323 us -> 298 us
  other arithmetic: 49 us -> 28.8 us
  between operations: 21.4 us -> 3.85 us
    unnamed x748 -> x214, local copies, waits for them, and re-layouts: 178 us -> 23.9 us
    psum x2 -> x0, waiting for transfers between devices: 108 us -> none  [the longest x1 78.6 us: per_device(): flat = lax.psum(jnp.concatenate([v.reshape(-1) for v in small]), both_axes)]
    slice x39 -> x20, local copies, waits for them, and re-layouts: 45.5 us -> 8.03 us  [the longest x8 4.9 us: per_device(): homes[ROLL - 1 - j][states:states + forces]]
    concatenate x10 -> x1, local copies, waits for them, and re-layouts: 35.6 us -> 0.65 us  [per_device(): table = jnp.concatenate([table, extra], axis=0)]
    dot_general x6 -> x1, matrix products: 31.2 us -> 1.2 us  [per_device(): lax.dot_general(w_out_block, hidden_share[:states], (((0,), (0,)), ((), (...]
    pallas_call x33 -> x38, Pallas kernels: 323 us -> 298 us  [call(): pl.pallas_call(body, in_specs=specs, out_specs=[HBM_SPEC if i in hbm_outs...]
    ppermute x31 -> x24, starting transfers between devices: 47.9 us -> 26.4 us  [the longest x23 23.3 us: trade(): lax.ppermute(values, axis, [(i, i ^ flip) for i in range(lax.axis_size(ax...]
    ppermute x31 -> x24, waiting for transfers between devices: 19.5 us -> 38.9 us  [the longest x23 38.9 us: trade(): lax.ppermute(values, axis, [(i, i ^ flip) for i in range(lax.axis_size(ax...]
  transfers between devices with their start and end apart: 71 -> 63, of which waited for: 19 -> 26; matrix products, arithmetic and copies ran while one was open for 27% -> 9% of each run, Pallas kernels for 34% -> 36%
where the time goes in v2:
time: 501 us; the launch traced here: 493 us
  Pallas kernels  298 us (59%)
  waiting for transfers between devices  57.1 us (11%)
  starting transfers between devices  56.1 us (11%)
  local copies, waits for them, and re-layouts  47.1 us (9%)
  other arithmetic  28.8 us (6%)
    pallas_call x38, Pallas kernels, call(): pl.pallas_call(body, in_specs=specs, out_specs=[HBM_SPEC if i in hbm_outs...  298 us
    ppermute x23, waiting for transfers between devices, trade(): lax.ppermute(values, axis, [(i, i ^ flip) for i in range(lax.axis_size(ax...  38.9 us
    unnamed x214, local copies, waits for them, and re-layouts  23.9 us
    ppermute x23, starting transfers between devices, trade(): lax.ppermute(values, axis, [(i, i ^ flip) for i in range(lax.axis_size(ax...  23.3 us
    ppermute x33, waiting for transfers between devices, to_sibling(): return lax.ppermute(values, 'step', siblings)  15.7 us
    ppermute x33, starting transfers between devices, to_sibling(): return lax.ppermute(values, 'step', siblings)  10.8 us
  transfers between devices with their start and end apart: 63, of which 26 were waited for; matrix products, arithmetic and copies ran while one was open for 9% of the time, Pallas kernels for 36%

profile of v2, /device:TPU:9, one launch (start us, length us, event | category | flops | bytes accessed | tf_op | source)
XLA Modules:
  0.0 493.5 jit_solution(16612684207491733130)
XLA Ops:
  20.0 6.8 %down.1 = (bf16[3328,256]{1,0:T(8,128)(2,1)S(1)}, bf16[256,3328]{1,0:T(8,128)(2,1)S(1)}) custom-call(f32[800,3200]{1,0:T(8,128)} %refs_6_.1, bf16[160,800]{1,0:T(8,128)(2,1)S(1)} %pad_maximum_fusion.13.refs_1_), custom_call_target="tpu_custom_call" | custom-call | flops 7699999744 | bytes 1024 | tf_op jit(solution)/shard_map/down/pallas_call | solution.py:425
  36.5 6.5 %up.1.refs_10_.refs_8_.refs_22_ = bf16[1664,3328]{1,0:T(8,128)(2,1)S(1)} custom-call(f32[800,3200]{1,0:T(8,128)} %bitcast.210), custom_call_target="tpu_custom_call" | custom-call | flops 7699999744 | bytes 1024 | tf_op jit(solution)/shard_map/up/pallas_call | solution.py:425
  51.1 8.6 %feed.8 = (f32[192,128]{1,0:T(8,128)S(1)}, f32[96,128]{1,0:T(8,128)S(1)}, f32[80,96]{1,0:T(8,128)S(1)}, f32[96,896]{1,0:T(8,128)S(1)}, f32[8,896]{1,0:T(8,128)S(...) custom-call(s32[2]{0:T(128)S(1)} %pad_add_fusion.refs_0_.refs_5_.refs_6_, ...), custom_call_target="tpu_custom_call" | custom-call | flops 9349999616 | bytes 1024 | tf_op jit(solution)/shard_map/feed/pallas_call | solution.py:425
  67.0 9.4 %feed.9 = (f32[192,128]{1,0:T(8,128)S(1)}, f32[96,128]{1,0:T(8,128)S(1)}, f32[80,96]{1,0:T(8,128)S(1)}, f32[96,896]{1,0:T(8,128)}, f32[8,896]{1,0:T(8,128)S(1)},...) custom-call(s32[2]{0:T(128)S(1)} %pad_add_fusion.refs_0_.refs_5_.ref, ...), custom_call_target="tpu_custom_call", output_to_operand_aliasing={{7}: (13, {})} | custom-call | flops 9349999616 | bytes 1024 | tf_op jit(solution)/shard_map/feed/pallas_call | solution.py:425
  83.5 8.6 %feed.10 = (f32[192,128]{1,0:T(8,128)S(1)}, f32[96,128]{1,0:T(8,128)S(1)}, f32[80,96]{1,0:T(8,128)S(1)}, f32[96,896]{1,0:T(8,128)S(1)}, f32[8,896]{1,0:T(8,128)S...) custom-call(s32[2]{0:T(128)S(1)} %pad_add_fusion.refs_0_.refs_5_.ref, ...), custom_call_target="tpu_custom_call", output_to_operand_aliasing={{7}: (13, {})} | custom-call | flops 9349999616 | bytes 1024 | tf_op jit(solution)/shard_map/feed/pallas_call | solution.py:425
  99.3 9.0 %feed.11 = (f32[192,128]{1,0:T(8,128)S(1)}, f32[96,128]{1,0:T(8,128)S(1)}, f32[80,96]{1,0:T(8,128)S(1)}, f32[96,896]{1,0:T(8,128)S(1)}, f32[8,896]{1,0:T(8,128)S...) custom-call(s32[2]{0:T(128)S(1)} %pad_add_fusion.refs_0_.refs_5_.ref, ...), custom_call_target="tpu_custom_call", output_to_operand_aliasing={{7}: (13, {})} | custom-call | flops 9349999616 | bytes 1024 | tf_op jit(solution)/shard_map/feed/pallas_call | solution.py:425
  115.4 8.6 %feed.12 = (f32[192,128]{1,0:T(8,128)S(1)}, f32[96,128]{1,0:T(8,128)S(1)}, f32[80,96]{1,0:T(8,128)S(1)}, f32[96,896]{1,0:T(8,128)S(1)}, f32[8,896]{1,0:T(8,128)S...) custom-call(s32[2]{0:T(128)S(1)} %pad_add_fusion.refs_0_.refs_5_.ref, ...), custom_call_target="tpu_custom_call", output_to_operand_aliasing={{7}: (13, {})} | custom-call | flops 9349999616 | bytes 1024 | tf_op jit(solution)/shard_map/feed/pallas_call | solution.py:425
  131.2 8.6 %feed.13 = (f32[192,128]{1,0:T(8,128)S(1)}, f32[96,128]{1,0:T(8,128)S(1)}, f32[80,96]{1,0:T(8,128)S(1)}, f32[96,896]{1,0:T(8,128)S(1)}, f32[8,896]{1,0:T(8,128)S...) custom-call(s32[2]{0:T(128)S(1)} %pad_add_fusion.refs_0_.refs_5_.ref, ...), custom_call_target="tpu_custom_call", output_to_operand_aliasing={{7}: (13, {})} | custom-call | flops 9349999616 | bytes 1024 | tf_op jit(solution)/shard_map/feed/pallas_call | solution.py:425
  147.0 8.6 %feed.14 = (f32[192,128]{1,0:T(8,128)S(1)}, f32[96,128]{1,0:T(8,128)S(1)}, f32[80,96]{1,0:T(8,128)S(1)}, f32[96,896]{1,0:T(8,128)S(1)}, f32[8,896]{1,0:T(8,128)S...) custom-call(s32[2]{0:T(128)S(1)} %pad_add_fusion.refs_0_.refs_5_.ref, ...), custom_call_target="tpu_custom_call", output_to_operand_aliasing={{7}: (13, {})} | custom-call | flops 9349999616 | bytes 1024 | tf_op jit(solution)/shard_map/feed/pallas_call | solution.py:425
  162.7 9.4 %feed.15 = (f32[192,128]{1,0:T(8,128)}, f32[96,128]{1,0:T(8,128)}, f32[80,96]{1,0:T(8,128)S(1)}, f32[96,896]{1,0:T(8,128)S(1)}, f32[8,896]{1,0:T(8,128)S(1)}, /*...) custom-call(s32[2]{0:T(128)S(1)} %pad_add_fusion.refs_0_.refs_5_.refs_, ...), custom_call_target="tpu_custom_call", output_to_operand_aliasing={{7}: (13, {})} | custom-call | flops 9349999616 | bytes 1024 | tf_op jit(solution)/shard_map/feed/pallas_call | solution.py:425
  173.9 9.2 %back.9 = (f32[192,896]{1,0:T(8,128)S(1)}, bf16[384,3328]{1,0:T(8,128)(2,1)S(1)}, f32[192,896]{1,0:T(8,128)S(1)}, f32[104,896]{1,0:T(8,128)S(1)}, f32[768,128]{1,0:T(8,128)}) custom-call(s32[2]{0:T(128)S(1)} %pad_add_fusion.refs_0_.refs_5_.refs_6_, f32[192,128]{1,0:T(8,128)S(1)} %get-tuple-element.312.refs_14_.refs_8_.refs_1_, ...), custom_call_target="tpu_custom_call" | custom-call | flops 8249999872 | bytes 1024 | tf_op jit(solution)/shard_map/back/pallas_call | solution.py:425
  190.3 13.9 %back.10 = (f32[192,128]{1,0:T(8,128)}, f32[192,128]{1,0:T(8,128)S(1)}, f32[56,896]{1,0:T(8,128)S(1)}, f32[256,96]{1,0:T(8,128)S(1)}, f32[768,896]{1,0:T(8,128)}...) custom-call(s32[2]{0:T(128)S(1)} %copy-done.31, ...), custom_call_target="tpu_custom_call", output_to_operand_aliasing={{9}: (23, {})} | custom-call | flops 15950000128 | bytes 1024 | tf_op jit(solution)/shard_map/back/pallas_call | solution.py:425
  204.4 5.7 %weight.9 = (f32[408,1664]{1,0:T(8,128)S(1)}, f32[408,1664]{1,0:T(8,128)S(1)}, f32[64,896]{1,0:T(8,128)S(1)}) custom-call(s32[2]{0:T(128)S(1)} %copy-done.31, f32[192,896]{1,0:T(8,128)S(1)} %copy-done.51, f32[1,896]{1,0:T(1,128)S(1)} %broadcast_in_dim.56.refs_6_.refs_2_.refs_9_, ...), custom_call_target="tpu_custom_call", output_to_operand_aliasing={{0}: (7, {}), {1}: (8, {}), {2}: (9, {})} | custom-call | flops 5500000256 | bytes 1024 | tf_op jit(solution)/shard_map/weight/pallas_call | solution.py:425
  210.6 13.9 %back.11 = (f32[192,128]{1,0:T(8,128)}, f32[192,128]{1,0:T(8,128)S(1)}, f32[56,896]{1,0:T(8,128)S(1)}, f32[256,96]{1,0:T(8,128)S(1)}, f32[768,896]{1,0:T(8,128)}...) custom-call(s32[2]{0:T(128)S(1)} %copy-done.31, ...), custom_call_target="tpu_custom_call", output_to_operand_aliasing={{4}: (23, {}), {9}: (24, {})} | custom-call | flops 15950000128 | bytes 1024 | tf_op jit(solution)/shard_map/back/pallas_call | solution.py:425
  230.7 14.3 %back.12 = (f32[192,128]{1,0:T(8,128)}, f32[192,128]{1,0:T(8,128)S(1)}, f32[56,896]{1,0:T(8,128)S(1)}, f32[256,96]{1,0:T(8,128)S(1)}, f32[768,896]{1,0:T(8,128)}...) custom-call(s32[2]{0:T(128)S(1)} %copy-done.31, ...), custom_call_target="tpu_custom_call", output_to_operand_aliasing={{4}: (23, {}), {9}: (24, {})} | custom-call | flops 15950000128 | bytes 1024 | tf_op jit(solution)/shard_map/back/pallas_call | solution.py:425
  250.7 13.9 %back.13 = (f32[192,128]{1,0:T(8,128)}, f32[192,128]{1,0:T(8,128)S(1)}, f32[56,896]{1,0:T(8,128)S(1)}, f32[256,96]{1,0:T(8,128)S(1)}, f32[768,896]{1,0:T(8,128)}...) custom-call(s32[2]{0:T(128)S(1)} %copy-done.31, ...), custom_call_target="tpu_custom_call", output_to_operand_aliasing={{4}: (23, {}), {9}: (24, {})} | custom-call | flops 15950000128 | bytes 1024 | tf_op jit(solution)/shard_map/back/pallas_call | solution.py:425
  270.6 14.1 %back.14 = (f32[192,128]{1,0:T(8,128)}, f32[192,128]{1,0:T(8,128)S(1)}, f32[56,896]{1,0:T(8,128)S(1)}, f32[256,96]{1,0:T(8,128)S(1)}, f32[768,896]{1,0:T(8,128)}...) custom-call(s32[2]{0:T(128)S(1)} %copy-done.31, ...), custom_call_target="tpu_custom_call", output_to_operand_aliasing={{4}: (23, {}), {9}: (24, {})} | custom-call | flops 15950000128 | bytes 1024 | tf_op jit(solution)/shard_map/back/pallas_call | solution.py:425
  290.5 13.9 %back.15 = (f32[192,128]{1,0:T(8,128)}, f32[192,128]{1,0:T(8,128)S(1)}, f32[56,896]{1,0:T(8,128)S(1)}, f32[256,96]{1,0:T(8,128)S(1)}, f32[768,896]{1,0:T(8,128)}...) custom-call(s32[2]{0:T(128)S(1)} %copy-done.31, ...), custom_call_target="tpu_custom_call", output_to_operand_aliasing={{4}: (23, {}), {9}: (24, {})} | custom-call | flops 15950000128 | bytes 1024 | tf_op jit(solution)/shard_map/back/pallas_call | solution.py:425
  310.4 14.6 %back.16 = (f32[192,128]{1,0:T(8,128)}, f32[192,128]{1,0:T(8,128)S(1)}, f32[56,896]{1,0:T(8,128)S(1)}, f32[256,96]{1,0:T(8,128)S(1)}, f32[768,896]{1,0:T(8,128)}...) custom-call(s32[2]{0:T(128)S(1)} %copy-done.31, ...), custom_call_target="tpu_custom_call", output_to_operand_aliasing={{4}: (23, {}), {9}: (24, {})} | custom-call | flops 15950000128 | bytes 1024 | tf_op jit(solution)/shard_map/back/pallas_call | solution.py:425
  325.1 7.0 %weight.15 = (f32[408,1664]{1,0:T(8,128)S(1)}, f32[408,1664]{1,0:T(8,128)}, f32[64,896]{1,0:T(8,128)S(1)}) custom-call(s32[2]{0:T(128)S(1)} %copy-done.31, f32[192,896]{1,0:T(8,128)S(1)} %copy-done.57, f32[1,896]{1,0:T(1,128)S(1)} %broadcast_in_dim.56.refs_6_.refs_2_.refs_9_, ...), custom_call_target="tpu_custom_call", output_to_operand_aliasing={{0}: (7, {}), {2}: (9, {})} | custom-call | flops 5500000256 | bytes 1024 | tf_op jit(solution)/shard_map/weight/pallas_call | solution.py:425
  352.7 7.2 %back.17 = (f32[192,128]{1,0:T(8,128)}, f32[192,128]{1,0:T(8,128)}, f32[56,896]{1,0:T(8,128)S(1)}, f32[256,96]{1,0:T(8,128)S(1)}, f32[768,896]{1,0:T(8,128)}) custom-call(s32[2]{0:T(128)S(1)} %copy-done.32, f32[192,128]{1,0:T(8,128)S(1)} %copy-done.56, f32[192,128]{1,0:T(8,128)S(1)} %copy-done.67, ...), custom_call_target="tpu_custom_call", output_to_operand_aliasing={{4}: (17, {})} | custom-call | flops 7699999744 | bytes 1024 | tf_op jit(solution)/shard_map/back/pallas_call | solution.py:425
  362.0 15.7 %last.1 = (f32[312,896]{1,0:T(8,128)S(1)}, f32[80,1664]{1,0:T(8,128)S(1)}, f32[80,1664]{1,0:T(8,128)S(1)}) custom-call(s32[2]{0:T(128)S(1)} %copy-done.33, f32[768,128]{1,0:T(8,128)} %get-tuple-element.549.refs_1_, f32[768,256]{1,0:T(8,128)} %get-tuple-element.550.refs_2_, f32[768,896]{1,0:T(8,128)} %get-tuple-element.551.refs_3_, ...), custom_call_target="tpu_custom_call" | custom-call | flops 13200000000 | bytes 1024 | tf_op jit(solution)/shard_map/last/pallas_call | solution.py:425
  391.2 9.8 %collective-permute-done.39 = f32[2,200,400]{2,1,0:T(8,128)} collective-permute-done((f32[2,200,400]{2,1,0:T(8,128)}, f32[2,200,400]{2,1,0:T(8,128)}, u32[]{:S(2)}, u32[]{:S(2)}) %collective-permute-start.39) | collective-permute-done | bytes 640032 | tf_op jit(solution)/shard_map/ppermute | solution.py:870
  423.3 7.1 %collective-permute-done.59 = f32[80,400]{1,0:T(8,128)S(1)} collective-permute-done((f32[80,400]{1,0:T(8,128)S(1)}, f32[80,400]{1,0:T(8,128)S(1)}, u32[]{:S(2)}, u32[]{:S(2)}) %collective-permute-start.59) | collective-permute-done | bytes 128032 | tf_op jit(solution)/shard_map/ppermute | solution.py:870
  (483 shorter events, 245.2 us)
Async XLA Ops:
  6.2 23.4 %collective-permute-start = (f32[159,96]{1,0:T(8,128)}, f32[159,96]{1,0:T(8,128)S(1)}, u32[]{:S(2)}, u32[]{:S(2)}) collective-permute-start(f32[159,96]{1,0:T(8,128)} %pad_maximum_fusion.14), channel_id=1, source_target_pairs={{0,0},{4,1},{1,2},{5,3},{2,4},{6,5},{3,6},{7,7},{8,8},{12,9},{9,10... | collective-permute-start | bytes 183176 | tf_op jit(solution)/shard_map/ppermute | solution.py:693
  11.0 18.6 %collective-permute-start.1 = (f32[159,96]{1,0:T(8,128)}, f32[159,96]{1,0:T(8,128)S(1)}, u32[]{:S(2)}, u32[]{:S(2)}) collective-permute-start(f32[159,96]{1,0:T(8,128)} %pad_maximum_fusion.14), channel_id=1, source_target_pairs={{1,0},{5,1},{0,2},{4,3},{3,4},{7,5},{2,6},{6,7},{9,8},{13,9},{8,10... | collective-permute-start | bytes 183176 | tf_op jit(solution)/shard_map/ppermute | solution.py:693
  11.9 18.5 %all-to-all-start = ((f32[8,81,96]{2,1,0:T(8,128)}), f32[8,81,96]{2,1,0:T(8,128)}, u32[]{:S(2)}, u32[]{:S(2)}) async-start(f32[8,81,96]{2,1,0:T(8,128)} %constant_dynamic-slice_fusion), calls=%async_computation | async-start | bytes 720896 | tf_op jit(solution)/shard_map/all_to_all | solution.py:705
  31.6 18.5 %collective-permute-start.5 = (f32[8,81,96]{2,1,0:T(8,128)S(1)}, f32[8,81,96]{2,1,0:T(8,128)S(1)}, u32[]{:S(2)}, u32[]{:S(2)}) collective-permute-start(f32[8,81,96]{2,1,0:T(8,128)S(1)} %fusion.13), channel_id=1, source_target_pairs={{0,0},{4,1},{1,2},{5,3},{2,4},{6,5},{3,6},{7,7},{8,8},{12,9},{9,10... | collective-permute-start | bytes 746504 | tf_op jit(solution)/shard_map/ppermute | solution.py:693
  36.2 13.9 %collective-permute-start.6 = (f32[8,81,96]{2,1,0:T(8,128)S(1)}, f32[8,81,96]{2,1,0:T(8,128)S(1)}, u32[]{:S(2)}, u32[]{:S(2)}) collective-permute-start(f32[8,81,96]{2,1,0:T(8,128)S(1)} %fusion.13), channel_id=1, source_target_pairs={{1,0},{5,1},{0,2},{4,3},{3,4},{7,5},{2,6},{6,7},{9,8},{13,9},{8,10... | collective-permute-start | bytes 746504 | tf_op jit(solution)/shard_map/ppermute | solution.py:693
  161.9 148.5 %collective-permute-start.34 = (f32[96,896]{1,0:T(8,128)}, f32[96,896]{1,0:T(8,128)}, u32[]{:S(2)}, u32[]{:S(2)}) collective-permute-start(f32[96,896]{1,0:T(8,128)} %get-tuple-element.519), channel_id=1, source_target_pairs={{0,4},{4,0},{8,12},{12,8},{16,20},{20,16},{24,28},{28,24},{1,5},{5... | collective-permute-start | bytes 1032200 | tf_op jit(solution)/shard_map/ppermute | solution.py:687
  162.0 128.4 %collective-permute-start.32 = (f32[96,896]{1,0:T(8,128)S(1)}, f32[96,896]{1,0:T(8,128)S(1)}, u32[]{:S(2)}, u32[]{:S(2)}) collective-permute-start(f32[96,896]{1,0:T(8,128)S(1)} %get-tuple-element.499), channel_id=1, source_target_pairs={{0,4},{4,0},{8,12},{12,8},{16,20},{20,16},{24,28},{28,24},{1,5},{5... | collective-permute-start | bytes 1032200 | tf_op jit(solution)/shard_map/ppermute | solution.py:687
  162.4 108.2 %collective-permute-start.30 = (f32[96,896]{1,0:T(8,128)S(1)}, f32[96,896]{1,0:T(8,128)S(1)}, u32[]{:S(2)}, u32[]{:S(2)}) collective-permute-start(f32[96,896]{1,0:T(8,128)S(1)} %get-tuple-element.479), channel_id=1, source_target_pairs={{0,4},{4,0},{8,12},{12,8},{16,20},{20,16},{24,28},{28,24},{1,5},{5... | collective-permute-start | bytes 1032200 | tf_op jit(solution)/shard_map/ppermute | solution.py:687
  189.8 20.3 %collective-permute-start.24 = (f32[96,896]{1,0:T(8,128)S(1)}, f32[96,896]{1,0:T(8,128)S(1)}, u32[]{:S(2)}, u32[]{:S(2)}) collective-permute-start(f32[96,896]{1,0:T(8,128)S(1)} %get-tuple-element.419), channel_id=1, source_target_pairs={{0,4},{4,0},{8,12},{12,8},{16,20},{20,16},{24,28},{28,24},{1,5},{5... | collective-permute-start | bytes 1032200 | tf_op jit(solution)/shard_map/ppermute | solution.py:687
  210.1 20.1 %collective-permute-start.26 = (f32[96,896]{1,0:T(8,128)S(1)}, f32[96,896]{1,0:T(8,128)S(1)}, u32[]{:S(2)}, u32[]{:S(2)}) collective-permute-start(f32[96,896]{1,0:T(8,128)S(1)} %get-tuple-element.439), channel_id=1, source_target_pairs={{0,4},{4,0},{8,12},{12,8},{16,20},{20,16},{24,28},{28,24},{1,5},{5... | collective-permute-start | bytes 1032200 | tf_op jit(solution)/shard_map/ppermute | solution.py:687
  230.2 20.5 %collective-permute-start.28 = (f32[96,896]{1,0:T(8,128)S(1)}, f32[96,896]{1,0:T(8,128)S(1)}, u32[]{:S(2)}, u32[]{:S(2)}) collective-permute-start(f32[96,896]{1,0:T(8,128)S(1)} %get-tuple-element.459), channel_id=1, source_target_pairs={{0,4},{4,0},{8,12},{12,8},{16,20},{20,16},{24,28},{28,24},{1,5},{5... | collective-permute-start | bytes 1032200 | tf_op jit(solution)/shard_map/ppermute | solution.py:687
  332.8 27.1 %collective-permute-start.37 = (f32[408,1664]{1,0:T(8,128)}, f32[408,1664]{1,0:T(8,128)}, u32[]{:S(2)}, u32[]{:S(2)}) collective-permute-start(f32[408,1664]{1,0:T(8,128)} %get-tuple-element.547), channel_id=1, source_target_pairs={{0,4},{4,0},{8,12},{12,8},{16,20},{20,16},{24,28},{28,24},{1,5},{5... | collective-permute-start | bytes 8146952 | tf_op jit(solution)/shard_map/ppermute | solution.py:870
  381.2 19.8 %collective-permute-start.39 = (f32[2,200,400]{2,1,0:T(8,128)}, f32[2,200,400]{2,1,0:T(8,128)}, u32[]{:S(2)}, u32[]{:S(2)}) collective-permute-start(f32[2,200,400]{2,1,0:T(8,128)} %fusion.5), channel_id=1, source_target_pairs={{0,16},{4,20},{8,24},{12,28},{16,0},{20,4},{24,8},{28,12},{1,17},{... | collective-permute-start | bytes 1920008 | tf_op jit(solution)/shard_map/ppermute | solution.py:870
  385.1 19.3 %collective-permute-start.38 = (f32[2,200,400]{2,1,0:T(8,128)S(1)}, f32[2,200,400]{2,1,0:T(8,128)S(1)}, u32[]{:S(2)}, u32[]{:S(2)}) collective-permute-start(f32[2,200,400]{2,1,0:T(8,128)S(1)} %fusion.6), channel_id=1, source_target_pairs={{0,8},{4,12},{8,0},{12,4},{16,24},{20,28},{24,16},{28,20},{1,9},{5... | collective-permute-start | bytes 1920008 | tf_op jit(solution)/shard_map/ppermute | solution.py:870
  388.6 27.9 %collective-permute-start.56 = (f32[80,400]{1,0:T(8,128)}, f32[80,400]{1,0:T(8,128)}, u32[]{:S(2)}, u32[]{:S(2)}) collective-permute-start(f32[80,400]{1,0:T(8,128)} %get-tuple-element.658), channel_id=1, source_target_pairs={{0,8},{4,12},{8,0},{12,4},{16,24},{20,28},{24,16},{28,20},{1,9},{5... | collective-permute-start | bytes 384008 | tf_op jit(solution)/shard_map/ppermute | solution.py:870
  388.9 30.6 %collective-permute-start.57 = (f32[80,400]{1,0:T(8,128)}, f32[80,400]{1,0:T(8,128)}, u32[]{:S(2)}, u32[]{:S(2)}) collective-permute-start(f32[80,400]{1,0:T(8,128)} %get-tuple-element.657), channel_id=1, source_target_pairs={{0,16},{4,20},{8,24},{12,28},{16,0},{20,4},{24,8},{28,12},{1,17},{... | collective-permute-start | bytes 384008 | tf_op jit(solution)/shard_map/ppermute | solution.py:870
  389.2 30.4 %collective-permute-start.58 = (f32[80,400]{1,0:T(8,128)}, f32[80,400]{1,0:T(8,128)}, u32[]{:S(2)}, u32[]{:S(2)}) collective-permute-start(f32[80,400]{1,0:T(8,128)} %get-tuple-element.656), channel_id=1, source_target_pairs={{0,24},{4,28},{8,16},{12,20},{16,8},{20,12},{24,0},{28,4},{1,25},{... | collective-permute-start | bytes 384008 | tf_op jit(solution)/shard_map/ppermute | solution.py:870
  406.2 65.7 %collective-permute-start.53 = (f32[200,400]{1,0:T(8,128)}, f32[200,400]{1,0:T(8,128)}, u32[]{:S(2)}, u32[]{:S(2)}) collective-permute-start(f32[200,400]{1,0:T(8,128)} %select_bitcast_fusion), channel_id=1, source_target_pairs={{0,8},{4,12},{8,0},{12,4},{16,24},{20,28},{24,16},{28,20},{1,9},{5... | collective-permute-start | bytes 960008 | tf_op jit(solution)/shard_map/ppermute | solution.py:870
  408.5 23.5 %collective-permute-start.41 = (f32[160,896]{1,0:T(8,128)}, f32[160,896]{1,0:T(8,128)}, u32[]{:S(2)}, u32[]{:S(2)}) collective-permute-start(f32[160,896]{1,0:T(8,128)} %dynamic-slice_bitcast_fusion), channel_id=1, source_target_pairs={{0,4},{4,0},{8,12},{12,8},{16,20},{20,16},{24,28},{28,24},{1,5},{5... | collective-permute-start | bytes 1720328 | tf_op jit(solution)/shard_map/ppermute | solution.py:870
  416.5 23.8 %collective-permute-start.40 = (f32[802,96]{1,0:T(8,128)S(1)}, f32[802,96]{1,0:T(8,128)S(1)}, u32[]{:S(2)}, u32[]{:S(2)}) collective-permute-start(f32[802,96]{1,0:T(8,128)S(1)} %pad_maximum_fusion.11), channel_id=1, source_target_pairs={{0,0},{1,4},{2,1},{3,5},{4,2},{5,6},{6,3},{7,7},{8,8},{9,12},{10,9... | collective-permute-start | bytes 923912 | tf_op jit(solution)/shard_map/ppermute | solution.py:973
  433.8 17.7 %collective-permute-start.42 = (f32[40,896]{1,0:T(8,128)}, f32[40,896]{1,0:T(8,128)S(1)}, u32[]{:S(2)}, u32[]{:S(2)}) collective-permute-start(f32[40,896]{1,0:T(8,128)} %get-tuple-element.665), channel_id=1, source_target_pairs={{0,8},{4,12},{8,0},{12,4},{16,24},{20,28},{24,16},{28,20},{1,9},{5... | collective-permute-start | bytes 430088 | tf_op jit(solution)/shard_map/ppermute | solution.py:870
  434.1 17.4 %collective-permute-start.43 = (f32[40,896]{1,0:T(8,128)}, f32[40,896]{1,0:T(8,128)}, u32[]{:S(2)}, u32[]{:S(2)}) collective-permute-start(f32[40,896]{1,0:T(8,128)} %get-tuple-element.664), channel_id=1, source_target_pairs={{0,16},{4,20},{8,24},{12,28},{16,0},{20,4},{24,8},{28,12},{1,17},{... | collective-permute-start | bytes 430088 | tf_op jit(solution)/shard_map/ppermute | solution.py:870
  440.2 31.7 %collective-permute-start.52 = (f32[200,400]{1,0:T(8,128)}, f32[200,400]{1,0:T(8,128)}, u32[]{:S(2)}, u32[]{:S(2)}) collective-permute-start(f32[200,400]{1,0:T(8,128)} %select_bitcast_fusion.1), channel_id=1, source_target_pairs={{0,16},{4,20},{8,24},{12,28},{16,0},{20,4},{24,8},{28,12},{1,17},{... | collective-permute-start | bytes 960008 | tf_op jit(solution)/shard_map/ppermute | solution.py:870
  446.4 35.3 %all-to-all-start.1 = ((f32[8,81,96]{2,1,0:T(8,128)}), f32[8,81,96]{2,1,0:T(8,128)}, u32[]{:S(2)}, u32[]{:S(2)}) async-start(f32[8,81,96]{2,1,0:T(8,128)} %copy.133), calls=%async_computation.1 | async-start | bytes 720896 | tf_op jit(solution)/shard_map/all_to_all | solution.py:710
  (142 other events, 2190.7 us)

commit v3 on v2

--- a/solution.py
+++ b/solution.py
@@ -146,8 +146,8 @@
 
 def feed_kernel(
     at, mixed, stats, stats_other, sent, came, gain, bias, ocean, base, w_up, b_up, w_od,
-    new_out, new_edge_out, state_out, norm_edge_out, inv_out, norm_out, slope_out, act_all,
-    stack, rem, acc, acc_lo, hold_a, hold_b, hold_act, norm, slope, act_part, sems, *, turn, width, k_main, k_rem,
+    new_out, new_edge_out, norm_edge_out, inv_out, norm_out, slope_out, act_all, state_all,
+    stack, rem, acc, acc_lo, hold_a, hold_b, hold_act, norm, slope, act_part, state, sems, *, turn, width, k_main, k_rem,
 ):
     core, part = at[0], at[1]
     px = mixed.shape[0]
@@ -219,8 +219,11 @@
     new_out[...] = new
     new_edge_out[...] = new_out[pl.ds(pl.multiple_of((1 - core) * (px - edge_px), 8), edge_px), :]
     mine = jnp.where(part == 0, new[:part_px], new[part_px:])
-    state_out[...] = mine.T[: state_out.shape[0]]
+    state[...] = mine.T[: state.shape[0]]
+    keep_state = pltpu.make_async_copy(state, state_all.at[turn], sems.at[2 * chunks + 1])
+    keep_state.start()
     keep_norm.wait()
+    keep_state.wait()
     for t in range(chunks):
         keep_slope(t).wait()
         keep_act(t).wait()
@@ -351,9 +354,9 @@
 
 def weight_kernel(at, norm, gain, bias, hidden, send, *rest, quarter, finish):
     if finish:
-        taps, keep_in, give_in, sums_in, keep_out, give_out, sums_out = rest
+        taps, keep_in, give_in, sums_in, keep_out, give_out, sums_out, *up_row = rest
     else:
-        keep_out, give_out, sums_out = rest
+        keep_out, give_out, sums_out, *up_row = rest
     core = at[0]
     part = at[1]
     px = norm.shape[0]
@@ -391,6 +394,10 @@
         lax.fori_loop(0, half // CHUNK, step, 0)
         if half % CHUNK:
             chunk(side, half // CHUNK * CHUNK, half % CHUNK)
+    if up_row:
+        line = quarter // 8 * 8
+        for side, acc_out in ((core, keep_out), (1 - core, give_out)):
+            up_row[0][:, pl.ds(pl.multiple_of(side * half, LANES), half)] = acc_out[line : line + 8, :]
 
 
 VMEM_SPEC = pl.BlockSpec(memory_space=pltpu.VMEM)
@@ -569,8 +576,8 @@
 
 
 def last_kernel(
-    at, masked_hbm, x_hbm, lifts_hbm, lifted_hbm, act_hbm, down_hbm, b_down, sums, taps, table, hidden_keep, hidden_give,
-    masked, x_parts, lifts, lifted, act, down, masked_t, x_t, g_hidden, natural, g_parts, sems, *, spans, blocks,
+    at, masked_hbm, x_hbm, lifts_hbm, lifted_hbm, act_hbm, down_hbm, b_down, sums, taps, up_row, token, table_keep, table_give, hidden_keep, hidden_give,
+    table,    masked, x_parts, lifts, lifted, act, down, masked_t, x_t, g_hidden, natural, g_parts, sems, *, spans, blocks,
 ):
     chunks = act.shape[0]
     half = hidden_keep.shape[1]
@@ -641,6 +648,154 @@
         both = dot_t(g_parts[...], high)
         g_out = (both[:SEG] + both[SEG:]) + dot_t(g_parts[:SEG], low)
         table[224:304, start : start + size] += g_out
+    table[312:] = jnp.zeros((table.shape[0] - 312, width), F32)
+    for i, start in enumerate(range(0, up_row.shape[1], width)):
+        size = min(width, up_row.shape[1] - start)
+        table[312 + i : 313 + i, :size] = up_row[:1, start : start + size] * scale
+    table[316:317, :LANES] = jnp.sum(masked[...], axis=0, keepdims=True)
+    rows = table_keep.shape[0]
+    table_keep[...] = table[pl.ds(pl.multiple_of(at[0] * rows, 8), rows), :]
+    table_give[...] = table[pl.ds(pl.multiple_of((1 - at[0]) * rows, 8), rows), :]
+
+
+def flags(at):
+    return at[3], at[4], at[5], at[2]
+
+
+def cut_first_kernel(at, keep, got, keep_a, give_a, keep_b, give_b, *, rows, cols):
+    x, y, _, _ = flags(at)
+
+    def part(row, k):
+        here = (slice(row * rows, (row + 1) * rows), slice(k * cols, (k + 1) * cols))
+        return keep[here] + got[here]
+
+    for i, (even, odd) in enumerate(((0, 1), (2, 3))):
+        one, two = part(0, even), part(0, odd)
+        keep_a[i] = jnp.where(x == 0, one, two)
+        give_a[i] = jnp.where(x == 0, two, one)
+    for i, (low, top) in enumerate(((0, 2), (1, 3))):
+        one, two = part(1, low), part(1, top)
+        keep_b[i] = jnp.where(y == 0, one, two)
+        give_b[i] = jnp.where(y == 0, two, one)
+
+
+def cut_second_kernel(at, keep_a, got_a, keep_b, got_b, keep_a_out, give_a_out, keep_b_out, give_b_out):
+    x, y, _, _ = flags(at)
+    for bit, keep, got, keep_out, give_out in (
+        (y, keep_a, got_a, keep_a_out, give_a_out),
+        (x, keep_b, got_b, keep_b_out, give_b_out),
+    ):
+        keep_out[...] = keep[bit] + got[bit]
+        give_out[...] = keep[1 - bit] + got[1 - bit]
+
+
+def cut_third_kernel(at, keep_a, got_a, keep_b, got_b, keep_out, give_out):
+    _, _, _, side = flags(at)
+    one, two = keep_a[...] + got_a[...], keep_b[...] + got_b[...]
+    keep_out[...] = jnp.where(side == 0, one, two)
+    give_out[...] = jnp.where(side == 0, two, one)
+
+
+def turn_sum_kernel(at, keep, got, out_ref):
+    out_ref[...] = (keep[...] + got[...]).T
+
+
+def quarter_rows_kernel(at, keep, got, *outs):
+    rows = outs[0].shape[0]
+    pair = at[5]
+    for b, out_ref in enumerate(outs):
+        place = pl.multiple_of((pair ^ b) * rows, 8)
+        out_ref[...] = keep[pl.ds(place, rows), :] + got[pl.ds(place, rows), :]
+
+
+def quarter_cols_kernel(at, keep, got, *outs):
+    cols = outs[0].shape[1]
+    pair = at[5]
+    parts = [keep[:, k * cols : (k + 1) * cols] + got[:, k * cols : (k + 1) * cols] for k in range(4)]
+    for b, out_ref in enumerate(outs):
+        k = pair ^ b
+        low = jnp.where(k == 0, parts[0], parts[1])
+        top = jnp.where(k == 2, parts[2], parts[3])
+        out_ref[...] = jnp.where(k < 2, low, top)
+
+
+def sum_two_kernel(at, a, b, out_ref):
+    out_ref[...] = a[...] + b[...]
+
+
+def sum_four_kernel(at, a, b, c, d, out_ref):
+    out_ref[...] = (a[...] + b[...]) + (c[...] + d[...])
+
+
+def join_rows_kernel(at, a, b, c, d, out_ref):
+    rows = a.shape[0]
+    for flip, ref in enumerate((a, b, c, d)):
+        out_ref[pl.ds(pl.multiple_of((at[5] ^ flip) * rows, 8), rows), :] = ref[...]
+
+
+def share_down_kernel(at, a, b, w_hi, w_lo, out_ref):
+    high, low = split(a[...] + b[...])
+    out_ref[...] = dot(w_hi[...], high) + dot(w_hi[...], low) + dot(w_lo[...], high)
+
+
+def table_kernel(at, mine, other, g_in, g_dw, g_out, rows_out, *, states, forces):
+    core = at[0]
+    half = mine.shape[0]
+    channels = g_in.shape[1]
+
+    def get(start, size):
+        pieces = []
+        for base in (0, half):
+            low, top = max(start, base), min(start + size, base + half)
+            if low < top:
+                here = slice(low - base, top - base)
+                pieces.append(jnp.where(core == (base > 0), mine[here, :channels], other[here, :channels]))
+        return pieces[0] if len(pieces) == 1 else jnp.concatenate(pieces, axis=0)
+
+    g_in[:states] = get(0, 88)[:states]
+    g_in[states : 2 * states] = get(88, 80)[:states]
+    g_in[2 * states :] = get(0, 88)[states : states + forces]
+    taps = get(168, 56)
+    for p in range(KW):
+        g_dw[p] = taps[p * KW : (p + 1) * KW]
+    g_out[...] = get(224, 80)[:states]
+    for i, start in enumerate((304, 312)):
+        piece = jnp.where(core == (start >= half), mine[start % half : start % half + 8], other[start % half : start % half + 8])
+        rows_out[8 * i : 8 * i + 8] = piece
+
+
+def going_kernel(at, *refs, states, forces):
+    homes, out_ref = refs[:-1], refs[-1]
+    steps = len(homes)
+    block = out_ref.shape[1]
+    for j in range(steps):
+        out_ref[8 * j : 8 * j + 8] = jnp.concatenate([homes[j][states : states + forces], jnp.zeros((8 - forces, block), F32)], axis=0)
+    out_ref[8 * steps : 8 * steps + 80] = homes[0][:80]
+    out_ref[8 * steps + 80 :] = homes[0][LANES : LANES + 80]
+
+
+def roll_kernel(at, states, forces, out_ref):
+    steps = out_ref.shape[0]
+    high = states.shape[1]
+    for i in range(steps):
+        here = lax.rem(i - at[6] + steps, steps)
+        out_ref[i, :high] = states[here]
+        out_ref[i, high:] = forces[pl.ds(pl.multiple_of(here * 8, 8), 8), :]
+
+
+def home_kernel(at, gone, ending, predicted, grad_forcing, grad_init, *, states):
+    steps = gone.shape[0]
+    total = gone[0, SEG:]
+    for i in range(steps):
+        predicted[i] = gone[lax.rem(at[6] - i + steps, steps), :states]
+        if i:
+            total = total + gone[i, SEG:]
+    grad_forcing[...] = total
+    base = 8 * steps
+    prev, cur = ending[base : base + SEG][:states], ending[base + SEG : base + 2 * SEG][:states]
+    single = at[7] == 1
+    grad_init[0] = jnp.where(single, 0.0, prev)
+    grad_init[1] = jnp.where(single, cur + prev, cur)
 
 
 def pad_to(values, shape):
@@ -681,6 +836,7 @@
         [(place(2 * k + q, 2 * c + (b ^ h)), place(2 * k + c, 2 * h + q)) for k, c, h, q in cells] for b in range(2)
     ]
 
+    column_perm = [(place(2 * k + c, 2 * h + q), place(2 * k + q, 2 * c + h)) for k, c, h, q in cells]
     siblings = [(s, s ^ 1) for s in range(steps)]
 
     def to_sibling(values):
@@ -694,8 +850,9 @@
         return got
 
     def turn_round(values):
+        n = values.shape[0]
         doubled = jnp.flip(jnp.concatenate([values, values]), axis=0)
-        return lax.dynamic_slice_in_dim(doubled, steps - 1 - step, steps, axis=0)
+        return lax.dynamic_slice_in_dim(doubled, n - 1 - step % n, n, axis=0)
 
     def rotate(values, by):
         return lax.dynamic_slice_in_dim(jnp.concatenate([values, values]), by, steps, axis=0)
@@ -710,7 +867,7 @@
             return turn_round(lax.all_to_all(rotate(values, (steps - step) % steps), "step", 0, 0, tiled=True))
         return jnp.stack([lax.ppermute(values[j], "step", [(s, (s + j) % steps) for s in range(steps)]) for j in range(ROLL)])
 
-    at = jnp.stack([core, part]).astype(jnp.int32)
+    at = jnp.stack([core, part, side, pair % 2, (pair // 2) % 2, pair, step % ROLL, history[0, 0]]).astype(jnp.int32)
     mask_row = land_mask.astype(F32)[None]
     current = init_states[0, 0, 1]
     previous = jnp.where(history[0, 0] == 2, init_states[0, 0, 0], current)
@@ -750,15 +907,17 @@
     b_in_row = row(b_in, width)
     b_up_row = pad_to(b_up.reshape(steps // 2, 2, ff_block).swapaxes(0, 1).reshape(2, hidden // 2), (2, half)).reshape(1, wide)
     b_down_row = row(b_down, width)
+    w_block = lax.dynamic_slice_in_dim(w_out, depth * col_block, col_block, axis=1).T
+    w_block_hi, w_block_lo = split_outside(pad_to(w_block, (col_block, SEG)))
     prev, cur, ocean, first_sent = call(
         functools.partial(start_kernel, states=states, forces=forces), "start", (at, *payload),
         [out(px, LANES), out(px, LANES), out(px, LANES), out(block + 8, 3 * LANES)], [], 4, micros=1, smem=1,
     )
     first_came = to_sibling(first_sent)
     ready = lax.optimization_barrier(
-        (w_up.T, timed, w_in_hi, w_in_lo, w_oi_hi, w_oi_lo, b_new, taps, gain, bias, w_out_bwd, b_in_row, b_up_row, b_down_row, at, first_sent)
+        (w_up.T, timed, w_in_hi, w_in_lo, w_oi_hi, w_oi_lo, b_new, taps, gain, bias, w_out_bwd, b_in_row, b_up_row, b_down_row, w_block_hi, w_block_lo, at, first_sent)
     )
-    up_source, timed, w_in_hi, w_in_lo, w_oi_hi, w_oi_lo, b_new, taps, gain, bias, w_out_bwd, b_in_row, b_up_row, b_down_row, at, first_sent = ready
+    up_source, timed, w_in_hi, w_in_lo, w_oi_hi, w_oi_lo, b_new, taps, gain, bias, w_out_bwd, b_in_row, b_up_row, b_down_row, w_block_hi, w_block_lo, at, first_sent = ready
     timed = fetch_own(timed)
     (w_up_all,) = call(
         functools.partial(up_kernel, k_main=k_main, k_rem=k_rem, spans=spans), "up", (up_source,),
@@ -774,8 +933,8 @@
     force_edge = to_sibling(force_send)
 
     chunks = wide // CHUNK
-    x_all, lifted_all, act_all = None, None, None
-    kept, predicted = [], []
+    x_all, lifted_all, act_all, state_all = None, None, None, None
+    kept = []
     prev_edge, cur_edge, prev_lanes, cur_lanes = first_came, first_came, 0, LANES
     for j in range(ROLL):
         mixed, stats, base, window, x_all, lifted_all = call(
@@ -792,28 +951,28 @@
             12, micros=4.5, smem=1, hbm_outs=(3,), stacked=((4, x_all), (5, lifted_all)),
         )
         stats_other = to_sibling(stats)
-        new, new_edge, state, norm_edge, inv, norm, slope, act_all = call(
+        new, new_edge, norm_edge, inv, norm, slope, act_all, state_all = call(
             functools.partial(feed_kernel, turn=j, width=width, k_main=k_main, k_rem=k_rem), "feed",
             (at, mixed, stats, stats_other, first_sent, first_came, gain, bias, ocean, base, w_up_all, b_up_row, w_od_fwd),
             [
-                out(px, LANES), out(block, LANES), out(SEG, block), out(block, width), out(8, width), out(px, width),
-                out(chunks, px, CHUNK), out(chunks, ROLL * block, CHUNK),
+                out(px, LANES), out(block, LANES), out(block, width), out(8, width), out(px, width),
+                out(chunks, px, CHUNK), out(chunks, ROLL * block, CHUNK), out(ROLL, SEG, block),
             ],
             [
                 pltpu.VMEM((2 * px, k_main), BF16), pltpu.VMEM((px, LANES), BF16),
                 pltpu.VMEM((px, CHUNK), F32), pltpu.VMEM((px, LANES), F32), pltpu.VMEM((px, CHUNK), F32), pltpu.VMEM((px, CHUNK), F32),
                 pltpu.VMEM((px, CHUNK), F32), pltpu.VMEM((px, width), F32), pltpu.VMEM((chunks, px, CHUNK), F32),
-                pltpu.VMEM((chunks, block, CHUNK), F32), pltpu.SemaphoreType.DMA((2 * chunks + 1,)),
+                pltpu.VMEM((chunks, block, CHUNK), F32), pltpu.VMEM((SEG, block), F32), pltpu.SemaphoreType.DMA((2 * chunks + 2,)),
             ],
-            14, micros=8.5, smem=1, hbm_outs=(5, 6), stacked=((7, act_all),),
+            14, micros=8.5, smem=1, hbm_outs=(4, 5), stacked=((6, act_all), (7, state_all)),
         )
         prev, prev_edge, prev_lanes, cur = cur, cur_edge, cur_lanes, new
         if j < ROLL - 1:
             cur_edge, cur_lanes = to_sibling(new_edge), 0
         norm_edge = to_sibling(norm_edge)
-        predicted.append(state)
         kept.append((window, norm, norm_edge, slope, inv))
 
+    states_home = lax.ppermute(state_all, both_axes, column_perm)
     quarter = channels // 2
     acc_rows = round_up(quarter + 1, 8)
     tap_rows = round_up(KW * KW, 8)
@@ -831,6 +990,8 @@
         finish, begin = j < ROLL - 1, j >= 0
         if finish:
             pending, keep_acc, give_acc = lax.optimization_barrier((pending, keep_acc, give_acc))
+        if j == ROLL - 4:
+            pending, states_home = lax.optimization_barrier((pending, states_home))
         args, outs, scratch, stacked, hbm = [at, ocean, pending], [], [], [], ()
         if finish:
             window, norm, norm_edge, slope, inv = kept[j + 1]
@@ -859,12 +1020,17 @@
             grad_branch, hidden_now, grad_n, sent, masked_all = results
             came = to_sibling(sent)
             previous_step = (grad_n, sent, came, grad_branch)
-            keep_acc, give_acc, sums = call(
+            keep_acc, give_acc, sums, *up_row = call(
                 functools.partial(weight_kernel, quarter=quarter, finish=finish), "weight",
                 (at, kept[j][1], gain, bias, hidden_now, sent) + ((tap_sum, keep_acc, give_acc, sums) if finish else ()),
-                [out(acc_rows, half), out(acc_rows, half), out(tap_rows + 8, width)], [], 8, micros=5, smem=1,
+                [out(acc_rows, half), out(acc_rows, half), out(tap_rows + 8, width)] + ([] if j else [out(8, wide)]), [], 8, micros=5, smem=1,
                 aliases=({7: 0, 8: 1, 9: 2} if j else {7: 0, 9: 2}) if finish else None, vmem_outs=(0, 1, 2) if j else (),
             )
+            if j == 0:
+                window, norm, norm_edge, slope, inv = kept[0]
+                give_acc, came, norm_edge = lax.optimization_barrier((give_acc, came, norm_edge))
+                kept[0] = (window, norm, norm_edge, slope, inv)
+                previous_step = (grad_n, sent, came, grad_branch)
 
     def trade(values, axis, flip):
         return lax.ppermute(values, axis, [(i, i ^ flip) for i in range(lax.axis_size(axis))])
@@ -872,39 +1038,35 @@
     def pick(first, second, bit):
         return jnp.where(bit == 0, first, second), jnp.where(bit == 0, second, first)
 
-    def at_index(values, index):
-        return lax.dynamic_index_in_dim(values, index, keepdims=False)
-
-    def cut(values, k):
-        return values[..., k * ff_block : (k + 1) * ff_block]
-
-    def sum_z(values):
-        near = values + trade(values, "rows", 1)
-        return near + trade(near, "rows", 2)
+    token = [tap_sum]
+
+    def local(kernel, args, outs, limit=8, **options):
+        def body(at_ref, *refs):
+            kernel(at_ref, *refs[: len(args)], *refs[len(args) + 1 : -1], **options)
+            refs[-1][...] = refs[len(args)][:8, :LANES]
+
+        results = call(body, kernel.__name__, (at, *args, token[0]), outs + [out(8, LANES)], [], limit, micros=1, smem=1)
+        token[0] = results[-1]
+        return results[:-1]
 
     direct = steps == 8 and devices_z == 4
-    bit_x, bit_y = pair % 2, pair // 2
-    mine_up = keep_acc + trade(give_acc, "step", 1)
-    masked_all, mine_up, lift_all = lax.optimization_barrier((masked_all, mine_up, lift_all))
+    home_outs = [out(ROLL, states, block), out(8, block), out(2, states, block)]
+    got = trade(give_acc, "step", 1)
     if direct:
-        rows_a, rows_b = mine_up[:col_block], mine_up[col_block : 2 * col_block]
-        even = jnp.stack([cut(rows_a, 0), cut(rows_a, 2)])
-        odd = jnp.stack([cut(rows_a, 1), cut(rows_a, 3)])
-        keep_a, give_a = pick(even, odd, bit_x)
-        low = jnp.stack([cut(rows_b, 0), cut(rows_b, 1)])
-        top = jnp.stack([cut(rows_b, 2), cut(rows_b, 3)])
-        keep_b, give_b = pick(low, top, bit_y)
-        got_a = keep_a + trade(give_a, "step", 2)
-        got_b = keep_b + trade(give_b, "step", 4)
+        pieces = [out(2, col_block, ff_block)] * 4
+        keep_a, give_a, keep_b, give_b = local(cut_first_kernel, (keep_acc, got), pieces, 16, rows=col_block, cols=ff_block)
+        got_a, got_b = trade(give_a, "step", 2), trade(give_b, "step", 4)
     part_px = ROLL * block
     blocks = [(start, min(CHUNK, channels - start)) for start in range(0, channels, CHUNK)]
-    table, hidden_keep, hidden_give = call(
+    table_keep, table_give, hidden_keep, hidden_give = call(
         functools.partial(last_kernel, spans=spans, blocks=blocks), "last",
         (
-            at, masked_all, x_all, lift_all, lifted_all, act_all, w_down, b_down_row, sums, tap_sum,
+            at, masked_all, x_all, lift_all, lifted_all, act_all, w_down, b_down_row, sums,
+            tap_sum, *up_row, token[0],
         ),
-        [out(312, width), out(SEG, half), out(SEG, half)],
+        [out(160, width), out(160, width), out(SEG, half), out(SEG, half)],
         [
+            pltpu.VMEM((320, width), F32),
             pltpu.VMEM((part_px, LANES), F32), pltpu.VMEM((part_px, 2 * LANES), F32), pltpu.VMEM((part_px, width), F32),
             pltpu.VMEM(lifted_all.shape, F32), pltpu.VMEM((chunks, part_px, CHUNK), F32), pltpu.VMEM((channels, hidden), F32),
             pltpu.VMEM((2 * SEG, part_px), BF16), pltpu.VMEM((2, 2 * LANES, part_px), BF16), pltpu.VMEM((SEG, wide), F32),
@@ -913,81 +1075,71 @@
         ],
         44, micros=12, smem=1, hbm=(1, 2, 3, 4, 5, 6),
     )
+    other = trade(table_give, "step", 1)
+    hidden_other = trade(hidden_give, "step", 1)
     if direct:
-        table, got_a, got_b = lax.optimization_barrier((table, got_a, got_b))
-    first_table = table
-    up_row = jnp.stack(pick(keep_acc[quarter], give_acc[quarter], core)).reshape(wide) * (part == 0).astype(F32)
-    masked_sum = jnp.sum(masked_all, axis=0)
-    extra = jnp.concatenate([pad_to(up_row, (4 * width,)).reshape(4, width), row(masked_sum, width), jnp.zeros((3, width), F32)], axis=0)
-    table = jnp.concatenate([table, extra], axis=0)
-    mine_down = hidden_keep + trade(hidden_give, "step", 1)
-    if direct:
-        table = table.reshape(2, -1, width)
-        own = at_index(table, core) + trade(at_index(table, 1 - core), "step", 1)
-        own = own.reshape(4, -1, width)
-        rest = [trade(at_index(own, pair ^ b), "step", 2 * b) for b in (1, 2, 3)]
-        own = (at_index(own, pair) + rest[0]) + (rest[1] + rest[2])
-
-        keep_a, give_a = pick(got_a[0], got_a[1], bit_y)
-        keep_b, give_b = pick(got_b[0], got_b[1], bit_x)
-        got_a = keep_a + trade(give_a, "step", 4)
-        got_b = keep_b + trade(give_b, "step", 2)
-
-        rest = [trade(own, "rows", b) for b in (1, 2, 3)]
-        own = (own + rest[0]) + (rest[1] + rest[2])
-        keep, give = pick(got_a, got_b, side)
-        share_up = (keep + trade(give, "rows", 1)).T
-        rest = jnp.stack([own] + [trade(own, "step", 2 * b) for b in (1, 2, 3)])
-        own = jnp.concatenate([at_index(rest, pair ^ b) for b in range(4)], axis=0)
-        other = trade(own, "step", 1)
-        table = jnp.concatenate(pick(own, other, core), axis=0)
-
-        pieces = jnp.stack([cut(mine_down, k) for k in range(4)])
-        near = at_index(pieces, pair) + trade(at_index(pieces, pair ^ 1), "step", 2)
-        far = trade(at_index(pieces, pair ^ 2), "step", 4) + trade(at_index(pieces, pair ^ 3), "step", 6)
-        hidden_share = sum_z(near + far)
+        fours = (1, 2, 3)
+        token[0] = table_keep
+        keep_a, give_a, keep_b, give_b = local(cut_second_kernel, (keep_a, got_a, keep_b, got_b), [out(col_block, ff_block)] * 4)
+        got_a, got_b = trade(give_a, "step", 4), trade(give_b, "step", 2)
+        own = local(quarter_rows_kernel, (table_keep, other), [out(40, width)] * 4)
+        from_xy = [trade(own[b], "step", 2 * b) for b in fours]
+        h_own = local(quarter_cols_kernel, (hidden_keep, hidden_other), [out(SEG, ff_block)] * 4)
+        h_xy = [trade(h_own[b], "step", 2 * b) for b in fours]
+        (ending,) = local(going_kernel, homes[::-1], [out(8 * ROLL + 160, block)], states=states, forces=forces)
+        ending = lax.ppermute(ending, both_axes, column_perm)
+        (piece,) = local(sum_four_kernel, (own[0], *from_xy), [out(40, width)])
+        near = trade(piece, "rows", 1)
+        (h_piece,) = local(sum_four_kernel, (h_own[0], *h_xy), [out(SEG, ff_block)])
+        h_near = trade(h_piece, "rows", 1)
+        (piece,) = local(sum_two_kernel, (piece, near), [out(40, width)])
+        far = trade(piece, "rows", 2)
+        (h_piece,) = local(sum_two_kernel, (h_piece, h_near), [out(SEG, ff_block)])
+        h_far = trade(h_piece, "rows", 2)
+        keep, give = local(cut_third_kernel, (keep_a, got_a, keep_b, got_b), [out(col_block, ff_block)] * 2)
+        got = trade(give, "rows", 1)
+        (rolled,) = local(roll_kernel, (states_home, ending), [out(ROLL, 88, block)])
+        gone = lax.all_to_all(rolled, "step", 0, 0, tiled=True)
+        (piece,) = local(sum_two_kernel, (piece, far), [out(40, width)])
+        from_xy = [trade(piece, "step", 2 * b) for b in fours]
+        (share_down,) = local(share_down_kernel, (h_piece, h_far, w_block_hi, w_block_lo), [out(col_block, ff_block)])
+        (share_up,) = local(turn_sum_kernel, (keep, got), [out(ff_block, col_block)])
+        predicted, grad_forcing, grad_init = local(home_kernel, (gone, ending), home_outs, states=states)
+        (mine,) = local(join_rows_kernel, (piece, *from_xy), [out(160, width)])
+        other = trade(mine, "step", 1)
     else:
         units = steps // 2
         same_core = [[2 * k + c for k in range(units)] for c in range(2)]
+        mine_up = keep_acc + got
         share = lax.psum_scatter(mine_up[:, : hidden // 2], "step", scatter_dimension=1, axis_index_groups=same_core, tiled=True)
         keep, give = pick(share[:col_block], share[col_block : 2 * col_block], side)
         share_up = (keep + trade(give, "rows", 1)).T
+        mine_down = hidden_keep + hidden_other
         hidden_share = lax.psum(
             lax.psum_scatter(mine_down[:, : hidden // 2], "step", scatter_dimension=1, axis_index_groups=same_core, tiled=True), "rows"
         )
-        table = lax.psum(table, both_axes)
-
-    g_w_in = jnp.concatenate([table[:states], table[88 : 88 + states], table[states : states + forces]], axis=0)[:, :channels].T
-    g_w_dw = table[168 : 168 + KW * KW, :channels].T.reshape(channels, KW, KW)
-    g_w_out = table[224 : 224 + states, :channels]
-    g_bias, g_gain, g_b_in = table[304, :channels], table[305, :channels], table[311, :channels]
-    g_b_up = table[312:316].reshape(-1)[:wide].reshape(2, half)[:, : hidden // 2].reshape(2, steps // 2, ff_block).swapaxes(0, 1).reshape(-1)
-    g_b_out = table[316, :states]
+        nothing = jnp.zeros_like(hidden_share)
+        (share_down,) = local(share_down_kernel, (hidden_share, nothing, w_block_hi, w_block_lo), [out(col_block, ff_block)])
+        mine, other = pick(*[lax.psum(v, both_axes) for v in pick(table_keep, table_give, core)], core)
+        (ending,) = local(going_kernel, homes[::-1], [out(8 * ROLL + 160, block)], states=states, forces=forces)
+        ending = lax.ppermute(ending, both_axes, column_perm)
+        gone = turn_round(to_later(jnp.concatenate([states_home, ending[: 8 * ROLL].reshape(ROLL, 8, block)], axis=1)))
+        predicted, grad_forcing, grad_init = local(home_kernel, (gone, ending), home_outs, states=states)
+    g_in, g_dw, g_w_out, lines = local(
+        table_kernel, (mine, other),
+        [out(2 * states + forces, channels), out(KW, KW, channels), out(states, channels), out(16, width)], states=states, forces=forces,
+    )
+    g_bias, g_gain, g_b_in = lines[0, :channels], lines[1, :channels], lines[7, :channels]
+    g_b_up = lines[8:12].reshape(-1)[:wide].reshape(2, half)[:, : hidden // 2].reshape(2, steps // 2, ff_block).swapaxes(0, 1).reshape(-1)
+    g_b_out = lines[12, :states]
     g_b_down = jnp.sum(w_out * g_b_out[:, None], axis=0)
-
-    *late, _ = lax.optimization_barrier((*predicted, *homes, first_table))
-    predicted, homes = late[:ROLL], late[ROLL:]
-    going = jnp.stack([jnp.concatenate([predicted[j][:states], homes[ROLL - 1 - j][states : states + forces]], axis=0) for j in range(ROLL)])
-    ending = jnp.concatenate([homes[-1][:states], homes[-1][LANES : LANES + states]], axis=0)
-    flat = jnp.concatenate([going.reshape(-1, block), ending], axis=0)
-    flat = lax.ppermute(flat, both_axes, [(place(2 * k + c, 2 * h + q), place(2 * k + q, 2 * c + h)) for k, c, h, q in cells])
-    gone = to_later(flat[: going.shape[0] * going.shape[1]].reshape(going.shape))
-    grad_prev, grad_cur = flat[-2 * states : -states], flat[-states:]
-    grad_forcing = jnp.sum(gone[:, states:], axis=0)[None, None]
-    grad_init_prev = jnp.where(history[0, 0] == 2, grad_prev, 0.0)
-    grad_init_cur = grad_cur + jnp.where(history[0, 0] == 1, grad_prev, 0.0)
-    grad_init = jnp.stack([grad_init_prev, grad_init_cur])[None, None]
-    w_out_block = lax.dynamic_slice_in_dim(w_out, depth * col_block, col_block, axis=1)
-    share_down = lax.dot_general(
-        w_out_block, hidden_share[:states], (((0,), (0,)), ((), ())), precision=lax.Precision.HIGH, preferred_element_type=F32
-    )
     return (
-        gone[None, :, None, :states],
-        grad_init,
-        grad_forcing,
-        g_w_in,
+        predicted[None, :, None],
+        grad_init[None, None],
+        grad_forcing[None, None, :forces],
+        g_in.T,
         g_b_in,
-        g_w_dw,
+        g_dw.transpose(2, 0, 1),
         g_gain,
         g_bias,
         share_up,

time: 501 us -> 433 us (0.86)
  waiting for transfers between devices: 57.1 us -> 29.3 us
  local copies, waits for them, and re-layouts: 47.1 us -> 20.7 us
  other arithmetic: 28.8 us -> 2.71 us
  Pallas kernels: 298 us -> 314 us
    ppermute x23 -> x22, waiting for transfers between devices: 38.9 us -> 16.2 us  [trade(): lax.ppermute(values, axis, [(i, i ^ flip) for i in range(lax.axis_size(ax...]
    pallas_call x38 -> x55, Pallas kernels: 298 us -> 314 us  [call(): pl.pallas_call(body, in_specs=specs, out_specs=[HBM_SPEC if i in hbm_outs...]
    unnamed x214 -> x94, local copies, waits for them, and re-layouts: 23.9 us -> 14.4 us
    add x9 -> x0, other arithmetic: 8.29 us -> none  [the longest x1 2.08 us: per_device(): mine_up = keep_acc + trade(give_acc, 'step', 1)]
    select_n x7 -> x0, other arithmetic: 8.26 us -> none  [the longest x6 7.45 us: pick(): jnp.where(bit == 0, second, first)]
    slice x15 -> x2, local copies, waits for them, and re-layouts: 6.94 us -> 0.63 us  [the longest x1 0.63 us: per_device(): lines[0, :channels]]
    ppermute x23 -> x22, starting transfers between devices: 23.3 us -> 20.4 us  [trade(): lax.ppermute(values, axis, [(i, i ^ flip) for i in range(lax.axis_size(ax...]
  transfers between devices with their start and end apart: 63 -> 63, of which waited for: 26 -> 26; matrix products, arithmetic and copies ran while one was open for 9% -> 1% of each run, Pallas kernels for 36% -> 52%
where the time goes in v3:
time: 433 us; the launch traced here: 429 us
  Pallas kernels  314 us (73%)
  starting transfers between devices  58.2 us (13%)
  waiting for transfers between devices  29.3 us (7%)
  local copies, waits for them, and re-layouts  20.7 us (5%)
    pallas_call x55, Pallas kernels, call(): pl.pallas_call(body, in_specs=specs, out_specs=[HBM_SPEC if i in hbm_outs...  314 us
    ppermute x22, starting transfers between devices, trade(): lax.ppermute(values, axis, [(i, i ^ flip) for i in range(lax.axis_size(ax...  20.4 us
    ppermute x22, waiting for transfers between devices, trade(): lax.ppermute(values, axis, [(i, i ^ flip) for i in range(lax.axis_size(ax...  16.2 us
    unnamed x94, local copies, waits for them, and re-layouts  14.4 us
    ppermute x33, waiting for transfers between devices, to_sibling(): return lax.ppermute(values, 'step', siblings)  11.6 us
    ppermute x4, starting transfers between devices, fetch_own(): got = [lax.ppermute(values, both_axes, perm) for perm in fetch_perms]  10.9 us
    ppermute x33, starting transfers between devices, to_sibling(): return lax.ppermute(values, 'step', siblings)  10.5 us
  transfers between devices with their start and end apart: 63, of which 26 were waited for; matrix products, arithmetic and copies ran while one was open for 1% of the time, Pallas kernels for 52%

profile of v3, /device:TPU:9, one launch (start us, length us, event | category | flops | bytes accessed | tf_op | source)
XLA Modules:
  0.0 429.1 jit_solution(12099817742593562761)
XLA Ops:
  17.4 6.7 %down.1 = (bf16[3328,256]{1,0:T(8,128)(2,1)S(1)}, bf16[256,3328]{1,0:T(8,128)(2,1)S(1)}) custom-call(f32[800,3200]{1,0:T(8,128)} %refs_6_.1, bf16[160,800]{1,0:T(8,128)(2,1)S(1)} %pad_maximum_fusion.2.refs_1_), custom_call_target="tpu_custom_call" | custom-call | flops 7699999744 | bytes 1024 | tf_op jit(solution)/shard_map/down/pallas_call | solution.py:432
  33.8 6.5 %up.1.refs_10_.refs_8_.refs_22_ = bf16[1664,3328]{1,0:T(8,128)(2,1)S(1)} custom-call(f32[800,3200]{1,0:T(8,128)} %bitcast.80), custom_call_target="tpu_custom_call" | custom-call | flops 7699999744 | bytes 1024 | tf_op jit(solution)/shard_map/up/pallas_call | solution.py:432
  48.4 9.5 %feed.8 = (f32[192,128]{1,0:T(8,128)S(1)}, f32[96,128]{1,0:T(8,128)S(1)}, f32[96,896]{1,0:T(8,128)}, f32[8,896]{1,0:T(8,128)S(1)}, f32[192,896]{1,0:T(8,128)}, /...) custom-call(s32[8]{0:T(128)S(1)} %stack.31.refs_0_.refs_5_.refs_6_, ...), custom_call_target="tpu_custom_call" | custom-call | flops 9349999616 | bytes 1024 | tf_op jit(solution)/shard_map/feed/pallas_call | solution.py:432
  65.1 9.5 %feed.9 = (f32[192,128]{1,0:T(8,128)S(1)}, f32[96,128]{1,0:T(8,128)S(1)}, f32[96,896]{1,0:T(8,128)}, f32[8,896]{1,0:T(8,128)S(1)}, f32[192,896]{1,0:T(8,128)}, /...) custom-call(s32[8]{0:T(128)S(1)} %stack.31.refs_0_.refs_5_.refs_6_, ...), custom_call_target="tpu_custom_call", output_to_operand_aliasing={{6}: (13, {}), {7}: (14, {})} | custom-call | flops 9349999616 | bytes 1024 | tf_op jit(solution)/shard_map/feed/pallas_call | solution.py:432
  81.7 8.7 %feed.10 = (f32[192,128]{1,0:T(8,128)S(1)}, f32[96,128]{1,0:T(8,128)S(1)}, f32[96,896]{1,0:T(8,128)S(1)}, f32[8,896]{1,0:T(8,128)S(1)}, f32[192,896]{1,0:T(8,128...) custom-call(s32[8]{0:T(128)S(1)} %stack.31.refs_0_.refs_5_.refs_6_, ...), custom_call_target="tpu_custom_call", output_to_operand_aliasing={{6}: (13, {}), {7}: (14, {})} | custom-call | flops 9349999616 | bytes 1024 | tf_op jit(solution)/shard_map/feed/pallas_call | solution.py:432
  97.6 8.9 %feed.11 = (f32[192,128]{1,0:T(8,128)S(1)}, f32[96,128]{1,0:T(8,128)S(1)}, f32[96,896]{1,0:T(8,128)S(1)}, f32[8,896]{1,0:T(8,128)S(1)}, f32[192,896]{1,0:T(8,128...) custom-call(s32[8]{0:T(128)S(1)} %stack.31.refs_0_.refs_5_.refs_6_, ...), custom_call_target="tpu_custom_call", output_to_operand_aliasing={{6}: (13, {}), {7}: (14, {})} | custom-call | flops 9349999616 | bytes 1024 | tf_op jit(solution)/shard_map/feed/pallas_call | solution.py:432
  113.7 8.7 %feed.12 = (f32[192,128]{1,0:T(8,128)S(1)}, f32[96,128]{1,0:T(8,128)S(1)}, f32[96,896]{1,0:T(8,128)S(1)}, f32[8,896]{1,0:T(8,128)S(1)}, f32[192,896]{1,0:T(8,128...) custom-call(s32[8]{0:T(128)S(1)} %stack.31.refs_0_.refs_5_.refs_6_, ...), custom_call_target="tpu_custom_call", output_to_operand_aliasing={{6}: (13, {}), {7}: (14, {})} | custom-call | flops 9349999616 | bytes 1024 | tf_op jit(solution)/shard_map/feed/pallas_call | solution.py:432
  129.6 8.8 %feed.13 = (f32[192,128]{1,0:T(8,128)S(1)}, f32[96,128]{1,0:T(8,128)S(1)}, f32[96,896]{1,0:T(8,128)S(1)}, f32[8,896]{1,0:T(8,128)S(1)}, f32[192,896]{1,0:T(8,128...) custom-call(s32[8]{0:T(128)S(1)} %stack.31.refs_0_.refs_5_.refs_6_, ...), custom_call_target="tpu_custom_call", output_to_operand_aliasing={{6}: (13, {}), {7}: (14, {})} | custom-call | flops 9349999616 | bytes 1024 | tf_op jit(solution)/shard_map/feed/pallas_call | solution.py:432
  145.5 8.8 %feed.14 = (f32[192,128]{1,0:T(8,128)S(1)}, f32[96,128]{1,0:T(8,128)S(1)}, f32[96,896]{1,0:T(8,128)S(1)}, f32[8,896]{1,0:T(8,128)S(1)}, f32[192,896]{1,0:T(8,128...) custom-call(s32[8]{0:T(128)S(1)} %stack.31.refs_0_.refs_5_.refs_6_, ...), custom_call_target="tpu_custom_call", output_to_operand_aliasing={{6}: (13, {}), {7}: (14, {})} | custom-call | flops 9349999616 | bytes 1024 | tf_op jit(solution)/shard_map/feed/pallas_call | solution.py:432
  161.4 9.8 %feed.15 = (f32[192,128]{1,0:T(8,128)}, f32[96,128]{1,0:T(8,128)}, f32[96,896]{1,0:T(8,128)S(1)}, f32[8,896]{1,0:T(8,128)S(1)}, f32[192,896]{1,0:T(8,128)}, /*in...) custom-call(s32[8]{0:T(128)S(1)} %stack.31.refs_0_.refs_5_.refs_6_, ...), custom_call_target="tpu_custom_call", output_to_operand_aliasing={{6}: (13, {}), {7}: (14, {})} | custom-call | flops 9349999616 | bytes 1024 | tf_op jit(solution)/shard_map/feed/pallas_call | solution.py:432
  172.8 9.2 %back.9 = (f32[192,896]{1,0:T(8,128)S(1)}, bf16[384,3328]{1,0:T(8,128)(2,1)S(1)}, f32[192,896]{1,0:T(8,128)S(1)}, f32[104,896]{1,0:T(8,128)S(1)}, f32[768,128]{1,0:T(8,128)}) custom-call(s32[8]{0:T(128)S(1)} %stack.31.refs_0_.refs_5_.refs_6_, f32[192,128]{1,0:T(8,128)S(1)} %get-tuple-element.339.refs_14_.refs_8_.refs_1_, ...), custom_call_target="tpu_custom_call" | custom-call | flops 8249999872 | bytes 1024 | tf_op jit(solution)/shard_map/back/pallas_call | solution.py:432
  189.5 13.9 %back.10 = (f32[192,128]{1,0:T(8,128)}, f32[192,128]{1,0:T(8,128)S(1)}, f32[56,896]{1,0:T(8,128)S(1)}, f32[256,96]{1,0:T(8,128)S(1)}, f32[768,896]{1,0:T(8,128)}...) custom-call(s32[8]{0:T(128)S(1)} %stack.31.refs_0_.refs_5_.refs_6_, ...), custom_call_target="tpu_custom_call", output_to_operand_aliasing={{9}: (23, {})} | custom-call | flops 15950000128 | bytes 1024 | tf_op jit(solution)/shard_map/back/pallas_call | solution.py:432
  208.5 5.5 %weight.9 = (f32[408,1664]{1,0:T(8,128)S(1)}, f32[408,1664]{1,0:T(8,128)S(1)}, f32[64,896]{1,0:T(8,128)S(1)}) custom-call(s32[8]{0:T(128)S(1)} %stack.31.refs_0_.refs_5_.refs_6_, f32[192,896]{1,0:T(8,128)S(1)} %copy-done.27, f32[1,896]{1,0:T(1,128)S(1)} %broadcast_in_dim.45.refs_6_.refs_2_.refs_9_, ...), custom_call_target="tpu_custom_call", output_to_operand_aliasing={{0}: (7, {}), {1}: (8, {}), {2}: (9, {})} | custom-call | flops 5500000256 | bytes 1024 | tf_op jit(solution)/shard_map/weight/pallas_call | solution.py:432
  219.6 14.1 %back.11 = (f32[192,128]{1,0:T(8,128)}, f32[192,128]{1,0:T(8,128)S(1)}, f32[56,896]{1,0:T(8,128)S(1)}, f32[256,96]{1,0:T(8,128)S(1)}, f32[768,896]{1,0:T(8,128)}...) custom-call(s32[8]{0:T(128)S(1)} %stack.31.refs_0_.refs_5_.refs_6_, ...), custom_call_target="tpu_custom_call", output_to_operand_aliasing={{4}: (23, {}), {9}: (24, {})} | custom-call | flops 15950000128 | bytes 1024 | tf_op jit(solution)/shard_map/back/pallas_call | solution.py:432
  239.9 13.9 %back.12 = (f32[192,128]{1,0:T(8,128)}, f32[192,128]{1,0:T(8,128)S(1)}, f32[56,896]{1,0:T(8,128)S(1)}, f32[256,96]{1,0:T(8,128)S(1)}, f32[768,896]{1,0:T(8,128)}...) custom-call(s32[8]{0:T(128)S(1)} %stack.31.refs_0_.refs_5_.refs_6_, ...), custom_call_target="tpu_custom_call", output_to_operand_aliasing={{4}: (23, {}), {9}: (24, {})} | custom-call | flops 15950000128 | bytes 1024 | tf_op jit(solution)/shard_map/back/pallas_call | solution.py:432
  254.4 5.7 %weight.11 = (f32[408,1664]{1,0:T(8,128)S(1)}, f32[408,1664]{1,0:T(8,128)S(1)}, f32[64,896]{1,0:T(8,128)S(1)}) custom-call(s32[8]{0:T(128)S(1)} %stack.31.refs_0_.refs_5_.refs_6_, f32[192,896]{1,0:T(8,128)S(1)} %copy-done.25, f32[1,896]{1,0:T(1,128)S(1)} %broadcast_in_dim.45.refs_6_.refs_2_.refs_9_, ...), custom_call_target="tpu_custom_call", output_to_operand_aliasing={{0}: (7, {}), {1}: (8, {}), {2}: (9, {})} | custom-call | flops 5500000256 | bytes 1024 | tf_op jit(solution)/shard_map/weight/pallas_call | solution.py:432
  260.2 13.9 %back.13 = (f32[192,128]{1,0:T(8,128)}, f32[192,128]{1,0:T(8,128)S(1)}, f32[56,896]{1,0:T(8,128)S(1)}, f32[256,96]{1,0:T(8,128)S(1)}, f32[768,896]{1,0:T(8,128)}...) custom-call(s32[8]{0:T(128)S(1)} %stack.31.refs_0_.refs_5_.refs_6_, ...), custom_call_target="tpu_custom_call", output_to_operand_aliasing={{4}: (23, {}), {9}: (24, {})} | custom-call | flops 15950000128 | bytes 1024 | tf_op jit(solution)/shard_map/back/pallas_call | solution.py:432
  280.1 13.9 %back.14 = (f32[192,128]{1,0:T(8,128)}, f32[192,128]{1,0:T(8,128)S(1)}, f32[56,896]{1,0:T(8,128)S(1)}, f32[256,96]{1,0:T(8,128)S(1)}, f32[768,896]{1,0:T(8,128)}...) custom-call(s32[8]{0:T(128)S(1)} %stack.31.refs_0_.refs_5_.refs_6_, ...), custom_call_target="tpu_custom_call", output_to_operand_aliasing={{4}: (23, {}), {9}: (24, {})} | custom-call | flops 15950000128 | bytes 1024 | tf_op jit(solution)/shard_map/back/pallas_call | solution.py:432
  294.2 5.9 %weight.13 = (f32[408,1664]{1,0:T(8,128)S(1)}, f32[408,1664]{1,0:T(8,128)S(1)}, f32[64,896]{1,0:T(8,128)S(1)}) custom-call(s32[8]{0:T(128)S(1)} %stack.31.refs_0_.refs_5_.refs_6_, f32[192,896]{1,0:T(8,128)S(1)} %copy-done.23, f32[1,896]{1,0:T(1,128)S(1)} %broadcast_in_dim.45.refs_6_.refs_2_.refs_9_, ...), custom_call_target="tpu_custom_call", output_to_operand_aliasing={{0}: (7, {}), {1}: (8, {}), {2}: (9, {})} | custom-call | flops 5500000256 | bytes 1024 | tf_op jit(solution)/shard_map/weight/pallas_call | solution.py:432
  300.1 13.9 %back.15 = (f32[192,128]{1,0:T(8,128)}, f32[192,128]{1,0:T(8,128)S(1)}, f32[56,896]{1,0:T(8,128)S(1)}, f32[256,96]{1,0:T(8,128)S(1)}, f32[768,896]{1,0:T(8,128)}...) custom-call(s32[8]{0:T(128)S(1)} %stack.31.refs_0_.refs_5_.refs_6_, ...), custom_call_target="tpu_custom_call", output_to_operand_aliasing={{4}: (23, {}), {9}: (24, {})} | custom-call | flops 15950000128 | bytes 1024 | tf_op jit(solution)/shard_map/back/pallas_call | solution.py:432
  320.0 14.5 %back.16 = (f32[192,128]{1,0:T(8,128)}, f32[192,128]{1,0:T(8,128)S(1)}, f32[56,896]{1,0:T(8,128)S(1)}, f32[256,96]{1,0:T(8,128)S(1)}, f32[768,896]{1,0:T(8,128)}...) custom-call(s32[8]{0:T(128)S(1)} %stack.31.refs_0_.refs_5_.refs_6_, ...), custom_call_target="tpu_custom_call", output_to_operand_aliasing={{4}: (23, {}), {9}: (24, {})} | custom-call | flops 15950000128 | bytes 1024 | tf_op jit(solution)/shard_map/back/pallas_call | solution.py:432
  340.7 7.6 %back.17 = (f32[192,128]{1,0:T(8,128)}, f32[192,128]{1,0:T(8,128)}, f32[56,896]{1,0:T(8,128)S(1)}, f32[256,96]{1,0:T(8,128)S(1)}, f32[768,896]{1,0:T(8,128)}) custom-call(s32[8]{0:T(128)S(1)} %stack.31.refs_0_.refs_5_.refs_6_, f32[192,128]{1,0:T(8,128)S(1)} %get-tuple-element.339.refs_14_.refs_8_.refs_1_, ...), custom_call_target="tpu_custom_call", output_to_operand_aliasing={{4}: (17, {})} | custom-call | flops 7699999744 | bytes 1024 | tf_op jit(solution)/shard_map/back/pallas_call | solution.py:432
  353.1 15.7 %last.1 = (f32[160,896]{1,0:T(8,128)S(1)}, f32[160,896]{1,0:T(8,128)S(1)}, f32[80,1664]{1,0:T(8,128)S(1)}, f32[80,1664]{1,0:T(8,128)S(1)}) custom-call(s32[8]{0:T(128)S(1)} %stack.31.refs_0_.refs_5_.refs_6_, f32[768,128]{1,0:T(8,128)} %get-tuple-element.588.refs_1_, f32[768,256]{1,0:T(8,128)} %get-tuple-element.589.refs_2_, ...), custom_call_target="tpu_custom_call" | custom-call | flops 13200000000 | bytes 1024 | tf_op jit(solution)/shard_map/last/pallas_call | solution.py:432
  402.2 6.6 %all-to-all-start.1 = ((f32[8,88,96]{2,1,0:T(8,128)}), f32[8,88,96]{2,1,0:T(8,128)S(1)}, u32[]{:S(2)}, u32[]{:S(2)}) async-start(f32[8,88,96]{2,1,0:T(8,128)} %get-tuple-element.632), calls=%async_computation.1 | async-start | bytes 720896 | tf_op jit(solution)/shard_map/all_to_all | solution.py:1102
  (309 shorter events, 186.2 us)
Async XLA Ops:
  5.5 21.3 %collective-permute-start.1 = (f32[159,96]{1,0:T(8,128)S(1)}, f32[159,96]{1,0:T(8,128)S(1)}, u32[]{:S(2)}, u32[]{:S(2)}) collective-permute-start(f32[159,96]{1,0:T(8,128)S(1)} %pad_maximum_fusion.3), channel_id=1, source_target_pairs={{1,0},{5,1},{0,2},{4,3},{3,4},{7,5},{2,6},{6,7},{9,8},{13,9},{8,10... | collective-permute-start | bytes 183176 | tf_op jit(solution)/shard_map/ppermute | solution.py:849
  6.3 20.5 %collective-permute-start = (f32[159,96]{1,0:T(8,128)S(1)}, f32[159,96]{1,0:T(8,128)S(1)}, u32[]{:S(2)}, u32[]{:S(2)}) collective-permute-start(f32[159,96]{1,0:T(8,128)S(1)} %pad_maximum_fusion.3), channel_id=1, source_target_pairs={{0,0},{4,1},{1,2},{5,3},{2,4},{6,5},{3,6},{7,7},{8,8},{12,9},{9,10... | collective-permute-start | bytes 183176 | tf_op jit(solution)/shard_map/ppermute | solution.py:849
  11.3 16.3 %all-to-all-start = ((f32[8,81,96]{2,1,0:T(8,128)}), f32[8,81,96]{2,1,0:T(8,128)S(1)}, u32[]{:S(2)}, u32[]{:S(2)}) async-start(f32[8,81,96]{2,1,0:T(8,128)} %constant_dynamic-slice_fusion.1), calls=%async_computation | async-start | bytes 720896 | tf_op jit(solution)/shard_map/all_to_all | solution.py:862
  27.5 12.8 %collective-permute-start.2 = (f32[104,384]{1,0:T(8,128)S(1)}, f32[104,384]{1,0:T(8,128)S(1)}, u32[]{:S(2)}, u32[]{:S(2)}) collective-permute-start(f32[104,384]{1,0:T(8,128)S(1)} %get-tuple-element.353.refs_4_.refs_10_), channel_id=1, source_target_pairs={{0,4},{4,0},{8,12},{12,8},{16,20},{20,16},{24,28},{28,24},{1,5},{5... | collective-permute-start | bytes 479240 | tf_op jit(solution)/shard_map/ppermute | solution.py:843
  27.8 17.2 %collective-permute-start.6 = (f32[8,81,96]{2,1,0:T(8,128)S(1)}, f32[8,81,96]{2,1,0:T(8,128)S(1)}, u32[]{:S(2)}, u32[]{:S(2)}) collective-permute-start(f32[8,81,96]{2,1,0:T(8,128)S(1)} %fusion.7), channel_id=1, source_target_pairs={{1,0},{5,1},{0,2},{4,3},{3,4},{7,5},{2,6},{6,7},{9,8},{13,9},{8,10... | collective-permute-start | bytes 746504 | tf_op jit(solution)/shard_map/ppermute | solution.py:849
  28.4 18.2 %collective-permute-start.5 = (f32[8,81,96]{2,1,0:T(8,128)S(1)}, f32[8,81,96]{2,1,0:T(8,128)S(1)}, u32[]{:S(2)}, u32[]{:S(2)}) collective-permute-start(f32[8,81,96]{2,1,0:T(8,128)S(1)} %fusion.7), channel_id=1, source_target_pairs={{0,0},{4,1},{1,2},{5,3},{2,4},{6,5},{3,6},{7,7},{8,8},{12,9},{9,10... | collective-permute-start | bytes 746504 | tf_op jit(solution)/shard_map/ppermute | solution.py:849
  160.6 179.6 %collective-permute-start.37 = (f32[96,896]{1,0:T(8,128)}, f32[96,896]{1,0:T(8,128)}, u32[]{:S(2)}, u32[]{:S(2)}) collective-permute-start(f32[96,896]{1,0:T(8,128)} %get-tuple-element.570), channel_id=1, source_target_pairs={{0,4},{4,0},{8,12},{12,8},{16,20},{20,16},{24,28},{28,24},{1,5},{5... | collective-permute-start | bytes 1032200 | tf_op jit(solution)/shard_map/ppermute | solution.py:843
  160.7 159.3 %collective-permute-start.35 = (f32[96,896]{1,0:T(8,128)}, f32[96,896]{1,0:T(8,128)}, u32[]{:S(2)}, u32[]{:S(2)}) collective-permute-start(f32[96,896]{1,0:T(8,128)} %get-tuple-element.553), channel_id=1, source_target_pairs={{0,4},{4,0},{8,12},{12,8},{16,20},{20,16},{24,28},{28,24},{1,5},{5... | collective-permute-start | bytes 1032200 | tf_op jit(solution)/shard_map/ppermute | solution.py:843
  161.1 78.8 %collective-permute-start.27 = (f32[96,896]{1,0:T(8,128)S(1)}, f32[96,896]{1,0:T(8,128)S(1)}, u32[]{:S(2)}, u32[]{:S(2)}) collective-permute-start(f32[96,896]{1,0:T(8,128)S(1)} %get-tuple-element.477), channel_id=1, source_target_pairs={{0,4},{4,0},{8,12},{12,8},{16,20},{20,16},{24,28},{28,24},{1,5},{5... | collective-permute-start | bytes 1032200 | tf_op jit(solution)/shard_map/ppermute | solution.py:843
  171.2 17.9 %collective-permute-start.22 = (f32[96,896]{1,0:T(8,128)S(1)}, f32[96,896]{1,0:T(8,128)S(1)}, u32[]{:S(2)}, u32[]{:S(2)}) collective-permute-start(f32[96,896]{1,0:T(8,128)S(1)} %get-tuple-element.437), channel_id=1, source_target_pairs={{0,4},{4,0},{8,12},{12,8},{16,20},{20,16},{24,28},{28,24},{1,5},{5... | collective-permute-start | bytes 1032200 | tf_op jit(solution)/shard_map/ppermute | solution.py:843
  189.1 26.4 %collective-permute-start.24 = (f32[96,896]{1,0:T(8,128)S(1)}, f32[96,896]{1,0:T(8,128)S(1)}, u32[]{:S(2)}, u32[]{:S(2)}) collective-permute-start(f32[96,896]{1,0:T(8,128)S(1)} %get-tuple-element.455), channel_id=1, source_target_pairs={{0,4},{4,0},{8,12},{12,8},{16,20},{20,16},{24,28},{28,24},{1,5},{5... | collective-permute-start | bytes 1032200 | tf_op jit(solution)/shard_map/ppermute | solution.py:843
  204.8 14.8 %collective-permute-start.23 = (f32[104,896]{1,0:T(8,128)S(1)}, f32[104,896]{1,0:T(8,128)S(1)}, u32[]{:S(2)}, u32[]{:S(2)}) collective-permute-start(f32[104,896]{1,0:T(8,128)S(1)} %get-tuple-element.446.refs_5_.refs_4_), channel_id=1, source_target_pairs={{0,4},{4,0},{8,12},{12,8},{16,20},{20,16},{24,28},{28,24},{1,5},{5... | collective-permute-start | bytes 1118216 | tf_op jit(solution)/shard_map/ppermute | solution.py:843
  215.5 23.8 %collective-permute-start.25 = (f32[8,80,96]{2,1,0:T(8,128)S(1)}, f32[8,80,96]{2,1,0:T(8,128)S(1)}, u32[]{:S(2)}, u32[]{:S(2)}) collective-permute-start(f32[8,80,96]{2,1,0:T(8,128)S(1)} %copy-done.43), channel_id=1, source_target_pairs={{0,0},{1,4},{2,1},{3,5},{4,2},{5,6},{6,3},{7,7},{8,8},{9,12},{10,9... | collective-permute-start | bytes 737288 | tf_op jit(solution)/shard_map/ppermute | solution.py:975
  239.3 60.8 %collective-permute-start.33 = (f32[96,896]{1,0:T(8,128)S(1)}, f32[96,896]{1,0:T(8,128)S(1)}, u32[]{:S(2)}, u32[]{:S(2)}) collective-permute-start(f32[96,896]{1,0:T(8,128)S(1)} %get-tuple-element.534), channel_id=1, source_target_pairs={{0,4},{4,0},{8,12},{12,8},{16,20},{20,16},{24,28},{28,24},{1,5},{5... | collective-permute-start | bytes 1032200 | tf_op jit(solution)/shard_map/ppermute | solution.py:843
  239.8 20.2 %collective-permute-start.29 = (f32[96,896]{1,0:T(8,128)S(1)}, f32[96,896]{1,0:T(8,128)S(1)}, u32[]{:S(2)}, u32[]{:S(2)}) collective-permute-start(f32[96,896]{1,0:T(8,128)S(1)} %get-tuple-element.496), channel_id=1, source_target_pairs={{0,4},{4,0},{8,12},{12,8},{16,20},{20,16},{24,28},{28,24},{1,5},{5... | collective-permute-start | bytes 1032200 | tf_op jit(solution)/shard_map/ppermute | solution.py:843
  260.0 20.0 %collective-permute-start.31 = (f32[96,896]{1,0:T(8,128)S(1)}, f32[96,896]{1,0:T(8,128)S(1)}, u32[]{:S(2)}, u32[]{:S(2)}) collective-permute-start(f32[96,896]{1,0:T(8,128)S(1)} %get-tuple-element.515), channel_id=1, source_target_pairs={{0,4},{4,0},{8,12},{12,8},{16,20},{20,16},{24,28},{28,24},{1,5},{5... | collective-permute-start | bytes 1032200 | tf_op jit(solution)/shard_map/ppermute | solution.py:843
  350.4 19.9 %collective-permute-start.41 = (f32[2,200,400]{2,1,0:T(8,128)S(1)}, f32[2,200,400]{2,1,0:T(8,128)S(1)}, u32[]{:S(2)}, u32[]{:S(2)}) collective-permute-start(f32[2,200,400]{2,1,0:T(8,128)S(1)} %get-tuple-element.605), channel_id=1, source_target_pairs={{0,8},{4,12},{8,0},{12,4},{16,24},{20,28},{24,16},{28,20},{1,9},{5... | collective-permute-start | bytes 1920008 | tf_op jit(solution)/shard_map/ppermute | solution.py:1036
  351.9 19.5 %collective-permute-start.42 = (f32[2,200,400]{2,1,0:T(8,128)S(1)}, f32[2,200,400]{2,1,0:T(8,128)S(1)}, u32[]{:S(2)}, u32[]{:S(2)}) collective-permute-start(f32[2,200,400]{2,1,0:T(8,128)S(1)} %get-tuple-element.607), channel_id=1, source_target_pairs={{0,16},{4,20},{8,24},{12,28},{16,0},{20,4},{24,8},{28,12},{1,17},{... | collective-permute-start | bytes 1920008 | tf_op jit(solution)/shard_map/ppermute | solution.py:1036
  382.4 14.0 %collective-permute-start.44 = (f32[200,400]{1,0:T(8,128)S(1)}, f32[200,400]{1,0:T(8,128)S(1)}, u32[]{:S(2)}, u32[]{:S(2)}) collective-permute-start(f32[200,400]{1,0:T(8,128)S(1)} %get-tuple-element.613), channel_id=1, source_target_pairs={{0,16},{4,20},{8,24},{12,28},{16,0},{20,4},{24,8},{28,12},{1,17},{... | collective-permute-start | bytes 960008 | tf_op jit(solution)/shard_map/ppermute | solution.py:1036
  383.4 12.9 %collective-permute-start.45 = (f32[200,400]{1,0:T(8,128)S(1)}, f32[200,400]{1,0:T(8,128)S(1)}, u32[]{:S(2)}, u32[]{:S(2)}) collective-permute-start(f32[200,400]{1,0:T(8,128)S(1)} %get-tuple-element.615), channel_id=1, source_target_pairs={{0,8},{4,12},{8,0},{12,4},{16,24},{20,28},{24,16},{28,20},{1,9},{5... | collective-permute-start | bytes 960008 | tf_op jit(solution)/shard_map/ppermute | solution.py:1036
  392.2 16.5 %collective-permute-start.56 = (f32[40,896]{1,0:T(8,128)S(1)}, f32[40,896]{1,0:T(8,128)S(1)}, u32[]{:S(2)}, u32[]{:S(2)}) collective-permute-start(f32[40,896]{1,0:T(8,128)S(1)} %get-tuple-element.638.refs_1_), channel_id=1, source_target_pairs={{0,2},{1,3},{2,0},{3,1},{4,6},{5,7},{6,4},{7,5},{8,10},{9,11},{10,... | collective-permute-start | bytes 430088 | tf_op jit(solution)/shard_map/ppermute | solution.py:1036
  397.0 18.3 %collective-permute-start.54 = (f32[200,400]{1,0:T(8,128)S(1)}, f32[200,400]{1,0:T(8,128)S(1)}, u32[]{:S(2)}, u32[]{:S(2)}) collective-permute-start(f32[200,400]{1,0:T(8,128)S(1)} %get-tuple-element.634), channel_id=1, source_target_pairs={{0,1},{1,0},{2,3},{3,2},{4,5},{5,4},{6,7},{7,6},{8,9},{9,8},{10,11... | collective-permute-start | bytes 960008 | tf_op jit(solution)/shard_map/ppermute | solution.py:1036
  400.2 11.9 %collective-permute-start.55 = (f32[80,400]{1,0:T(8,128)S(1)}, f32[80,400]{1,0:T(8,128)S(1)}, u32[]{:S(2)}, u32[]{:S(2)}) collective-permute-start(f32[80,400]{1,0:T(8,128)S(1)} %get-tuple-element.635.refs_1_), channel_id=1, source_target_pairs={{0,2},{1,3},{2,0},{3,1},{4,6},{5,7},{6,4},{7,5},{8,10},{9,11},{10,... | collective-permute-start | bytes 384008 | tf_op jit(solution)/shard_map/ppermute | solution.py:1036
  402.2 14.7 %all-to-all-start.1 = ((f32[8,88,96]{2,1,0:T(8,128)}), f32[8,88,96]{2,1,0:T(8,128)S(1)}, u32[]{:S(2)}, u32[]{:S(2)}) async-start(f32[8,88,96]{2,1,0:T(8,128)} %get-tuple-element.632), calls=%async_computation.1 | async-start | bytes 720896 | tf_op jit(solution)/shard_map/all_to_all | solution.py:1102
  (83 other events, 603.8 us)

commit v4 on v3

--- a/solution.py
+++ b/solution.py
@@ -249,7 +249,7 @@
     if finish:
         (ext, shifted, mixed, grad_lift, lift_sem) = take(5)
     if begin:
-        (cot, slope, masked_part, begin_sems) = take(4)
+        (cot, slope, masked_part, pulled, begin_sems) = take(5)
     core, part = at[0], at[1]
     px = ocean.shape[0]
     rows = px // COLS
@@ -326,9 +326,18 @@
         chunks = w_od.shape[1] // CHUNK
         get_slope.wait()
 
+        half = w_od.shape[1] // 2
+
+        def pull(t, _):
+            cols = pl.ds(pl.multiple_of(t * half, half), half)
+            pulled[:, cols] = dot(left, w_od[:, cols])
+            return 0
+
+        lax.fori_loop(0, 2, pull, 0)
+
         def chunk(t, _):
             cols = pl.ds(pl.multiple_of(t * CHUNK, CHUNK), CHUNK)
-            high, low = split(dot(left, w_od[:, cols]) * slope[t])
+            high, low = split(pulled[:, cols] * slope[t])
             hidden_out[:px, cols] = high
             hidden_out[px:, cols] = low
             return 0
@@ -377,23 +386,11 @@
     high, low = split(mine.T[: keep_out.shape[0]])
     half = keep_out.shape[1]
 
-    def chunk(side, start, size):
-        acc_out = (keep_out, give_out)[side]
-        here = pl.ds(start, size)
+    for side, acc_out in enumerate((keep_out, give_out)):
         actual = core if side == 0 else 1 - core
-        cols = pl.ds(pl.multiple_of(actual * half + start, LANES), size)
+        cols = pl.ds(pl.multiple_of(actual * half, LANES), half)
         new = dot(high, hidden[:px, cols]) + dot(high, hidden[px:, cols]) + dot(low, hidden[:px, cols])
-        acc_out[:, here] = (keep_in, give_in)[side][:, here] + new if finish else new
-
-    for side in range(2):
-
-        def step(t, _):
-            chunk(side, pl.multiple_of(t * CHUNK, CHUNK), CHUNK)
-            return 0
-
-        lax.fori_loop(0, half // CHUNK, step, 0)
-        if half % CHUNK:
-            chunk(side, half // CHUNK * CHUNK, half % CHUNK)
+        acc_out[...] = (keep_in, give_in)[side][...] + new if finish else new
     if up_row:
         line = quarter // 8 * 8
         for side, acc_out in ((core, keep_out), (1 - core, give_out)):
@@ -964,7 +961,7 @@
                 pltpu.VMEM((px, CHUNK), F32), pltpu.VMEM((px, width), F32), pltpu.VMEM((chunks, px, CHUNK), F32),
                 pltpu.VMEM((chunks, block, CHUNK), F32), pltpu.VMEM((SEG, block), F32), pltpu.SemaphoreType.DMA((2 * chunks + 2,)),
             ],
-            14, micros=8.5, smem=1, hbm_outs=(4, 5), stacked=((6, act_all), (7, state_all)),
+            16, micros=8.5, smem=1, hbm_outs=(4, 5), stacked=((6, act_all), (7, state_all)),
         )
         prev, prev_edge, prev_lanes, cur = cur, cur_edge, cur_lanes, new
         if j < ROLL - 1:
@@ -980,7 +977,8 @@
     previous_step, keep_acc, give_acc, sums, lift_all, masked_all = None, None, None, None, None, None
     homes = []
     begin_scratch = [
-        pltpu.VMEM((px, LANES), F32), pltpu.VMEM((chunks, px, CHUNK), F32), pltpu.VMEM((block, LANES), F32), pltpu.SemaphoreType.DMA((3,)),
+        pltpu.VMEM((px, LANES), F32), pltpu.VMEM((chunks, px, CHUNK), F32), pltpu.VMEM((block, LANES), F32),
+        pltpu.VMEM((px, wide), F32), pltpu.SemaphoreType.DMA((3,)),
     ]
     finish_scratch = [
         pltpu.VMEM((rows + 2 * HALO, COLS + 16, width), F32), pltpu.VMEM((KW, rows + 2 * HALO, COLS, LANES), F32),
@@ -1010,7 +1008,7 @@
             back_kernel, finish=finish, begin=begin, turn=j, width=width, k_main=k_main, k_rem=k_rem, states=states
         )
         results = list(
-            call(kernel, "back", args, outs, scratch, 18, micros=7 * finish + 7.5 * begin, smem=1, hbm=hbm, stacked=stacked)
+            call(kernel, "back", args, outs, scratch, 20, micros=7 * finish + 7.5 * begin, smem=1, hbm=hbm, stacked=stacked)
         )
         if finish:
             carry, pending, tap_sum, home, lift_all = results[:5]

time: 433 us -> 424 us (0.979)
  Pallas kernels: 314 us -> 292 us
  local copies, waits for them, and re-layouts: 20.7 us -> 33.4 us
    pallas_call x55, Pallas kernels: 314 us -> 292 us  [call(): pl.pallas_call(body, in_specs=specs, out_specs=[HBM_SPEC if i in hbm_outs...]
    unnamed x94 -> x86, local copies, waits for them, and re-layouts: 14.4 us -> 27.2 us
  transfers between devices with their start and end apart: 63 -> 63, of which waited for: 26 -> 26; matrix products, arithmetic and copies ran while one was open for 1% -> 1% of each run, Pallas kernels for 52% -> 48%
where the time goes in v4:
time: 424 us; the launch traced here: 420 us
  Pallas kernels  292 us (69%)
  starting transfers between devices  57.8 us (14%)
  local copies, waits for them, and re-layouts  33.4 us (8%)
  waiting for transfers between devices  29.8 us (7%)
    pallas_call x55, Pallas kernels, call(): pl.pallas_call(body, in_specs=specs, out_specs=[HBM_SPEC if i in hbm_outs...  292 us
    unnamed x86, local copies, waits for them, and re-layouts  27.2 us
    ppermute x22, starting transfers between devices, trade(): lax.ppermute(values, axis, [(i, i ^ flip) for i in range(lax.axis_size(ax...  20.4 us
    ppermute x22, waiting for transfers between devices, trade(): lax.ppermute(values, axis, [(i, i ^ flip) for i in range(lax.axis_size(ax...  16.3 us
    ppermute x33, waiting for transfers between devices, to_sibling(): return lax.ppermute(values, 'step', siblings)  11.6 us
    ppermute x4, starting transfers between devices, fetch_own(): got = [lax.ppermute(values, both_axes, perm) for perm in fetch_perms]  10.5 us
    ppermute x33, starting transfers between devices, to_sibling(): return lax.ppermute(values, 'step', siblings)  10.5 us
  transfers between devices with their start and end apart: 63, of which 26 were waited for; matrix products, arithmetic and copies ran while one was open for 1% of the time, Pallas kernels for 48%

profile of v4, /device:TPU:9, one launch (start us, length us, event | category | flops | bytes accessed | tf_op | source)
XLA Modules:
  0.0 420.0 jit_solution(7046538413644053695)
XLA Ops:
  17.4 6.7 %down.1 = (bf16[3328,256]{1,0:T(8,128)(2,1)S(1)}, bf16[256,3328]{1,0:T(8,128)(2,1)S(1)}) custom-call(f32[800,3200]{1,0:T(8,128)} %refs_6_.1, bf16[160,800]{1,0:T(8,128)(2,1)S(1)} %pad_maximum_fusion.2.refs_1_), custom_call_target="tpu_custom_call" | custom-call | flops 7699999744 | bytes 1024 | tf_op jit(solution)/shard_map/down/pallas_call | solution.py:429
  28.4 5.1 %collective-permute-start.5 = (f32[8,81,96]{2,1,0:T(8,128)S(1)}, f32[8,81,96]{2,1,0:T(8,128)S(1)}, u32[]{:S(2)}, u32[]{:S(2)}) collective-permute-start(f32[8,81,96]{2,1,0:T(8,128)S(1)} %fusion.7), channel_id=1, source_target_pairs={{0,0},{4,1},{1,2},{5,3},{2,4},{6,5},{3,6},{7,7},{8,8},{12,9},{9,10... | collective-permute-start | bytes 746504 | tf_op jit(solution)/shard_map/ppermute | solution.py:846
  33.5 6.5 %up.1.refs_10_.refs_8_.refs_22_ = bf16[1664,3328]{1,0:T(8,128)(2,1)S(1)} custom-call(f32[800,3200]{1,0:T(8,128)} %bitcast.80), custom_call_target="tpu_custom_call" | custom-call | flops 7699999744 | bytes 1024 | tf_op jit(solution)/shard_map/up/pallas_call | solution.py:429
  40.0 4.6 %mix.8 = (f32[192,896]{1,0:T(8,128)S(1)}, f32[8,896]{1,0:T(8,128)S(1)}, f32[192,128]{1,0:T(8,128)S(1)}, f32[9,32,896]{2,1,0:T(8,128)}, f32[768,256]{1,0:T(8,128)}, /*index=5*/f32[24,32,896]{2,1,0:T(8,128)}) custom-call(s32[8]{0:T(128)S(1)} %stack.31.refs_0_.refs_5_.refs_6_, f32[192,128]{1,0:T(8,128)S(1)} %get-tuple-element.340.refs_1_.refs_3_, ...), custom_call_target="tpu_custom_call" | custom-call | flops 4950000128 | bytes 1024 | tf_op jit(solution)/shard_map/mix/pallas_call | solution.py:429
  48.4 9.5 %feed.8 = (f32[192,128]{1,0:T(8,128)S(1)}, f32[96,128]{1,0:T(8,128)S(1)}, f32[96,896]{1,0:T(8,128)}, f32[8,896]{1,0:T(8,128)S(1)}, f32[192,896]{1,0:T(8,128)}, /...) custom-call(s32[8]{0:T(128)S(1)} %stack.31.refs_0_.refs_5_.refs_6_, ...), custom_call_target="tpu_custom_call" | custom-call | flops 9349999616 | bytes 1024 | tf_op jit(solution)/shard_map/feed/pallas_call | solution.py:429
  65.1 9.5 %feed.9 = (f32[192,128]{1,0:T(8,128)S(1)}, f32[96,128]{1,0:T(8,128)S(1)}, f32[96,896]{1,0:T(8,128)}, f32[8,896]{1,0:T(8,128)S(1)}, f32[192,896]{1,0:T(8,128)}, /...) custom-call(s32[8]{0:T(128)S(1)} %stack.31.refs_0_.refs_5_.refs_6_, ...), custom_call_target="tpu_custom_call", output_to_operand_aliasing={{6}: (13, {}), {7}: (14, {})} | custom-call | flops 9349999616 | bytes 1024 | tf_op jit(solution)/shard_map/feed/pallas_call | solution.py:429
  75.9 4.6 %mix.10 = (f32[192,896]{1,0:T(8,128)S(1)}, f32[8,896]{1,0:T(8,128)S(1)}, f32[192,128]{1,0:T(8,128)S(1)}, f32[9,32,896]{2,1,0:T(8,128)}, f32[768,256]{1,0:T(8,128)}, /*index=5*/f32[24,32,896]{2,1,0:T(8,128)}) custom-call(s32[8]{0:T(128)S(1)} %stack.31.refs_0_.refs_5_.refs_6_, ...), custom_call_target="tpu_custom_call", output_to_operand_aliasing={{4}: (15, {}), {5}: (16, {})} | custom-call | flops 4950000128 | bytes 1024 | tf_op jit(solution)/shard_map/mix/pallas_call | solution.py:429
  81.7 8.8 %feed.10 = (f32[192,128]{1,0:T(8,128)S(1)}, f32[96,128]{1,0:T(8,128)S(1)}, f32[96,896]{1,0:T(8,128)S(1)}, f32[8,896]{1,0:T(8,128)S(1)}, f32[192,896]{1,0:T(8,128...) custom-call(s32[8]{0:T(128)S(1)} %stack.31.refs_0_.refs_5_.refs_6_, ...), custom_call_target="tpu_custom_call", output_to_operand_aliasing={{6}: (13, {}), {7}: (14, {})} | custom-call | flops 9349999616 | bytes 1024 | tf_op jit(solution)/shard_map/feed/pallas_call | solution.py:429
  97.6 9.2 %feed.11 = (f32[192,128]{1,0:T(8,128)S(1)}, f32[96,128]{1,0:T(8,128)S(1)}, f32[96,896]{1,0:T(8,128)S(1)}, f32[8,896]{1,0:T(8,128)S(1)}, f32[192,896]{1,0:T(8,128...) custom-call(s32[8]{0:T(128)S(1)} %stack.31.refs_0_.refs_5_.refs_6_, ...), custom_call_target="tpu_custom_call", output_to_operand_aliasing={{6}: (13, {}), {7}: (14, {})} | custom-call | flops 9349999616 | bytes 1024 | tf_op jit(solution)/shard_map/feed/pallas_call | solution.py:429
  113.9 8.7 %feed.12 = (f32[192,128]{1,0:T(8,128)S(1)}, f32[96,128]{1,0:T(8,128)S(1)}, f32[96,896]{1,0:T(8,128)S(1)}, f32[8,896]{1,0:T(8,128)S(1)}, f32[192,896]{1,0:T(8,128...) custom-call(s32[8]{0:T(128)S(1)} %stack.31.refs_0_.refs_5_.refs_6_, ...), custom_call_target="tpu_custom_call", output_to_operand_aliasing={{6}: (13, {}), {7}: (14, {})} | custom-call | flops 9349999616 | bytes 1024 | tf_op jit(solution)/shard_map/feed/pallas_call | solution.py:429
  129.8 8.8 %feed.13 = (f32[192,128]{1,0:T(8,128)S(1)}, f32[96,128]{1,0:T(8,128)S(1)}, f32[96,896]{1,0:T(8,128)S(1)}, f32[8,896]{1,0:T(8,128)S(1)}, f32[192,896]{1,0:T(8,128...) custom-call(s32[8]{0:T(128)S(1)} %stack.31.refs_0_.refs_5_.refs_6_, ...), custom_call_target="tpu_custom_call", output_to_operand_aliasing={{6}: (13, {}), {7}: (14, {})} | custom-call | flops 9349999616 | bytes 1024 | tf_op jit(solution)/shard_map/feed/pallas_call | solution.py:429
  149.9 8.7 %feed.14 = (f32[192,128]{1,0:T(8,128)S(1)}, f32[96,128]{1,0:T(8,128)S(1)}, f32[96,896]{1,0:T(8,128)S(1)}, f32[8,896]{1,0:T(8,128)S(1)}, f32[192,896]{1,0:T(8,128...) custom-call(s32[8]{0:T(128)S(1)} %stack.31.refs_0_.refs_5_.refs_6_, ...), custom_call_target="tpu_custom_call", output_to_operand_aliasing={{6}: (13, {}), {7}: (14, {})} | custom-call | flops 9349999616 | bytes 1024 | tf_op jit(solution)/shard_map/feed/pallas_call | solution.py:429
  169.9 9.6 %feed.15 = (f32[192,128]{1,0:T(8,128)}, f32[96,128]{1,0:T(8,128)}, f32[96,896]{1,0:T(8,128)S(1)}, f32[8,896]{1,0:T(8,128)S(1)}, f32[192,896]{1,0:T(8,128)}, /*in...) custom-call(s32[8]{0:T(128)S(1)} %stack.31.refs_0_.refs_5_.refs_6_, ...), custom_call_target="tpu_custom_call", output_to_operand_aliasing={{6}: (13, {}), {7}: (14, {})} | custom-call | flops 9349999616 | bytes 1024 | tf_op jit(solution)/shard_map/feed/pallas_call | solution.py:429
  185.2 7.9 %back.9 = (f32[192,896]{1,0:T(8,128)S(1)}, bf16[384,3328]{1,0:T(8,128)(2,1)S(1)}, f32[192,896]{1,0:T(8,128)S(1)}, f32[104,896]{1,0:T(8,128)S(1)}, f32[768,128]{1,0:T(8,128)}) custom-call(s32[8]{0:T(128)S(1)} %stack.31.refs_0_.refs_5_.refs_6_, f32[192,128]{1,0:T(8,128)S(1)} %get-tuple-element.339.refs_14_.refs_8_.refs_1_, ...), custom_call_target="tpu_custom_call" | custom-call | flops 8249999872 | bytes 1024 | tf_op jit(solution)/shard_map/back/pallas_call | solution.py:429
  201.2 12.6 %back.10 = (f32[192,128]{1,0:T(8,128)}, f32[192,128]{1,0:T(8,128)S(1)}, f32[56,896]{1,0:T(8,128)S(1)}, f32[256,96]{1,0:T(8,128)S(1)}, f32[768,896]{1,0:T(8,128)}...) custom-call(s32[8]{0:T(128)S(1)} %stack.31.refs_0_.refs_5_.refs_6_, ...), custom_call_target="tpu_custom_call", output_to_operand_aliasing={{9}: (23, {})} | custom-call | flops 15950000128 | bytes 1024 | tf_op jit(solution)/shard_map/back/pallas_call | solution.py:429
  222.2 12.9 %back.11 = (f32[192,128]{1,0:T(8,128)}, f32[192,128]{1,0:T(8,128)S(1)}, f32[56,896]{1,0:T(8,128)S(1)}, f32[256,96]{1,0:T(8,128)S(1)}, f32[768,896]{1,0:T(8,128)}...) custom-call(s32[8]{0:T(128)S(1)} %stack.31.refs_0_.refs_5_.refs_6_, ...), custom_call_target="tpu_custom_call", output_to_operand_aliasing={{4}: (23, {}), {9}: (24, {})} | custom-call | flops 15950000128 | bytes 1024 | tf_op jit(solution)/shard_map/back/pallas_call | solution.py:429
  244.0 13.0 %back.12 = (f32[192,128]{1,0:T(8,128)}, f32[192,128]{1,0:T(8,128)S(1)}, f32[56,896]{1,0:T(8,128)S(1)}, f32[256,96]{1,0:T(8,128)S(1)}, f32[768,896]{1,0:T(8,128)}...) custom-call(s32[8]{0:T(128)S(1)} %stack.31.refs_0_.refs_5_.refs_6_, ...), custom_call_target="tpu_custom_call", output_to_operand_aliasing={{4}: (23, {}), {9}: (24, {})} | custom-call | flops 15950000128 | bytes 1024 | tf_op jit(solution)/shard_map/back/pallas_call | solution.py:429
  261.7 12.8 %back.13 = (f32[192,128]{1,0:T(8,128)}, f32[192,128]{1,0:T(8,128)S(1)}, f32[56,896]{1,0:T(8,128)S(1)}, f32[256,96]{1,0:T(8,128)S(1)}, f32[768,896]{1,0:T(8,128)}...) custom-call(s32[8]{0:T(128)S(1)} %stack.31.refs_0_.refs_5_.refs_6_, ...), custom_call_target="tpu_custom_call", output_to_operand_aliasing={{4}: (23, {}), {9}: (24, {})} | custom-call | flops 15950000128 | bytes 1024 | tf_op jit(solution)/shard_map/back/pallas_call | solution.py:429
  279.1 12.9 %back.14 = (f32[192,128]{1,0:T(8,128)}, f32[192,128]{1,0:T(8,128)S(1)}, f32[56,896]{1,0:T(8,128)S(1)}, f32[256,96]{1,0:T(8,128)S(1)}, f32[768,896]{1,0:T(8,128)}...) custom-call(s32[8]{0:T(128)S(1)} %stack.31.refs_0_.refs_5_.refs_6_, ...), custom_call_target="tpu_custom_call", output_to_operand_aliasing={{4}: (23, {}), {9}: (24, {})} | custom-call | flops 15950000128 | bytes 1024 | tf_op jit(solution)/shard_map/back/pallas_call | solution.py:429
  296.1 12.9 %back.15 = (f32[192,128]{1,0:T(8,128)}, f32[192,128]{1,0:T(8,128)S(1)}, f32[56,896]{1,0:T(8,128)S(1)}, f32[256,96]{1,0:T(8,128)S(1)}, f32[768,896]{1,0:T(8,128)}...) custom-call(s32[8]{0:T(128)S(1)} %stack.31.refs_0_.refs_5_.refs_6_, ...), custom_call_target="tpu_custom_call", output_to_operand_aliasing={{4}: (23, {}), {9}: (24, {})} | custom-call | flops 15950000128 | bytes 1024 | tf_op jit(solution)/shard_map/back/pallas_call | solution.py:429
  313.6 13.6 %back.16 = (f32[192,128]{1,0:T(8,128)}, f32[192,128]{1,0:T(8,128)S(1)}, f32[56,896]{1,0:T(8,128)S(1)}, f32[256,96]{1,0:T(8,128)S(1)}, f32[768,896]{1,0:T(8,128)}...) custom-call(s32[8]{0:T(128)S(1)} %stack.31.refs_0_.refs_5_.refs_6_, ...), custom_call_target="tpu_custom_call", output_to_operand_aliasing={{4}: (23, {}), {9}: (24, {})} | custom-call | flops 15950000128 | bytes 1024 | tf_op jit(solution)/shard_map/back/pallas_call | solution.py:429
  331.6 7.6 %back.17 = (f32[192,128]{1,0:T(8,128)}, f32[192,128]{1,0:T(8,128)}, f32[56,896]{1,0:T(8,128)S(1)}, f32[256,96]{1,0:T(8,128)S(1)}, f32[768,896]{1,0:T(8,128)}) custom-call(s32[8]{0:T(128)S(1)} %stack.31.refs_0_.refs_5_.refs_6_, f32[192,128]{1,0:T(8,128)S(1)} %get-tuple-element.339.refs_14_.refs_8_.refs_1_, ...), custom_call_target="tpu_custom_call", output_to_operand_aliasing={{4}: (17, {})} | custom-call | flops 7699999744 | bytes 1024 | tf_op jit(solution)/shard_map/back/pallas_call | solution.py:429
  344.0 15.7 %last.1 = (f32[160,896]{1,0:T(8,128)S(1)}, f32[160,896]{1,0:T(8,128)S(1)}, f32[80,1664]{1,0:T(8,128)S(1)}, f32[80,1664]{1,0:T(8,128)S(1)}) custom-call(s32[8]{0:T(128)S(1)} %stack.31.refs_0_.refs_5_.refs_6_, f32[768,128]{1,0:T(8,128)} %get-tuple-element.588.refs_1_, f32[768,256]{1,0:T(8,128)} %get-tuple-element.589.refs_2_, ...), custom_call_target="tpu_custom_call" | custom-call | flops 13200000000 | bytes 1024 | tf_op jit(solution)/shard_map/last/pallas_call | solution.py:429
  393.1 6.5 %all-to-all-start.1 = ((f32[8,88,96]{2,1,0:T(8,128)}), f32[8,88,96]{2,1,0:T(8,128)S(1)}, u32[]{:S(2)}, u32[]{:S(2)}) async-start(f32[8,88,96]{2,1,0:T(8,128)} %get-tuple-element.632), calls=%async_computation.1 | async-start | bytes 720896 | tf_op jit(solution)/shard_map/all_to_all | solution.py:1100
  (301 shorter events, 188.7 us)
Async XLA Ops:
  5.5 21.3 %collective-permute-start.1 = (f32[159,96]{1,0:T(8,128)S(1)}, f32[159,96]{1,0:T(8,128)S(1)}, u32[]{:S(2)}, u32[]{:S(2)}) collective-permute-start(f32[159,96]{1,0:T(8,128)S(1)} %pad_maximum_fusion.3), channel_id=1, source_target_pairs={{1,0},{5,1},{0,2},{4,3},{3,4},{7,5},{2,6},{6,7},{9,8},{13,9},{8,10... | collective-permute-start | bytes 183176 | tf_op jit(solution)/shard_map/ppermute | solution.py:846
  6.3 20.5 %collective-permute-start = (f32[159,96]{1,0:T(8,128)S(1)}, f32[159,96]{1,0:T(8,128)S(1)}, u32[]{:S(2)}, u32[]{:S(2)}) collective-permute-start(f32[159,96]{1,0:T(8,128)S(1)} %pad_maximum_fusion.3), channel_id=1, source_target_pairs={{0,0},{4,1},{1,2},{5,3},{2,4},{6,5},{3,6},{7,7},{8,8},{12,9},{9,10... | collective-permute-start | bytes 183176 | tf_op jit(solution)/shard_map/ppermute | solution.py:846
  11.3 16.3 %all-to-all-start = ((f32[8,81,96]{2,1,0:T(8,128)}), f32[8,81,96]{2,1,0:T(8,128)S(1)}, u32[]{:S(2)}, u32[]{:S(2)}) async-start(f32[8,81,96]{2,1,0:T(8,128)} %constant_dynamic-slice_fusion.1), calls=%async_computation | async-start | bytes 720896 | tf_op jit(solution)/shard_map/all_to_all | solution.py:859
  27.6 12.4 %collective-permute-start.2 = (f32[104,384]{1,0:T(8,128)S(1)}, f32[104,384]{1,0:T(8,128)S(1)}, u32[]{:S(2)}, u32[]{:S(2)}) collective-permute-start(f32[104,384]{1,0:T(8,128)S(1)} %get-tuple-element.353.refs_4_.refs_10_), channel_id=1, source_target_pairs={{0,4},{4,0},{8,12},{12,8},{16,20},{20,16},{24,28},{28,24},{1,5},{5... | collective-permute-start | bytes 479240 | tf_op jit(solution)/shard_map/ppermute | solution.py:840
  27.8 16.8 %collective-permute-start.6 = (f32[8,81,96]{2,1,0:T(8,128)S(1)}, f32[8,81,96]{2,1,0:T(8,128)S(1)}, u32[]{:S(2)}, u32[]{:S(2)}) collective-permute-start(f32[8,81,96]{2,1,0:T(8,128)S(1)} %fusion.7), channel_id=1, source_target_pairs={{1,0},{5,1},{0,2},{4,3},{3,4},{7,5},{2,6},{6,7},{9,8},{13,9},{8,10... | collective-permute-start | bytes 746504 | tf_op jit(solution)/shard_map/ppermute | solution.py:846
  28.4 18.2 %collective-permute-start.5 = (f32[8,81,96]{2,1,0:T(8,128)S(1)}, f32[8,81,96]{2,1,0:T(8,128)S(1)}, u32[]{:S(2)}, u32[]{:S(2)}) collective-permute-start(f32[8,81,96]{2,1,0:T(8,128)S(1)} %fusion.7), channel_id=1, source_target_pairs={{0,0},{4,1},{1,2},{5,3},{2,4},{6,5},{3,6},{7,7},{8,8},{12,9},{9,10... | collective-permute-start | bytes 746504 | tf_op jit(solution)/shard_map/ppermute | solution.py:846
  164.9 166.2 %collective-permute-start.37 = (f32[96,896]{1,0:T(8,128)}, f32[96,896]{1,0:T(8,128)}, u32[]{:S(2)}, u32[]{:S(2)}) collective-permute-start(f32[96,896]{1,0:T(8,128)} %get-tuple-element.570), channel_id=1, source_target_pairs={{0,4},{4,0},{8,12},{12,8},{16,20},{20,16},{24,28},{28,24},{1,5},{5... | collective-permute-start | bytes 1032200 | tf_op jit(solution)/shard_map/ppermute | solution.py:840
  165.1 148.5 %collective-permute-start.35 = (f32[96,896]{1,0:T(8,128)}, f32[96,896]{1,0:T(8,128)}, u32[]{:S(2)}, u32[]{:S(2)}) collective-permute-start(f32[96,896]{1,0:T(8,128)} %get-tuple-element.553), channel_id=1, source_target_pairs={{0,4},{4,0},{8,12},{12,8},{16,20},{20,16},{24,28},{28,24},{1,5},{5... | collective-permute-start | bytes 1032200 | tf_op jit(solution)/shard_map/ppermute | solution.py:840
  165.4 74.3 %collective-permute-start.27 = (f32[96,896]{1,0:T(8,128)S(1)}, f32[96,896]{1,0:T(8,128)S(1)}, u32[]{:S(2)}, u32[]{:S(2)}) collective-permute-start(f32[96,896]{1,0:T(8,128)S(1)} %get-tuple-element.477), channel_id=1, source_target_pairs={{0,4},{4,0},{8,12},{12,8},{16,20},{20,16},{24,28},{28,24},{1,5},{5... | collective-permute-start | bytes 1032200 | tf_op jit(solution)/shard_map/ppermute | solution.py:840
  179.5 17.1 %collective-permute-start.22 = (f32[96,896]{1,0:T(8,128)S(1)}, f32[96,896]{1,0:T(8,128)S(1)}, u32[]{:S(2)}, u32[]{:S(2)}) collective-permute-start(f32[96,896]{1,0:T(8,128)S(1)} %get-tuple-element.437), channel_id=1, source_target_pairs={{0,4},{4,0},{8,12},{12,8},{16,20},{20,16},{24,28},{28,24},{1,5},{5... | collective-permute-start | bytes 1032200 | tf_op jit(solution)/shard_map/ppermute | solution.py:840
  196.6 21.5 %collective-permute-start.24 = (f32[96,896]{1,0:T(8,128)S(1)}, f32[96,896]{1,0:T(8,128)S(1)}, u32[]{:S(2)}, u32[]{:S(2)}) collective-permute-start(f32[96,896]{1,0:T(8,128)S(1)} %get-tuple-element.455), channel_id=1, source_target_pairs={{0,4},{4,0},{8,12},{12,8},{16,20},{20,16},{24,28},{28,24},{1,5},{5... | collective-permute-start | bytes 1032200 | tf_op jit(solution)/shard_map/ppermute | solution.py:840
  218.1 21.1 %collective-permute-start.25 = (f32[8,80,96]{2,1,0:T(8,128)S(1)}, f32[8,80,96]{2,1,0:T(8,128)S(1)}, u32[]{:S(2)}, u32[]{:S(2)}) collective-permute-start(f32[8,80,96]{2,1,0:T(8,128)S(1)} %copy-done.39), channel_id=1, source_target_pairs={{0,0},{1,4},{2,1},{3,5},{4,2},{5,6},{6,3},{7,7},{8,8},{9,12},{10,9... | collective-permute-start | bytes 737288 | tf_op jit(solution)/shard_map/ppermute | solution.py:972
  239.2 56.9 %collective-permute-start.33 = (f32[96,896]{1,0:T(8,128)S(1)}, f32[96,896]{1,0:T(8,128)S(1)}, u32[]{:S(2)}, u32[]{:S(2)}) collective-permute-start(f32[96,896]{1,0:T(8,128)S(1)} %get-tuple-element.534), channel_id=1, source_target_pairs={{0,4},{4,0},{8,12},{12,8},{16,20},{20,16},{24,28},{28,24},{1,5},{5... | collective-permute-start | bytes 1032200 | tf_op jit(solution)/shard_map/ppermute | solution.py:840
  239.8 21.8 %collective-permute-start.29 = (f32[96,896]{1,0:T(8,128)S(1)}, f32[96,896]{1,0:T(8,128)S(1)}, u32[]{:S(2)}, u32[]{:S(2)}) collective-permute-start(f32[96,896]{1,0:T(8,128)S(1)} %get-tuple-element.496), channel_id=1, source_target_pairs={{0,4},{4,0},{8,12},{12,8},{16,20},{20,16},{24,28},{28,24},{1,5},{5... | collective-permute-start | bytes 1032200 | tf_op jit(solution)/shard_map/ppermute | solution.py:840
  261.6 17.5 %collective-permute-start.31 = (f32[96,896]{1,0:T(8,128)S(1)}, f32[96,896]{1,0:T(8,128)S(1)}, u32[]{:S(2)}, u32[]{:S(2)}) collective-permute-start(f32[96,896]{1,0:T(8,128)S(1)} %get-tuple-element.515), channel_id=1, source_target_pairs={{0,4},{4,0},{8,12},{12,8},{16,20},{20,16},{24,28},{28,24},{1,5},{5... | collective-permute-start | bytes 1032200 | tf_op jit(solution)/shard_map/ppermute | solution.py:840
  341.4 19.9 %collective-permute-start.41 = (f32[2,200,400]{2,1,0:T(8,128)S(1)}, f32[2,200,400]{2,1,0:T(8,128)S(1)}, u32[]{:S(2)}, u32[]{:S(2)}) collective-permute-start(f32[2,200,400]{2,1,0:T(8,128)S(1)} %get-tuple-element.605), channel_id=1, source_target_pairs={{0,8},{4,12},{8,0},{12,4},{16,24},{20,28},{24,16},{28,20},{1,9},{5... | collective-permute-start | bytes 1920008 | tf_op jit(solution)/shard_map/ppermute | solution.py:1034
  342.8 19.5 %collective-permute-start.42 = (f32[2,200,400]{2,1,0:T(8,128)S(1)}, f32[2,200,400]{2,1,0:T(8,128)S(1)}, u32[]{:S(2)}, u32[]{:S(2)}) collective-permute-start(f32[2,200,400]{2,1,0:T(8,128)S(1)} %get-tuple-element.607), channel_id=1, source_target_pairs={{0,16},{4,20},{8,24},{12,28},{16,0},{20,4},{24,8},{28,12},{1,17},{... | collective-permute-start | bytes 1920008 | tf_op jit(solution)/shard_map/ppermute | solution.py:1034
  373.4 13.9 %collective-permute-start.44 = (f32[200,400]{1,0:T(8,128)S(1)}, f32[200,400]{1,0:T(8,128)S(1)}, u32[]{:S(2)}, u32[]{:S(2)}) collective-permute-start(f32[200,400]{1,0:T(8,128)S(1)} %get-tuple-element.613), channel_id=1, source_target_pairs={{0,16},{4,20},{8,24},{12,28},{16,0},{20,4},{24,8},{28,12},{1,17},{... | collective-permute-start | bytes 960008 | tf_op jit(solution)/shard_map/ppermute | solution.py:1034
  374.4 12.9 %collective-permute-start.45 = (f32[200,400]{1,0:T(8,128)S(1)}, f32[200,400]{1,0:T(8,128)S(1)}, u32[]{:S(2)}, u32[]{:S(2)}) collective-permute-start(f32[200,400]{1,0:T(8,128)S(1)} %get-tuple-element.615), channel_id=1, source_target_pairs={{0,8},{4,12},{8,0},{12,4},{16,24},{20,28},{24,16},{28,20},{1,9},{5... | collective-permute-start | bytes 960008 | tf_op jit(solution)/shard_map/ppermute | solution.py:1034
  380.7 11.1 %collective-permute-start.43 = (f32[224,96]{1,0:T(8,128)S(1)}, f32[224,96]{1,0:T(8,128)S(1)}, u32[]{:S(2)}, u32[]{:S(2)}) collective-permute-start(f32[224,96]{1,0:T(8,128)S(1)} %get-tuple-element.611), channel_id=1, source_target_pairs={{0,0},{1,4},{2,1},{3,5},{4,2},{5,6},{6,3},{7,7},{8,8},{9,12},{10,9... | collective-permute-start | bytes 258056 | tf_op jit(solution)/shard_map/ppermute | solution.py:1088
  383.2 16.4 %collective-permute-start.56 = (f32[40,896]{1,0:T(8,128)S(1)}, f32[40,896]{1,0:T(8,128)S(1)}, u32[]{:S(2)}, u32[]{:S(2)}) collective-permute-start(f32[40,896]{1,0:T(8,128)S(1)} %get-tuple-element.638.refs_1_), channel_id=1, source_target_pairs={{0,2},{1,3},{2,0},{3,1},{4,6},{5,7},{6,4},{7,5},{8,10},{9,11},{10,... | collective-permute-start | bytes 430088 | tf_op jit(solution)/shard_map/ppermute | solution.py:1034
  388.0 18.4 %collective-permute-start.54 = (f32[200,400]{1,0:T(8,128)S(1)}, f32[200,400]{1,0:T(8,128)S(1)}, u32[]{:S(2)}, u32[]{:S(2)}) collective-permute-start(f32[200,400]{1,0:T(8,128)S(1)} %get-tuple-element.634), channel_id=1, source_target_pairs={{0,1},{1,0},{2,3},{3,2},{4,5},{5,4},{6,7},{7,6},{8,9},{9,8},{10,11... | collective-permute-start | bytes 960008 | tf_op jit(solution)/shard_map/ppermute | solution.py:1034
  391.2 11.8 %collective-permute-start.55 = (f32[80,400]{1,0:T(8,128)S(1)}, f32[80,400]{1,0:T(8,128)S(1)}, u32[]{:S(2)}, u32[]{:S(2)}) collective-permute-start(f32[80,400]{1,0:T(8,128)S(1)} %get-tuple-element.635.refs_1_), channel_id=1, source_target_pairs={{0,2},{1,3},{2,0},{3,1},{4,6},{5,7},{6,4},{7,5},{8,10},{9,11},{10,... | collective-permute-start | bytes 384008 | tf_op jit(solution)/shard_map/ppermute | solution.py:1034
  393.1 14.7 %all-to-all-start.1 = ((f32[8,88,96]{2,1,0:T(8,128)}), f32[8,88,96]{2,1,0:T(8,128)S(1)}, u32[]{:S(2)}, u32[]{:S(2)}) async-start(f32[8,88,96]{2,1,0:T(8,128)} %get-tuple-element.632), calls=%async_computation.1 | async-start | bytes 720896 | tf_op jit(solution)/shard_map/all_to_all | solution.py:1100
  (79 other events, 460.1 us)

commit v5 on v4

--- a/solution.py
+++ b/solution.py
@@ -80,6 +80,25 @@
             mixed[i, v : v + 8, lanes] = total[i]
 
 
+def depthwise_direct(ext, kernel, mixed, lanes, rows):
+    tiles = range(0, COLS, 8)
+    total = [[None] * len(tiles) for _ in range(rows)]
+    for q in range(KW):
+        taps = [kernel[p * KW + q, :, lanes] for p in range(KW)]
+        for r in range(rows + 2 * HALO):
+            cells = ext[r, 5 + q : 5 + q + COLS, lanes]
+            for t, v in enumerate(tiles):
+                cell = cells[v : v + 8]
+                for p in range(KW):
+                    i = r - p
+                    if 0 <= i < rows:
+                        term = taps[p] * cell
+                        total[i][t] = term if total[i][t] is None else total[i][t] + term
+    for i in range(rows):
+        for t, v in enumerate(tiles):
+            mixed[i, v : v + 8, lanes] = total[i][t]
+
+
 def ocean_count(sent, came):
     last = sent.shape[0] - 1
     return jnp.maximum(sent[last:, :LANES] + came[last:, :LANES], 1.0)
@@ -92,7 +111,7 @@
 def mix_kernel(
     at, cur, cur_edge, prev, prev_edge, force, force_edge, w_in_hi, w_in_lo, b_in, w_oi_hi, w_oi_lo, b_new, taps, ocean,
     mixed_out, stats_out, base_out, window_out, x_all, lifted_all,
-    ext, shifted, mixed, x_part, sems, *, turn, cur_lanes, prev_lanes,
+    ext, mixed, x_part, sems, *, turn, cur_lanes, prev_lanes,
 ):
     core, part = at[0], at[1]
     px = cur.shape[0]
@@ -131,7 +150,7 @@
 
     def group(g, _):
         lanes = group_lanes(g)
-        depthwise(ext, shifted, taps, mixed, lanes, False, rows)
+        depthwise_direct(ext, taps, mixed, lanes, rows)
         cells = mixed[:, :, lanes].reshape(px, LANES)
         mixed_out[:, lanes] = cells
         masked = cells * mask
@@ -213,7 +232,8 @@
         act(2 * i + 1, hold_b)
         return 0
 
-    lax.fori_loop(0, chunks // 2, pair, 0)
+    for i in range(chunks // 2):
+        pair(i, 0)
     act(chunks - 1, hold_a)
     new = (acc[:, :LANES] + acc[:, LANES:] + acc_lo[...]) * ocean[...]
     new_out[...] = new
@@ -942,7 +962,7 @@
                 out(ROLL * HALO, COLS, width),
             ],
             [
-                pltpu.VMEM((rows + 2 * HALO, COLS + 16, width), F32), pltpu.VMEM((KW, rows + 2 * HALO, COLS, LANES), F32),
+                pltpu.VMEM((rows + 2 * HALO, COLS + 16, width), F32),
                 pltpu.VMEM((rows, COLS, width), F32), pltpu.VMEM((block, 2 * LANES), F32), pltpu.SemaphoreType.DMA((3,)),
             ],
             12, micros=4.5, smem=1, hbm_outs=(3,), stacked=((4, x_all), (5, lifted_all)),
@@ -961,7 +981,7 @@
                 pltpu.VMEM((px, CHUNK), F32), pltpu.VMEM((px, width), F32), pltpu.VMEM((chunks, px, CHUNK), F32),
                 pltpu.VMEM((chunks, block, CHUNK), F32), pltpu.VMEM((SEG, block), F32), pltpu.SemaphoreType.DMA((2 * chunks + 2,)),
             ],
-            16, micros=8.5, smem=1, hbm_outs=(4, 5), stacked=((6, act_all), (7, state_all)),
+            14, micros=8.5, smem=1, hbm_outs=(4, 5), stacked=((6, act_all), (7, state_all)),
         )
         prev, prev_edge, prev_lanes, cur = cur, cur_edge, cur_lanes, new
         if j < ROLL - 1:
@@ -1008,7 +1028,7 @@
             back_kernel, finish=finish, begin=begin, turn=j, width=width, k_main=k_main, k_rem=k_rem, states=states
         )
         results = list(
-            call(kernel, "back", args, outs, scratch, 20, micros=7 * finish + 7.5 * begin, smem=1, hbm=hbm, stacked=stacked)
+            call(kernel, "back", args, outs, scratch, 18, micros=7 * finish + 7.5 * begin, smem=1, hbm=hbm, stacked=stacked)
         )
         if finish:
             carry, pending, tap_sum, home, lift_all = results[:5]

time: 424 us -> 401 us (0.946)
  local copies, waits for them, and re-layouts: 33.4 us -> 20.7 us
  Pallas kernels: 292 us -> 281 us
    unnamed x86 -> x94, local copies, waits for them, and re-layouts: 27.2 us -> 14.4 us
    pallas_call x55, Pallas kernels: 292 us -> 281 us  [call(): pl.pallas_call(body, in_specs=specs, out_specs=[HBM_SPEC if i in hbm_outs...]
  transfers between devices with their start and end apart: 63 -> 63, of which waited for: 26 -> 26; matrix products, arithmetic and copies ran while one was open for 1% -> 1% of each run, Pallas kernels for 48% -> 50%
where the time goes in v5:
time: 401 us; the launch traced here: 396 us
  Pallas kernels  281 us (70%)
  starting transfers between devices  57.9 us (14%)
  waiting for transfers between devices  29.9 us (7%)
  local copies, waits for them, and re-layouts  20.7 us (5%)
    pallas_call x55, Pallas kernels, call(): pl.pallas_call(body, in_specs=specs, out_specs=[HBM_SPEC if i in hbm_outs...  281 us
    ppermute x22, starting transfers between devices, trade(): lax.ppermute(values, axis, [(i, i ^ flip) for i in range(lax.axis_size(ax...  20.4 us
    ppermute x22, waiting for transfers between devices, trade(): lax.ppermute(values, axis, [(i, i ^ flip) for i in range(lax.axis_size(ax...  16.3 us
    unnamed x94, local copies, waits for them, and re-layouts  14.4 us
    ppermute x33, waiting for transfers between devices, to_sibling(): return lax.ppermute(values, 'step', siblings)  11.6 us
    ppermute x4, starting transfers between devices, fetch_own(): got = [lax.ppermute(values, both_axes, perm) for perm in fetch_perms]  10.5 us
    ppermute x33, starting transfers between devices, to_sibling(): return lax.ppermute(values, 'step', siblings)  10.5 us
  transfers between devices with their start and end apart: 63, of which 26 were waited for; matrix products, arithmetic and copies ran while one was open for 1% of the time, Pallas kernels for 50%

profile of v5, /device:TPU:9, one launch (start us, length us, event | category | flops | bytes accessed | tf_op | source)
XLA Modules:
  0.0 396.2 jit_solution(6720867855319999113)
XLA Ops:
  17.4 6.7 %down.1 = (bf16[3328,256]{1,0:T(8,128)(2,1)S(1)}, bf16[256,3328]{1,0:T(8,128)(2,1)S(1)}) custom-call(f32[800,3200]{1,0:T(8,128)} %refs_6_.1, bf16[160,800]{1,0:T(8,128)(2,1)S(1)} %pad_maximum_fusion.2.refs_1_), custom_call_target="tpu_custom_call" | custom-call | flops 7699999744 | bytes 1024 | tf_op jit(solution)/shard_map/down/pallas_call | solution.py:449
  28.4 5.2 %collective-permute-start.5 = (f32[8,81,96]{2,1,0:T(8,128)S(1)}, f32[8,81,96]{2,1,0:T(8,128)S(1)}, u32[]{:S(2)}, u32[]{:S(2)}) collective-permute-start(f32[8,81,96]{2,1,0:T(8,128)S(1)} %fusion.7), channel_id=1, source_target_pairs={{0,0},{4,1},{1,2},{5,3},{2,4},{6,5},{3,6},{7,7},{8,8},{12,9},{9,10... | collective-permute-start | bytes 746504 | tf_op jit(solution)/shard_map/ppermute | solution.py:866
  33.5 6.5 %up.1.refs_10_.refs_8_.refs_22_ = bf16[1664,3328]{1,0:T(8,128)(2,1)S(1)} custom-call(f32[800,3200]{1,0:T(8,128)} %bitcast.80), custom_call_target="tpu_custom_call" | custom-call | flops 7699999744 | bytes 1024 | tf_op jit(solution)/shard_map/up/pallas_call | solution.py:449
  48.4 8.0 %feed.8 = (f32[192,128]{1,0:T(8,128)S(1)}, f32[96,128]{1,0:T(8,128)S(1)}, f32[96,896]{1,0:T(8,128)}, f32[8,896]{1,0:T(8,128)S(1)}, f32[192,896]{1,0:T(8,128)}, /...) custom-call(s32[8]{0:T(128)S(1)} %stack.31.refs_0_.refs_5_.refs_6_, ...), custom_call_target="tpu_custom_call" | custom-call | flops 9349999616 | bytes 1024 | tf_op jit(solution)/shard_map/feed/pallas_call | solution.py:449
  63.6 8.0 %feed.9 = (f32[192,128]{1,0:T(8,128)S(1)}, f32[96,128]{1,0:T(8,128)S(1)}, f32[96,896]{1,0:T(8,128)}, f32[8,896]{1,0:T(8,128)S(1)}, f32[192,896]{1,0:T(8,128)}, /...) custom-call(s32[8]{0:T(128)S(1)} %stack.31.refs_0_.refs_5_.refs_6_, ...), custom_call_target="tpu_custom_call", output_to_operand_aliasing={{6}: (13, {}), {7}: (14, {})} | custom-call | flops 9349999616 | bytes 1024 | tf_op jit(solution)/shard_map/feed/pallas_call | solution.py:449
  78.9 7.3 %feed.10 = (f32[192,128]{1,0:T(8,128)S(1)}, f32[96,128]{1,0:T(8,128)S(1)}, f32[96,896]{1,0:T(8,128)S(1)}, f32[8,896]{1,0:T(8,128)S(1)}, f32[192,896]{1,0:T(8,128...) custom-call(s32[8]{0:T(128)S(1)} %stack.31.refs_0_.refs_5_.refs_6_, ...), custom_call_target="tpu_custom_call", output_to_operand_aliasing={{6}: (13, {}), {7}: (14, {})} | custom-call | flops 9349999616 | bytes 1024 | tf_op jit(solution)/shard_map/feed/pallas_call | solution.py:449
  87.5 4.9 %mix.11 = (f32[192,896]{1,0:T(8,128)S(1)}, f32[8,896]{1,0:T(8,128)S(1)}, f32[192,128]{1,0:T(8,128)S(1)}, f32[9,32,896]{2,1,0:T(8,128)}, f32[768,256]{1,0:T(8,128)}, /*index=5*/f32[24,32,896]{2,1,0:T(8,128)}) custom-call(s32[8]{0:T(128)S(1)} %stack.31.refs_0_.refs_5_.refs_6_, ...), custom_call_target="tpu_custom_call", output_to_operand_aliasing={{4}: (15, {}), {5}: (16, {})} | custom-call | flops 4950000128 | bytes 1024 | tf_op jit(solution)/shard_map/mix/pallas_call | solution.py:449
  93.6 7.3 %feed.11 = (f32[192,128]{1,0:T(8,128)S(1)}, f32[96,128]{1,0:T(8,128)S(1)}, f32[96,896]{1,0:T(8,128)S(1)}, f32[8,896]{1,0:T(8,128)S(1)}, f32[192,896]{1,0:T(8,128...) custom-call(s32[8]{0:T(128)S(1)} %stack.31.refs_0_.refs_5_.refs_6_, ...), custom_call_target="tpu_custom_call", output_to_operand_aliasing={{6}: (13, {}), {7}: (14, {})} | custom-call | flops 9349999616 | bytes 1024 | tf_op jit(solution)/shard_map/feed/pallas_call | solution.py:449
  108.0 7.3 %feed.12 = (f32[192,128]{1,0:T(8,128)S(1)}, f32[96,128]{1,0:T(8,128)S(1)}, f32[96,896]{1,0:T(8,128)S(1)}, f32[8,896]{1,0:T(8,128)S(1)}, f32[192,896]{1,0:T(8,128...) custom-call(s32[8]{0:T(128)S(1)} %stack.31.refs_0_.refs_5_.refs_6_, ...), custom_call_target="tpu_custom_call", output_to_operand_aliasing={{6}: (13, {}), {7}: (14, {})} | custom-call | flops 9349999616 | bytes 1024 | tf_op jit(solution)/shard_map/feed/pallas_call | solution.py:449
  122.4 7.3 %feed.13 = (f32[192,128]{1,0:T(8,128)S(1)}, f32[96,128]{1,0:T(8,128)S(1)}, f32[96,896]{1,0:T(8,128)S(1)}, f32[8,896]{1,0:T(8,128)S(1)}, f32[192,896]{1,0:T(8,128...) custom-call(s32[8]{0:T(128)S(1)} %stack.31.refs_0_.refs_5_.refs_6_, ...), custom_call_target="tpu_custom_call", output_to_operand_aliasing={{6}: (13, {}), {7}: (14, {})} | custom-call | flops 9349999616 | bytes 1024 | tf_op jit(solution)/shard_map/feed/pallas_call | solution.py:449
  136.8 7.3 %feed.14 = (f32[192,128]{1,0:T(8,128)S(1)}, f32[96,128]{1,0:T(8,128)S(1)}, f32[96,896]{1,0:T(8,128)S(1)}, f32[8,896]{1,0:T(8,128)S(1)}, f32[192,896]{1,0:T(8,128...) custom-call(s32[8]{0:T(128)S(1)} %stack.31.refs_0_.refs_5_.refs_6_, ...), custom_call_target="tpu_custom_call", output_to_operand_aliasing={{6}: (13, {}), {7}: (14, {})} | custom-call | flops 9349999616 | bytes 1024 | tf_op jit(solution)/shard_map/feed/pallas_call | solution.py:449
  145.4 4.6 %mix.15 = (f32[192,896]{1,0:T(8,128)S(1)}, f32[8,896]{1,0:T(8,128)S(1)}, f32[192,128]{1,0:T(8,128)S(1)}, f32[9,32,896]{2,1,0:T(8,128)}, f32[768,256]{1,0:T(8,128)}, /*index=5*/f32[24,32,896]{2,1,0:T(8,128)}) custom-call(s32[8]{0:T(128)S(1)} %stack.31.refs_0_.refs_5_.refs_6_, ...), custom_call_target="tpu_custom_call", output_to_operand_aliasing={{4}: (15, {}), {5}: (16, {})} | custom-call | flops 4950000128 | bytes 1024 | tf_op jit(solution)/shard_map/mix/pallas_call | solution.py:449
  151.3 7.9 %feed.15 = (f32[192,128]{1,0:T(8,128)}, f32[96,128]{1,0:T(8,128)}, f32[96,896]{1,0:T(8,128)S(1)}, f32[8,896]{1,0:T(8,128)S(1)}, f32[192,896]{1,0:T(8,128)}, /*in...) custom-call(s32[8]{0:T(128)S(1)} %stack.31.refs_0_.refs_5_.refs_6_, ...), custom_call_target="tpu_custom_call", output_to_operand_aliasing={{6}: (13, {}), {7}: (14, {})} | custom-call | flops 9349999616 | bytes 1024 | tf_op jit(solution)/shard_map/feed/pallas_call | solution.py:449
  160.8 8.4 %back.9 = (f32[192,896]{1,0:T(8,128)S(1)}, bf16[384,3328]{1,0:T(8,128)(2,1)S(1)}, f32[192,896]{1,0:T(8,128)S(1)}, f32[104,896]{1,0:T(8,128)S(1)}, f32[768,128]{1,0:T(8,128)}) custom-call(s32[8]{0:T(128)S(1)} %stack.31.refs_0_.refs_5_.refs_6_, f32[192,128]{1,0:T(8,128)S(1)} %get-tuple-element.339.refs_14_.refs_8_.refs_1_, ...), custom_call_target="tpu_custom_call" | custom-call | flops 8249999872 | bytes 1024 | tf_op jit(solution)/shard_map/back/pallas_call | solution.py:449
  174.7 12.8 %back.10 = (f32[192,128]{1,0:T(8,128)}, f32[192,128]{1,0:T(8,128)S(1)}, f32[56,896]{1,0:T(8,128)S(1)}, f32[256,96]{1,0:T(8,128)S(1)}, f32[768,896]{1,0:T(8,128)}...) custom-call(s32[8]{0:T(128)S(1)} %stack.31.refs_0_.refs_5_.refs_6_, ...), custom_call_target="tpu_custom_call", output_to_operand_aliasing={{9}: (23, {})} | custom-call | flops 15950000128 | bytes 1024 | tf_op jit(solution)/shard_map/back/pallas_call | solution.py:449
  202.3 12.9 %back.11 = (f32[192,128]{1,0:T(8,128)}, f32[192,128]{1,0:T(8,128)S(1)}, f32[56,896]{1,0:T(8,128)S(1)}, f32[256,96]{1,0:T(8,128)S(1)}, f32[768,896]{1,0:T(8,128)}...) custom-call(s32[8]{0:T(128)S(1)} %stack.31.refs_0_.refs_5_.refs_6_, ...), custom_call_target="tpu_custom_call", output_to_operand_aliasing={{4}: (23, {}), {9}: (24, {})} | custom-call | flops 15950000128 | bytes 1024 | tf_op jit(solution)/shard_map/back/pallas_call | solution.py:449
  220.0 12.9 %back.12 = (f32[192,128]{1,0:T(8,128)}, f32[192,128]{1,0:T(8,128)S(1)}, f32[56,896]{1,0:T(8,128)S(1)}, f32[256,96]{1,0:T(8,128)S(1)}, f32[768,896]{1,0:T(8,128)}...) custom-call(s32[8]{0:T(128)S(1)} %stack.31.refs_0_.refs_5_.refs_6_, ...), custom_call_target="tpu_custom_call", output_to_operand_aliasing={{4}: (23, {}), {9}: (24, {})} | custom-call | flops 15950000128 | bytes 1024 | tf_op jit(solution)/shard_map/back/pallas_call | solution.py:449
  237.6 13.1 %back.13 = (f32[192,128]{1,0:T(8,128)}, f32[192,128]{1,0:T(8,128)S(1)}, f32[56,896]{1,0:T(8,128)S(1)}, f32[256,96]{1,0:T(8,128)S(1)}, f32[768,896]{1,0:T(8,128)}...) custom-call(s32[8]{0:T(128)S(1)} %stack.31.refs_0_.refs_5_.refs_6_, ...), custom_call_target="tpu_custom_call", output_to_operand_aliasing={{4}: (23, {}), {9}: (24, {})} | custom-call | flops 15950000128 | bytes 1024 | tf_op jit(solution)/shard_map/back/pallas_call | solution.py:449
  255.2 12.8 %back.14 = (f32[192,128]{1,0:T(8,128)}, f32[192,128]{1,0:T(8,128)S(1)}, f32[56,896]{1,0:T(8,128)S(1)}, f32[256,96]{1,0:T(8,128)S(1)}, f32[768,896]{1,0:T(8,128)}...) custom-call(s32[8]{0:T(128)S(1)} %stack.31.refs_0_.refs_5_.refs_6_, ...), custom_call_target="tpu_custom_call", output_to_operand_aliasing={{4}: (23, {}), {9}: (24, {})} | custom-call | flops 15950000128 | bytes 1024 | tf_op jit(solution)/shard_map/back/pallas_call | solution.py:449
  272.3 12.9 %back.15 = (f32[192,128]{1,0:T(8,128)}, f32[192,128]{1,0:T(8,128)S(1)}, f32[56,896]{1,0:T(8,128)S(1)}, f32[256,96]{1,0:T(8,128)S(1)}, f32[768,896]{1,0:T(8,128)}...) custom-call(s32[8]{0:T(128)S(1)} %stack.31.refs_0_.refs_5_.refs_6_, ...), custom_call_target="tpu_custom_call", output_to_operand_aliasing={{4}: (23, {}), {9}: (24, {})} | custom-call | flops 15950000128 | bytes 1024 | tf_op jit(solution)/shard_map/back/pallas_call | solution.py:449
  289.7 13.3 %back.16 = (f32[192,128]{1,0:T(8,128)}, f32[192,128]{1,0:T(8,128)S(1)}, f32[56,896]{1,0:T(8,128)S(1)}, f32[256,96]{1,0:T(8,128)S(1)}, f32[768,896]{1,0:T(8,128)}...) custom-call(s32[8]{0:T(128)S(1)} %stack.31.refs_0_.refs_5_.refs_6_, ...), custom_call_target="tpu_custom_call", output_to_operand_aliasing={{4}: (23, {}), {9}: (24, {})} | custom-call | flops 15950000128 | bytes 1024 | tf_op jit(solution)/shard_map/back/pallas_call | solution.py:449
  307.5 7.6 %back.17 = (f32[192,128]{1,0:T(8,128)}, f32[192,128]{1,0:T(8,128)}, f32[56,896]{1,0:T(8,128)S(1)}, f32[256,96]{1,0:T(8,128)S(1)}, f32[768,896]{1,0:T(8,128)}) custom-call(s32[8]{0:T(128)S(1)} %stack.31.refs_0_.refs_5_.refs_6_, f32[192,128]{1,0:T(8,128)S(1)} %get-tuple-element.339.refs_14_.refs_8_.refs_1_, ...), custom_call_target="tpu_custom_call", output_to_operand_aliasing={{4}: (17, {})} | custom-call | flops 7699999744 | bytes 1024 | tf_op jit(solution)/shard_map/back/pallas_call | solution.py:449
  319.9 15.7 %last.1 = (f32[160,896]{1,0:T(8,128)S(1)}, f32[160,896]{1,0:T(8,128)S(1)}, f32[80,1664]{1,0:T(8,128)S(1)}, f32[80,1664]{1,0:T(8,128)S(1)}) custom-call(s32[8]{0:T(128)S(1)} %stack.31.refs_0_.refs_5_.refs_6_, f32[768,128]{1,0:T(8,128)} %get-tuple-element.588.refs_1_, f32[768,256]{1,0:T(8,128)} %get-tuple-element.589.refs_2_, ...), custom_call_target="tpu_custom_call" | custom-call | flops 13200000000 | bytes 1024 | tf_op jit(solution)/shard_map/last/pallas_call | solution.py:449
  369.0 6.6 %all-to-all-start.1 = ((f32[8,88,96]{2,1,0:T(8,128)}), f32[8,88,96]{2,1,0:T(8,128)S(1)}, u32[]{:S(2)}, u32[]{:S(2)}) async-start(f32[8,88,96]{2,1,0:T(8,128)} %get-tuple-element.632), calls=%async_computation.1 | async-start | bytes 720896 | tf_op jit(solution)/shard_map/all_to_all | solution.py:1120
  (309 shorter events, 175.8 us)
Async XLA Ops:
  5.5 21.3 %collective-permute-start.1 = (f32[159,96]{1,0:T(8,128)S(1)}, f32[159,96]{1,0:T(8,128)S(1)}, u32[]{:S(2)}, u32[]{:S(2)}) collective-permute-start(f32[159,96]{1,0:T(8,128)S(1)} %pad_maximum_fusion.3), channel_id=1, source_target_pairs={{1,0},{5,1},{0,2},{4,3},{3,4},{7,5},{2,6},{6,7},{9,8},{13,9},{8,10... | collective-permute-start | bytes 183176 | tf_op jit(solution)/shard_map/ppermute | solution.py:866
  6.3 20.5 %collective-permute-start = (f32[159,96]{1,0:T(8,128)S(1)}, f32[159,96]{1,0:T(8,128)S(1)}, u32[]{:S(2)}, u32[]{:S(2)}) collective-permute-start(f32[159,96]{1,0:T(8,128)S(1)} %pad_maximum_fusion.3), channel_id=1, source_target_pairs={{0,0},{4,1},{1,2},{5,3},{2,4},{6,5},{3,6},{7,7},{8,8},{12,9},{9,10... | collective-permute-start | bytes 183176 | tf_op jit(solution)/shard_map/ppermute | solution.py:866
  11.3 16.3 %all-to-all-start = ((f32[8,81,96]{2,1,0:T(8,128)}), f32[8,81,96]{2,1,0:T(8,128)S(1)}, u32[]{:S(2)}, u32[]{:S(2)}) async-start(f32[8,81,96]{2,1,0:T(8,128)} %constant_dynamic-slice_fusion.1), calls=%async_computation | async-start | bytes 720896 | tf_op jit(solution)/shard_map/all_to_all | solution.py:879
  27.5 12.5 %collective-permute-start.2 = (f32[104,384]{1,0:T(8,128)S(1)}, f32[104,384]{1,0:T(8,128)S(1)}, u32[]{:S(2)}, u32[]{:S(2)}) collective-permute-start(f32[104,384]{1,0:T(8,128)S(1)} %get-tuple-element.353.refs_4_.refs_10_), channel_id=1, source_target_pairs={{0,4},{4,0},{8,12},{12,8},{16,20},{20,16},{24,28},{28,24},{1,5},{5... | collective-permute-start | bytes 479240 | tf_op jit(solution)/shard_map/ppermute | solution.py:860
  27.8 16.6 %collective-permute-start.6 = (f32[8,81,96]{2,1,0:T(8,128)S(1)}, f32[8,81,96]{2,1,0:T(8,128)S(1)}, u32[]{:S(2)}, u32[]{:S(2)}) collective-permute-start(f32[8,81,96]{2,1,0:T(8,128)S(1)} %fusion.7), channel_id=1, source_target_pairs={{1,0},{5,1},{0,2},{4,3},{3,4},{7,5},{2,6},{6,7},{9,8},{13,9},{8,10... | collective-permute-start | bytes 746504 | tf_op jit(solution)/shard_map/ppermute | solution.py:866
  28.4 18.2 %collective-permute-start.5 = (f32[8,81,96]{2,1,0:T(8,128)S(1)}, f32[8,81,96]{2,1,0:T(8,128)S(1)}, u32[]{:S(2)}, u32[]{:S(2)}) collective-permute-start(f32[8,81,96]{2,1,0:T(8,128)S(1)} %fusion.7), channel_id=1, source_target_pairs={{0,0},{4,1},{1,2},{5,3},{2,4},{6,5},{3,6},{7,7},{8,8},{12,9},{9,10... | collective-permute-start | bytes 746504 | tf_op jit(solution)/shard_map/ppermute | solution.py:866
  150.5 156.5 %collective-permute-start.37 = (f32[96,896]{1,0:T(8,128)}, f32[96,896]{1,0:T(8,128)}, u32[]{:S(2)}, u32[]{:S(2)}) collective-permute-start(f32[96,896]{1,0:T(8,128)} %get-tuple-element.570), channel_id=1, source_target_pairs={{0,4},{4,0},{8,12},{12,8},{16,20},{20,16},{24,28},{28,24},{1,5},{5... | collective-permute-start | bytes 1032200 | tf_op jit(solution)/shard_map/ppermute | solution.py:860
  150.7 139.0 %collective-permute-start.35 = (f32[96,896]{1,0:T(8,128)}, f32[96,896]{1,0:T(8,128)}, u32[]{:S(2)}, u32[]{:S(2)}) collective-permute-start(f32[96,896]{1,0:T(8,128)} %get-tuple-element.553), channel_id=1, source_target_pairs={{0,4},{4,0},{8,12},{12,8},{16,20},{20,16},{24,28},{28,24},{1,5},{5... | collective-permute-start | bytes 1032200 | tf_op jit(solution)/shard_map/ppermute | solution.py:860
  151.0 68.9 %collective-permute-start.27 = (f32[96,896]{1,0:T(8,128)S(1)}, f32[96,896]{1,0:T(8,128)S(1)}, u32[]{:S(2)}, u32[]{:S(2)}) collective-permute-start(f32[96,896]{1,0:T(8,128)S(1)} %get-tuple-element.477), channel_id=1, source_target_pairs={{0,4},{4,0},{8,12},{12,8},{16,20},{20,16},{24,28},{28,24},{1,5},{5... | collective-permute-start | bytes 1032200 | tf_op jit(solution)/shard_map/ppermute | solution.py:860
  159.3 15.0 %collective-permute-start.22 = (f32[96,896]{1,0:T(8,128)S(1)}, f32[96,896]{1,0:T(8,128)S(1)}, u32[]{:S(2)}, u32[]{:S(2)}) collective-permute-start(f32[96,896]{1,0:T(8,128)S(1)} %get-tuple-element.437), channel_id=1, source_target_pairs={{0,4},{4,0},{8,12},{12,8},{16,20},{20,16},{24,28},{28,24},{1,5},{5... | collective-permute-start | bytes 1032200 | tf_op jit(solution)/shard_map/ppermute | solution.py:860
  174.3 23.8 %collective-permute-start.24 = (f32[96,896]{1,0:T(8,128)S(1)}, f32[96,896]{1,0:T(8,128)S(1)}, u32[]{:S(2)}, u32[]{:S(2)}) collective-permute-start(f32[96,896]{1,0:T(8,128)S(1)} %get-tuple-element.455), channel_id=1, source_target_pairs={{0,4},{4,0},{8,12},{12,8},{16,20},{20,16},{24,28},{28,24},{1,5},{5... | collective-permute-start | bytes 1032200 | tf_op jit(solution)/shard_map/ppermute | solution.py:860
  188.9 13.3 %collective-permute-start.23 = (f32[104,896]{1,0:T(8,128)S(1)}, f32[104,896]{1,0:T(8,128)S(1)}, u32[]{:S(2)}, u32[]{:S(2)}) collective-permute-start(f32[104,896]{1,0:T(8,128)S(1)} %get-tuple-element.446.refs_5_.refs_4_), channel_id=1, source_target_pairs={{0,4},{4,0},{8,12},{12,8},{16,20},{20,16},{24,28},{28,24},{1,5},{5... | collective-permute-start | bytes 1118216 | tf_op jit(solution)/shard_map/ppermute | solution.py:860
  198.1 21.2 %collective-permute-start.25 = (f32[8,80,96]{2,1,0:T(8,128)S(1)}, f32[8,80,96]{2,1,0:T(8,128)S(1)}, u32[]{:S(2)}, u32[]{:S(2)}) collective-permute-start(f32[8,80,96]{2,1,0:T(8,128)S(1)} %copy-done.43), channel_id=1, source_target_pairs={{0,0},{1,4},{2,1},{3,5},{4,2},{5,6},{6,3},{7,7},{8,8},{9,12},{10,9... | collective-permute-start | bytes 737288 | tf_op jit(solution)/shard_map/ppermute | solution.py:992
  219.3 52.9 %collective-permute-start.33 = (f32[96,896]{1,0:T(8,128)S(1)}, f32[96,896]{1,0:T(8,128)S(1)}, u32[]{:S(2)}, u32[]{:S(2)}) collective-permute-start(f32[96,896]{1,0:T(8,128)S(1)} %get-tuple-element.534), channel_id=1, source_target_pairs={{0,4},{4,0},{8,12},{12,8},{16,20},{20,16},{24,28},{28,24},{1,5},{5... | collective-permute-start | bytes 1032200 | tf_op jit(solution)/shard_map/ppermute | solution.py:860
  219.9 17.5 %collective-permute-start.29 = (f32[96,896]{1,0:T(8,128)S(1)}, f32[96,896]{1,0:T(8,128)S(1)}, u32[]{:S(2)}, u32[]{:S(2)}) collective-permute-start(f32[96,896]{1,0:T(8,128)S(1)} %get-tuple-element.496), channel_id=1, source_target_pairs={{0,4},{4,0},{8,12},{12,8},{16,20},{20,16},{24,28},{28,24},{1,5},{5... | collective-permute-start | bytes 1032200 | tf_op jit(solution)/shard_map/ppermute | solution.py:860
  237.4 17.8 %collective-permute-start.31 = (f32[96,896]{1,0:T(8,128)S(1)}, f32[96,896]{1,0:T(8,128)S(1)}, u32[]{:S(2)}, u32[]{:S(2)}) collective-permute-start(f32[96,896]{1,0:T(8,128)S(1)} %get-tuple-element.515), channel_id=1, source_target_pairs={{0,4},{4,0},{8,12},{12,8},{16,20},{20,16},{24,28},{28,24},{1,5},{5... | collective-permute-start | bytes 1032200 | tf_op jit(solution)/shard_map/ppermute | solution.py:860
  317.2 19.9 %collective-permute-start.41 = (f32[2,200,400]{2,1,0:T(8,128)S(1)}, f32[2,200,400]{2,1,0:T(8,128)S(1)}, u32[]{:S(2)}, u32[]{:S(2)}) collective-permute-start(f32[2,200,400]{2,1,0:T(8,128)S(1)} %get-tuple-element.605), channel_id=1, source_target_pairs={{0,8},{4,12},{8,0},{12,4},{16,24},{20,28},{24,16},{28,20},{1,9},{5... | collective-permute-start | bytes 1920008 | tf_op jit(solution)/shard_map/ppermute | solution.py:1054
  318.7 19.5 %collective-permute-start.42 = (f32[2,200,400]{2,1,0:T(8,128)S(1)}, f32[2,200,400]{2,1,0:T(8,128)S(1)}, u32[]{:S(2)}, u32[]{:S(2)}) collective-permute-start(f32[2,200,400]{2,1,0:T(8,128)S(1)} %get-tuple-element.607), channel_id=1, source_target_pairs={{0,16},{4,20},{8,24},{12,28},{16,0},{20,4},{24,8},{28,12},{1,17},{... | collective-permute-start | bytes 1920008 | tf_op jit(solution)/shard_map/ppermute | solution.py:1054
  349.2 13.9 %collective-permute-start.44 = (f32[200,400]{1,0:T(8,128)S(1)}, f32[200,400]{1,0:T(8,128)S(1)}, u32[]{:S(2)}, u32[]{:S(2)}) collective-permute-start(f32[200,400]{1,0:T(8,128)S(1)} %get-tuple-element.613), channel_id=1, source_target_pairs={{0,16},{4,20},{8,24},{12,28},{16,0},{20,4},{24,8},{28,12},{1,17},{... | collective-permute-start | bytes 960008 | tf_op jit(solution)/shard_map/ppermute | solution.py:1054
  350.2 12.9 %collective-permute-start.45 = (f32[200,400]{1,0:T(8,128)S(1)}, f32[200,400]{1,0:T(8,128)S(1)}, u32[]{:S(2)}, u32[]{:S(2)}) collective-permute-start(f32[200,400]{1,0:T(8,128)S(1)} %get-tuple-element.615), channel_id=1, source_target_pairs={{0,8},{4,12},{8,0},{12,4},{16,24},{20,28},{24,16},{28,20},{1,9},{5... | collective-permute-start | bytes 960008 | tf_op jit(solution)/shard_map/ppermute | solution.py:1054
  359.0 16.5 %collective-permute-start.56 = (f32[40,896]{1,0:T(8,128)S(1)}, f32[40,896]{1,0:T(8,128)S(1)}, u32[]{:S(2)}, u32[]{:S(2)}) collective-permute-start(f32[40,896]{1,0:T(8,128)S(1)} %get-tuple-element.638.refs_1_), channel_id=1, source_target_pairs={{0,2},{1,3},{2,0},{3,1},{4,6},{5,7},{6,4},{7,5},{8,10},{9,11},{10,... | collective-permute-start | bytes 430088 | tf_op jit(solution)/shard_map/ppermute | solution.py:1054
  363.8 18.3 %collective-permute-start.54 = (f32[200,400]{1,0:T(8,128)S(1)}, f32[200,400]{1,0:T(8,128)S(1)}, u32[]{:S(2)}, u32[]{:S(2)}) collective-permute-start(f32[200,400]{1,0:T(8,128)S(1)} %get-tuple-element.634), channel_id=1, source_target_pairs={{0,1},{1,0},{2,3},{3,2},{4,5},{5,4},{6,7},{7,6},{8,9},{9,8},{10,11... | collective-permute-start | bytes 960008 | tf_op jit(solution)/shard_map/ppermute | solution.py:1054
  367.0 11.9 %collective-permute-start.55 = (f32[80,400]{1,0:T(8,128)S(1)}, f32[80,400]{1,0:T(8,128)S(1)}, u32[]{:S(2)}, u32[]{:S(2)}) collective-permute-start(f32[80,400]{1,0:T(8,128)S(1)} %get-tuple-element.635.refs_1_), channel_id=1, source_target_pairs={{0,2},{1,3},{2,0},{3,1},{4,6},{5,7},{6,4},{7,5},{8,10},{9,11},{10,... | collective-permute-start | bytes 384008 | tf_op jit(solution)/shard_map/ppermute | solution.py:1054
  369.0 14.7 %all-to-all-start.1 = ((f32[8,88,96]{2,1,0:T(8,128)}), f32[8,88,96]{2,1,0:T(8,128)S(1)}, u32[]{:S(2)}, u32[]{:S(2)}) async-start(f32[8,88,96]{2,1,0:T(8,128)} %get-tuple-element.632), calls=%async_computation.1 | async-start | bytes 720896 | tf_op jit(solution)/shard_map/all_to_all | solution.py:1120
  (83 other events, 543.2 us)

commit v6 on v5

--- a/solution.py
+++ b/solution.py
@@ -109,7 +109,7 @@
 
 
 def mix_kernel(
-    at, cur, cur_edge, prev, prev_edge, force, force_edge, w_in_hi, w_in_lo, b_in, w_oi_hi, w_oi_lo, b_new, taps, ocean,
+    at, cur, cur_edge, prev, prev_edge, force, force_edge, w_in_hi, w_in_lo, b_in, b_new, taps, ocean,
     mixed_out, stats_out, base_out, window_out, x_all, lifted_all,
     ext, mixed, x_part, sems, *, turn, cur_lanes, prev_lanes,
 ):
@@ -127,8 +127,9 @@
     edge_hi, edge_lo = split(edge)
     both = dot(jnp.concatenate([own_hi, edge_hi, own_lo, edge_lo], axis=0), w_in_hi[...])
     high = dot(jnp.concatenate([own_hi, edge_hi], axis=0), w_in_lo[...])
-    lifted = (both[: px + edge_px] + both[px + edge_px :]) + (high + b_in[...])
-    base_out[...] = dot(own_hi, w_oi_hi[...]) + dot(own_lo, w_oi_hi[...]) + dot(own_hi, w_oi_lo[...]) + b_new[...]
+    both = (both[: px + edge_px] + both[px + edge_px :]) + high
+    lifted = both[:, :width] + b_in[...]
+    base_out[...] = both[:px, width:] + b_new[...]
     zeros = jnp.zeros((rows + 2 * HALO, 8, width), F32)
     ext[:, :8, :] = zeros
     ext[:, 8 + COLS :, :] = zeros
@@ -320,8 +321,8 @@
         )
         keep_lift.start()
         high, low = split(grad_lift[...])
-        both = dot_t(jnp.concatenate([high, low], axis=0), w_in_hi[...])
-        grad_x = (both[:px] + both[px:]) + dot_t(high, w_in_lo[...])
+        both = dot_t(jnp.concatenate([high, low], axis=0), w_in_hi[:, :width])
+        grad_x = (both[:px] + both[px:]) + dot_t(high, w_in_lo[:, :width])
         carry = grad_x[:, LANES:] + pending_in[...]
         carry_out[...] = carry
         pending_out[...] = grad_x[:, :LANES]
@@ -353,7 +354,8 @@
             pulled[:, cols] = dot(left, w_od[:, cols])
             return 0
 
-        lax.fori_loop(0, 2, pull, 0)
+        pull(0, 0)
+        pull(1, 0)
 
         def chunk(t, _):
             cols = pl.ds(pl.multiple_of(t * CHUNK, CHUNK), CHUNK)
@@ -362,7 +364,8 @@
             hidden_out[px:, cols] = low
             return 0
 
-        lax.fori_loop(0, chunks, chunk, 0)
+        for t in range(chunks):
+            chunk(t, 0)
         both = dot_t(hidden_out[...], w_up[:k_main])
         grad_n_out[:, :k_main] = (both[:px] + both[px:]) + dot_t(hidden_out[:px], w_up[k_main : 2 * k_main])
         rest = dot_t(hidden_out[...], w_up[2 * k_main :])
@@ -902,9 +905,9 @@
     def row(values, size):
         return jnp.pad(values, (0, size - values.shape[0]))[None]
 
-    w_in_hi, w_in_lo = split_outside(pad_to(in_rows(w_in.T), (2 * LANES, width)))
-    w_oi = pad_to(in_rows(jnp.dot(w_out, w_in, precision=HIGHEST).T), (2 * LANES, LANES))
-    w_oi_hi, w_oi_lo = split_outside(w_oi)
+    w_oi = jnp.dot(w_out, w_in, precision=HIGHEST)
+    w_first = jnp.concatenate([pad_to(in_rows(v.T), (2 * LANES, round_up(v.shape[0], LANES))) for v in (w_in, w_oi)], axis=1)
+    w_in_hi, w_in_lo = split_outside(w_first)
     b_new = row(jnp.dot(w_out, b_in + b_down, precision=HIGHEST) + b_out, LANES)
     taps = jnp.broadcast_to(
         pad_to(w_dw.reshape(channels, KW * KW).T, (KW * KW, width))[:, None], (KW * KW, 8, width)
@@ -932,9 +935,9 @@
     )
     first_came = to_sibling(first_sent)
     ready = lax.optimization_barrier(
-        (w_up.T, timed, w_in_hi, w_in_lo, w_oi_hi, w_oi_lo, b_new, taps, gain, bias, w_out_bwd, b_in_row, b_up_row, b_down_row, w_block_hi, w_block_lo, at, first_sent)
+        (w_up.T, timed, w_in_hi, w_in_lo, b_new, taps, gain, bias, w_out_bwd, b_in_row, b_up_row, b_down_row, w_block_hi, w_block_lo, at, first_sent)
     )
-    up_source, timed, w_in_hi, w_in_lo, w_oi_hi, w_oi_lo, b_new, taps, gain, bias, w_out_bwd, b_in_row, b_up_row, b_down_row, w_block_hi, w_block_lo, at, first_sent = ready
+    up_source, timed, w_in_hi, w_in_lo, b_new, taps, gain, bias, w_out_bwd, b_in_row, b_up_row, b_down_row, w_block_hi, w_block_lo, at, first_sent = ready
     timed = fetch_own(timed)
     (w_up_all,) = call(
         functools.partial(up_kernel, k_main=k_main, k_rem=k_rem, spans=spans), "up", (up_source,),
@@ -956,7 +959,7 @@
     for j in range(ROLL):
         mixed, stats, base, window, x_all, lifted_all = call(
             functools.partial(mix_kernel, turn=j, cur_lanes=cur_lanes, prev_lanes=prev_lanes), "mix",
-            (at, cur, cur_edge, prev, prev_edge) + ((force, force_edge) if j else (at, at)) + (w_in_hi, w_in_lo, b_in_row, w_oi_hi, w_oi_lo, b_new, taps, ocean),
+            (at, cur, cur_edge, prev, prev_edge) + ((force, force_edge) if j else (at, at)) + (w_in_hi, w_in_lo, b_in_row, b_new, taps, ocean),
             [
                 out(px, width), out(8, width), out(px, LANES), out(HALO + 2 * HALO, COLS, width), out(ROLL * block, 2 * LANES),
                 out(ROLL * HALO, COLS, width),

time: 401 us -> 394 us (0.983)
  Pallas kernels: 281 us -> 275 us
    pallas_call x55, Pallas kernels: 281 us -> 275 us  [call(): pl.pallas_call(body, in_specs=specs, out_specs=[HBM_SPEC if i in hbm_outs...]
where the time goes in v6:
time: 394 us; the launch traced here: 390 us
  Pallas kernels  275 us (70%)
  starting transfers between devices  58.1 us (15%)
  waiting for transfers between devices  29.7 us (8%)
  local copies, waits for them, and re-layouts  20.6 us (5%)
    pallas_call x55, Pallas kernels, call(): pl.pallas_call(body, in_specs=specs, out_specs=[HBM_SPEC if i in hbm_outs...  275 us
    ppermute x22, starting transfers between devices, trade(): lax.ppermute(values, axis, [(i, i ^ flip) for i in range(lax.axis_size(ax...  20.4 us
    ppermute x22, waiting for transfers between devices, trade(): lax.ppermute(values, axis, [(i, i ^ flip) for i in range(lax.axis_size(ax...  16.3 us
    unnamed x94, local copies, waits for them, and re-layouts  14.3 us
    ppermute x33, waiting for transfers between devices, to_sibling(): return lax.ppermute(values, 'step', siblings)  11.5 us
    ppermute x4, starting transfers between devices, fetch_own(): got = [lax.ppermute(values, both_axes, perm) for perm in fetch_perms]  10.9 us
    ppermute x33, starting transfers between devices, to_sibling(): return lax.ppermute(values, 'step', siblings)  10.5 us
  transfers between devices with their start and end apart: 63, of which 26 were waited for; matrix products, arithmetic and copies ran while one was open for 1% of the time, Pallas kernels for 50%

profile of v6, /device:TPU:9, one launch (start us, length us, event | category | flops | bytes accessed | tf_op | source)
XLA Modules:
  0.0 389.8 jit_solution(9886557096965673908)
XLA Ops:
  17.3 6.7 %down.1 = (bf16[3328,256]{1,0:T(8,128)(2,1)S(1)}, bf16[256,3328]{1,0:T(8,128)(2,1)S(1)}) custom-call(f32[800,3200]{1,0:T(8,128)} %refs_6_.1, bf16[160,800]{1,0:T(8,128)(2,1)S(1)} %pad_maximum_fusion.2.refs_1_), custom_call_target="tpu_custom_call" | custom-call | flops 7699999744 | bytes 1024 | tf_op jit(solution)/shard_map/down/pallas_call | solution.py:452
  28.3 5.5 %collective-permute-start.5 = (f32[8,81,96]{2,1,0:T(8,128)S(1)}, f32[8,81,96]{2,1,0:T(8,128)S(1)}, u32[]{:S(2)}, u32[]{:S(2)}) collective-permute-start(f32[8,81,96]{2,1,0:T(8,128)S(1)} %fusion.7), channel_id=1, source_target_pairs={{0,0},{4,1},{1,2},{5,3},{2,4},{6,5},{3,6},{7,7},{8,8},{12,9},{9,10... | collective-permute-start | bytes 746504 | tf_op jit(solution)/shard_map/ppermute | solution.py:869
  33.8 6.5 %up.1.refs_10_.refs_8_.refs_22_ = bf16[1664,3328]{1,0:T(8,128)(2,1)S(1)} custom-call(f32[800,3200]{1,0:T(8,128)} %bitcast.80), custom_call_target="tpu_custom_call" | custom-call | flops 7699999744 | bytes 1024 | tf_op jit(solution)/shard_map/up/pallas_call | solution.py:452
  48.4 8.0 %feed.8 = (f32[192,128]{1,0:T(8,128)S(1)}, f32[96,128]{1,0:T(8,128)S(1)}, f32[96,896]{1,0:T(8,128)}, f32[8,896]{1,0:T(8,128)S(1)}, f32[192,896]{1,0:T(8,128)}, /...) custom-call(s32[8]{0:T(128)S(1)} %stack.31.refs_0_.refs_5_.refs_6_, ...), custom_call_target="tpu_custom_call" | custom-call | flops 9349999616 | bytes 1024 | tf_op jit(solution)/shard_map/feed/pallas_call | solution.py:452
  63.4 8.0 %feed.9 = (f32[192,128]{1,0:T(8,128)S(1)}, f32[96,128]{1,0:T(8,128)S(1)}, f32[96,896]{1,0:T(8,128)}, f32[8,896]{1,0:T(8,128)S(1)}, f32[192,896]{1,0:T(8,128)}, /...) custom-call(s32[8]{0:T(128)S(1)} %stack.31.refs_0_.refs_5_.refs_6_, ...), custom_call_target="tpu_custom_call", output_to_operand_aliasing={{6}: (13, {}), {7}: (14, {})} | custom-call | flops 9349999616 | bytes 1024 | tf_op jit(solution)/shard_map/feed/pallas_call | solution.py:452
  78.4 7.3 %feed.10 = (f32[192,128]{1,0:T(8,128)S(1)}, f32[96,128]{1,0:T(8,128)S(1)}, f32[96,896]{1,0:T(8,128)S(1)}, f32[8,896]{1,0:T(8,128)S(1)}, f32[192,896]{1,0:T(8,128...) custom-call(s32[8]{0:T(128)S(1)} %stack.31.refs_0_.refs_5_.refs_6_, ...), custom_call_target="tpu_custom_call", output_to_operand_aliasing={{6}: (13, {}), {7}: (14, {})} | custom-call | flops 9349999616 | bytes 1024 | tf_op jit(solution)/shard_map/feed/pallas_call | solution.py:452
  92.8 7.3 %feed.11 = (f32[192,128]{1,0:T(8,128)S(1)}, f32[96,128]{1,0:T(8,128)S(1)}, f32[96,896]{1,0:T(8,128)S(1)}, f32[8,896]{1,0:T(8,128)S(1)}, f32[192,896]{1,0:T(8,128...) custom-call(s32[8]{0:T(128)S(1)} %stack.31.refs_0_.refs_5_.refs_6_, ...), custom_call_target="tpu_custom_call", output_to_operand_aliasing={{6}: (13, {}), {7}: (14, {})} | custom-call | flops 9349999616 | bytes 1024 | tf_op jit(solution)/shard_map/feed/pallas_call | solution.py:452
  101.4 4.5 %mix.12 = (f32[192,896]{1,0:T(8,128)S(1)}, f32[8,896]{1,0:T(8,128)S(1)}, f32[192,128]{1,0:T(8,128)S(1)}, f32[9,32,896]{2,1,0:T(8,128)}, f32[768,256]{1,0:T(8,128)}, /*index=5*/f32[24,32,896]{2,1,0:T(8,128)}) custom-call(s32[8]{0:T(128)S(1)} %stack.31.refs_0_.refs_5_.refs_6_, ...), custom_call_target="tpu_custom_call", output_to_operand_aliasing={{4}: (13, {}), {5}: (14, {})} | custom-call | flops 4950000128 | bytes 1024 | tf_op jit(solution)/shard_map/mix/pallas_call | solution.py:452
  107.2 7.3 %feed.12 = (f32[192,128]{1,0:T(8,128)S(1)}, f32[96,128]{1,0:T(8,128)S(1)}, f32[96,896]{1,0:T(8,128)S(1)}, f32[8,896]{1,0:T(8,128)S(1)}, f32[192,896]{1,0:T(8,128...) custom-call(s32[8]{0:T(128)S(1)} %stack.31.refs_0_.refs_5_.refs_6_, ...), custom_call_target="tpu_custom_call", output_to_operand_aliasing={{6}: (13, {}), {7}: (14, {})} | custom-call | flops 9349999616 | bytes 1024 | tf_op jit(solution)/shard_map/feed/pallas_call | solution.py:452
  115.8 4.8 %mix.13 = (f32[192,896]{1,0:T(8,128)S(1)}, f32[8,896]{1,0:T(8,128)S(1)}, f32[192,128]{1,0:T(8,128)S(1)}, f32[9,32,896]{2,1,0:T(8,128)}, f32[768,256]{1,0:T(8,128)}, /*index=5*/f32[24,32,896]{2,1,0:T(8,128)}) custom-call(s32[8]{0:T(128)S(1)} %stack.31.refs_0_.refs_5_.refs_6_, ...), custom_call_target="tpu_custom_call", output_to_operand_aliasing={{4}: (13, {}), {5}: (14, {})} | custom-call | flops 4950000128 | bytes 1024 | tf_op jit(solution)/shard_map/mix/pallas_call | solution.py:452
  121.8 7.3 %feed.13 = (f32[192,128]{1,0:T(8,128)S(1)}, f32[96,128]{1,0:T(8,128)S(1)}, f32[96,896]{1,0:T(8,128)S(1)}, f32[8,896]{1,0:T(8,128)S(1)}, f32[192,896]{1,0:T(8,128...) custom-call(s32[8]{0:T(128)S(1)} %stack.31.refs_0_.refs_5_.refs_6_, ...), custom_call_target="tpu_custom_call", output_to_operand_aliasing={{6}: (13, {}), {7}: (14, {})} | custom-call | flops 9349999616 | bytes 1024 | tf_op jit(solution)/shard_map/feed/pallas_call | solution.py:452
  136.1 7.3 %feed.14 = (f32[192,128]{1,0:T(8,128)S(1)}, f32[96,128]{1,0:T(8,128)S(1)}, f32[96,896]{1,0:T(8,128)S(1)}, f32[8,896]{1,0:T(8,128)S(1)}, f32[192,896]{1,0:T(8,128...) custom-call(s32[8]{0:T(128)S(1)} %stack.31.refs_0_.refs_5_.refs_6_, ...), custom_call_target="tpu_custom_call", output_to_operand_aliasing={{6}: (13, {}), {7}: (14, {})} | custom-call | flops 9349999616 | bytes 1024 | tf_op jit(solution)/shard_map/feed/pallas_call | solution.py:452
  150.4 7.9 %feed.15 = (f32[192,128]{1,0:T(8,128)}, f32[96,128]{1,0:T(8,128)}, f32[96,896]{1,0:T(8,128)S(1)}, f32[8,896]{1,0:T(8,128)S(1)}, f32[192,896]{1,0:T(8,128)}, /*in...) custom-call(s32[8]{0:T(128)S(1)} %stack.31.refs_0_.refs_5_.refs_6_, ...), custom_call_target="tpu_custom_call", output_to_operand_aliasing={{6}: (13, {}), {7}: (14, {})} | custom-call | flops 9349999616 | bytes 1024 | tf_op jit(solution)/shard_map/feed/pallas_call | solution.py:452
  159.9 7.2 %back.9 = (f32[192,896]{1,0:T(8,128)S(1)}, bf16[384,3328]{1,0:T(8,128)(2,1)S(1)}, f32[192,896]{1,0:T(8,128)S(1)}, f32[104,896]{1,0:T(8,128)S(1)}, f32[768,128]{1,0:T(8,128)}) custom-call(s32[8]{0:T(128)S(1)} %stack.31.refs_0_.refs_5_.refs_6_, f32[192,128]{1,0:T(8,128)S(1)} %get-tuple-element.337.refs_12_.refs_8_.refs_1_, ...), custom_call_target="tpu_custom_call" | custom-call | flops 8249999872 | bytes 1024 | tf_op jit(solution)/shard_map/back/pallas_call | solution.py:452
  172.6 12.3 %back.10 = (f32[192,128]{1,0:T(8,128)}, f32[192,128]{1,0:T(8,128)S(1)}, f32[56,896]{1,0:T(8,128)S(1)}, f32[256,96]{1,0:T(8,128)S(1)}, f32[768,896]{1,0:T(8,128)}...) custom-call(s32[8]{0:T(128)S(1)} %stack.31.refs_0_.refs_5_.refs_6_, ...), custom_call_target="tpu_custom_call", output_to_operand_aliasing={{9}: (23, {})} | custom-call | flops 15950000128 | bytes 1024 | tf_op jit(solution)/shard_map/back/pallas_call | solution.py:452
  199.7 12.5 %back.11 = (f32[192,128]{1,0:T(8,128)}, f32[192,128]{1,0:T(8,128)S(1)}, f32[56,896]{1,0:T(8,128)S(1)}, f32[256,96]{1,0:T(8,128)S(1)}, f32[768,896]{1,0:T(8,128)}...) custom-call(s32[8]{0:T(128)S(1)} %stack.31.refs_0_.refs_5_.refs_6_, ...), custom_call_target="tpu_custom_call", output_to_operand_aliasing={{4}: (23, {}), {9}: (24, {})} | custom-call | flops 15950000128 | bytes 1024 | tf_op jit(solution)/shard_map/back/pallas_call | solution.py:452
  217.0 12.2 %back.12 = (f32[192,128]{1,0:T(8,128)}, f32[192,128]{1,0:T(8,128)S(1)}, f32[56,896]{1,0:T(8,128)S(1)}, f32[256,96]{1,0:T(8,128)S(1)}, f32[768,896]{1,0:T(8,128)}...) custom-call(s32[8]{0:T(128)S(1)} %stack.31.refs_0_.refs_5_.refs_6_, ...), custom_call_target="tpu_custom_call", output_to_operand_aliasing={{4}: (23, {}), {9}: (24, {})} | custom-call | flops 15950000128 | bytes 1024 | tf_op jit(solution)/shard_map/back/pallas_call | solution.py:452
  233.9 12.3 %back.13 = (f32[192,128]{1,0:T(8,128)}, f32[192,128]{1,0:T(8,128)S(1)}, f32[56,896]{1,0:T(8,128)S(1)}, f32[256,96]{1,0:T(8,128)S(1)}, f32[768,896]{1,0:T(8,128)}...) custom-call(s32[8]{0:T(128)S(1)} %stack.31.refs_0_.refs_5_.refs_6_, ...), custom_call_target="tpu_custom_call", output_to_operand_aliasing={{4}: (23, {}), {9}: (24, {})} | custom-call | flops 15950000128 | bytes 1024 | tf_op jit(solution)/shard_map/back/pallas_call | solution.py:452
  250.7 12.3 %back.14 = (f32[192,128]{1,0:T(8,128)}, f32[192,128]{1,0:T(8,128)S(1)}, f32[56,896]{1,0:T(8,128)S(1)}, f32[256,96]{1,0:T(8,128)S(1)}, f32[768,896]{1,0:T(8,128)}...) custom-call(s32[8]{0:T(128)S(1)} %stack.31.refs_0_.refs_5_.refs_6_, ...), custom_call_target="tpu_custom_call", output_to_operand_aliasing={{4}: (23, {}), {9}: (24, {})} | custom-call | flops 15950000128 | bytes 1024 | tf_op jit(solution)/shard_map/back/pallas_call | solution.py:452
  267.2 12.5 %back.15 = (f32[192,128]{1,0:T(8,128)}, f32[192,128]{1,0:T(8,128)S(1)}, f32[56,896]{1,0:T(8,128)S(1)}, f32[256,96]{1,0:T(8,128)S(1)}, f32[768,896]{1,0:T(8,128)}...) custom-call(s32[8]{0:T(128)S(1)} %stack.31.refs_0_.refs_5_.refs_6_, ...), custom_call_target="tpu_custom_call", output_to_operand_aliasing={{4}: (23, {}), {9}: (24, {})} | custom-call | flops 15950000128 | bytes 1024 | tf_op jit(solution)/shard_map/back/pallas_call | solution.py:452
  284.2 12.7 %back.16 = (f32[192,128]{1,0:T(8,128)}, f32[192,128]{1,0:T(8,128)S(1)}, f32[56,896]{1,0:T(8,128)S(1)}, f32[256,96]{1,0:T(8,128)S(1)}, f32[768,896]{1,0:T(8,128)}...) custom-call(s32[8]{0:T(128)S(1)} %stack.31.refs_0_.refs_5_.refs_6_, ...), custom_call_target="tpu_custom_call", output_to_operand_aliasing={{4}: (23, {}), {9}: (24, {})} | custom-call | flops 15950000128 | bytes 1024 | tf_op jit(solution)/shard_map/back/pallas_call | solution.py:452
  301.4 7.6 %back.17 = (f32[192,128]{1,0:T(8,128)}, f32[192,128]{1,0:T(8,128)}, f32[56,896]{1,0:T(8,128)S(1)}, f32[256,96]{1,0:T(8,128)S(1)}, f32[768,896]{1,0:T(8,128)}) custom-call(s32[8]{0:T(128)S(1)} %stack.31.refs_0_.refs_5_.refs_6_, f32[192,128]{1,0:T(8,128)S(1)} %get-tuple-element.337.refs_12_.refs_8_.refs_1_, ...), custom_call_target="tpu_custom_call", output_to_operand_aliasing={{4}: (17, {})} | custom-call | flops 7699999744 | bytes 1024 | tf_op jit(solution)/shard_map/back/pallas_call | solution.py:452
  313.8 15.7 %last.1 = (f32[160,896]{1,0:T(8,128)S(1)}, f32[160,896]{1,0:T(8,128)S(1)}, f32[80,1664]{1,0:T(8,128)S(1)}, f32[80,1664]{1,0:T(8,128)S(1)}) custom-call(s32[8]{0:T(128)S(1)} %stack.31.refs_0_.refs_5_.refs_6_, f32[768,128]{1,0:T(8,128)} %get-tuple-element.584.refs_1_, f32[768,256]{1,0:T(8,128)} %get-tuple-element.585.refs_2_, ...), custom_call_target="tpu_custom_call" | custom-call | flops 13200000000 | bytes 1024 | tf_op jit(solution)/shard_map/last/pallas_call | solution.py:452
  362.9 6.5 %all-to-all-start.1 = ((f32[8,88,96]{2,1,0:T(8,128)}), f32[8,88,96]{2,1,0:T(8,128)S(1)}, u32[]{:S(2)}, u32[]{:S(2)}) async-start(f32[8,88,96]{2,1,0:T(8,128)} %get-tuple-element.628), calls=%async_computation.1 | async-start | bytes 720896 | tf_op jit(solution)/shard_map/all_to_all | solution.py:1123
  (308 shorter events, 174.8 us)
Async XLA Ops:
  5.5 21.2 %collective-permute-start.1 = (f32[159,96]{1,0:T(8,128)S(1)}, f32[159,96]{1,0:T(8,128)S(1)}, u32[]{:S(2)}, u32[]{:S(2)}) collective-permute-start(f32[159,96]{1,0:T(8,128)S(1)} %pad_maximum_fusion.3), channel_id=1, source_target_pairs={{1,0},{5,1},{0,2},{4,3},{3,4},{7,5},{2,6},{6,7},{9,8},{13,9},{8,10... | collective-permute-start | bytes 183176 | tf_op jit(solution)/shard_map/ppermute | solution.py:869
  6.3 20.5 %collective-permute-start = (f32[159,96]{1,0:T(8,128)S(1)}, f32[159,96]{1,0:T(8,128)S(1)}, u32[]{:S(2)}, u32[]{:S(2)}) collective-permute-start(f32[159,96]{1,0:T(8,128)S(1)} %pad_maximum_fusion.3), channel_id=1, source_target_pairs={{0,0},{4,1},{1,2},{5,3},{2,4},{6,5},{3,6},{7,7},{8,8},{12,9},{9,10... | collective-permute-start | bytes 183176 | tf_op jit(solution)/shard_map/ppermute | solution.py:869
  11.3 16.2 %all-to-all-start = ((f32[8,81,96]{2,1,0:T(8,128)}), f32[8,81,96]{2,1,0:T(8,128)S(1)}, u32[]{:S(2)}, u32[]{:S(2)}) async-start(f32[8,81,96]{2,1,0:T(8,128)} %constant_dynamic-slice_fusion.1), calls=%async_computation | async-start | bytes 720896 | tf_op jit(solution)/shard_map/all_to_all | solution.py:882
  27.5 12.8 %collective-permute-start.2 = (f32[104,384]{1,0:T(8,128)S(1)}, f32[104,384]{1,0:T(8,128)S(1)}, u32[]{:S(2)}, u32[]{:S(2)}) collective-permute-start(f32[104,384]{1,0:T(8,128)S(1)} %get-tuple-element.349.refs_4_.refs_10_), channel_id=1, source_target_pairs={{0,4},{4,0},{8,12},{12,8},{16,20},{20,16},{24,28},{28,24},{1,5},{5... | collective-permute-start | bytes 479240 | tf_op jit(solution)/shard_map/ppermute | solution.py:863
  27.8 16.9 %collective-permute-start.6 = (f32[8,81,96]{2,1,0:T(8,128)S(1)}, f32[8,81,96]{2,1,0:T(8,128)S(1)}, u32[]{:S(2)}, u32[]{:S(2)}) collective-permute-start(f32[8,81,96]{2,1,0:T(8,128)S(1)} %fusion.7), channel_id=1, source_target_pairs={{1,0},{5,1},{0,2},{4,3},{3,4},{7,5},{2,6},{6,7},{9,8},{13,9},{8,10... | collective-permute-start | bytes 746504 | tf_op jit(solution)/shard_map/ppermute | solution.py:869
  28.3 18.2 %collective-permute-start.5 = (f32[8,81,96]{2,1,0:T(8,128)S(1)}, f32[8,81,96]{2,1,0:T(8,128)S(1)}, u32[]{:S(2)}, u32[]{:S(2)}) collective-permute-start(f32[8,81,96]{2,1,0:T(8,128)S(1)} %fusion.7), channel_id=1, source_target_pairs={{0,0},{4,1},{1,2},{5,3},{2,4},{6,5},{3,6},{7,7},{8,8},{12,9},{9,10... | collective-permute-start | bytes 746504 | tf_op jit(solution)/shard_map/ppermute | solution.py:869
  149.6 151.3 %collective-permute-start.37 = (f32[96,896]{1,0:T(8,128)}, f32[96,896]{1,0:T(8,128)}, u32[]{:S(2)}, u32[]{:S(2)}) collective-permute-start(f32[96,896]{1,0:T(8,128)} %get-tuple-element.566), channel_id=1, source_target_pairs={{0,4},{4,0},{8,12},{12,8},{16,20},{20,16},{24,28},{28,24},{1,5},{5... | collective-permute-start | bytes 1032200 | tf_op jit(solution)/shard_map/ppermute | solution.py:863
  149.7 134.5 %collective-permute-start.35 = (f32[96,896]{1,0:T(8,128)}, f32[96,896]{1,0:T(8,128)}, u32[]{:S(2)}, u32[]{:S(2)}) collective-permute-start(f32[96,896]{1,0:T(8,128)} %get-tuple-element.549), channel_id=1, source_target_pairs={{0,4},{4,0},{8,12},{12,8},{16,20},{20,16},{24,28},{28,24},{1,5},{5... | collective-permute-start | bytes 1032200 | tf_op jit(solution)/shard_map/ppermute | solution.py:863
  150.1 66.8 %collective-permute-start.27 = (f32[96,896]{1,0:T(8,128)S(1)}, f32[96,896]{1,0:T(8,128)S(1)}, u32[]{:S(2)}, u32[]{:S(2)}) collective-permute-start(f32[96,896]{1,0:T(8,128)S(1)} %get-tuple-element.473), channel_id=1, source_target_pairs={{0,4},{4,0},{8,12},{12,8},{16,20},{20,16},{24,28},{28,24},{1,5},{5... | collective-permute-start | bytes 1032200 | tf_op jit(solution)/shard_map/ppermute | solution.py:863
  158.4 13.8 %collective-permute-start.22 = (f32[96,896]{1,0:T(8,128)S(1)}, f32[96,896]{1,0:T(8,128)S(1)}, u32[]{:S(2)}, u32[]{:S(2)}) collective-permute-start(f32[96,896]{1,0:T(8,128)S(1)} %get-tuple-element.433), channel_id=1, source_target_pairs={{0,4},{4,0},{8,12},{12,8},{16,20},{20,16},{24,28},{28,24},{1,5},{5... | collective-permute-start | bytes 1032200 | tf_op jit(solution)/shard_map/ppermute | solution.py:863
  172.2 23.3 %collective-permute-start.24 = (f32[96,896]{1,0:T(8,128)S(1)}, f32[96,896]{1,0:T(8,128)S(1)}, u32[]{:S(2)}, u32[]{:S(2)}) collective-permute-start(f32[96,896]{1,0:T(8,128)S(1)} %get-tuple-element.451), channel_id=1, source_target_pairs={{0,4},{4,0},{8,12},{12,8},{16,20},{20,16},{24,28},{28,24},{1,5},{5... | collective-permute-start | bytes 1032200 | tf_op jit(solution)/shard_map/ppermute | solution.py:863
  186.3 13.3 %collective-permute-start.23 = (f32[104,896]{1,0:T(8,128)S(1)}, f32[104,896]{1,0:T(8,128)S(1)}, u32[]{:S(2)}, u32[]{:S(2)}) collective-permute-start(f32[104,896]{1,0:T(8,128)S(1)} %get-tuple-element.442.refs_5_.refs_4_), channel_id=1, source_target_pairs={{0,4},{4,0},{8,12},{12,8},{16,20},{20,16},{24,28},{28,24},{1,5},{5... | collective-permute-start | bytes 1118216 | tf_op jit(solution)/shard_map/ppermute | solution.py:863
  195.5 20.8 %collective-permute-start.25 = (f32[8,80,96]{2,1,0:T(8,128)S(1)}, f32[8,80,96]{2,1,0:T(8,128)S(1)}, u32[]{:S(2)}, u32[]{:S(2)}) collective-permute-start(f32[8,80,96]{2,1,0:T(8,128)S(1)} %copy-done.43), channel_id=1, source_target_pairs={{0,0},{1,4},{2,1},{3,5},{4,2},{5,6},{6,3},{7,7},{8,8},{9,12},{10,9... | collective-permute-start | bytes 737288 | tf_op jit(solution)/shard_map/ppermute | solution.py:995
  216.3 50.8 %collective-permute-start.33 = (f32[96,896]{1,0:T(8,128)S(1)}, f32[96,896]{1,0:T(8,128)S(1)}, u32[]{:S(2)}, u32[]{:S(2)}) collective-permute-start(f32[96,896]{1,0:T(8,128)S(1)} %get-tuple-element.530), channel_id=1, source_target_pairs={{0,4},{4,0},{8,12},{12,8},{16,20},{20,16},{24,28},{28,24},{1,5},{5... | collective-permute-start | bytes 1032200 | tf_op jit(solution)/shard_map/ppermute | solution.py:863
  216.9 16.8 %collective-permute-start.29 = (f32[96,896]{1,0:T(8,128)S(1)}, f32[96,896]{1,0:T(8,128)S(1)}, u32[]{:S(2)}, u32[]{:S(2)}) collective-permute-start(f32[96,896]{1,0:T(8,128)S(1)} %get-tuple-element.492), channel_id=1, source_target_pairs={{0,4},{4,0},{8,12},{12,8},{16,20},{20,16},{24,28},{28,24},{1,5},{5... | collective-permute-start | bytes 1032200 | tf_op jit(solution)/shard_map/ppermute | solution.py:863
  233.7 16.9 %collective-permute-start.31 = (f32[96,896]{1,0:T(8,128)S(1)}, f32[96,896]{1,0:T(8,128)S(1)}, u32[]{:S(2)}, u32[]{:S(2)}) collective-permute-start(f32[96,896]{1,0:T(8,128)S(1)} %get-tuple-element.511), channel_id=1, source_target_pairs={{0,4},{4,0},{8,12},{12,8},{16,20},{20,16},{24,28},{28,24},{1,5},{5... | collective-permute-start | bytes 1032200 | tf_op jit(solution)/shard_map/ppermute | solution.py:863
  311.1 19.9 %collective-permute-start.41 = (f32[2,200,400]{2,1,0:T(8,128)S(1)}, f32[2,200,400]{2,1,0:T(8,128)S(1)}, u32[]{:S(2)}, u32[]{:S(2)}) collective-permute-start(f32[2,200,400]{2,1,0:T(8,128)S(1)} %get-tuple-element.601), channel_id=1, source_target_pairs={{0,8},{4,12},{8,0},{12,4},{16,24},{20,28},{24,16},{28,20},{1,9},{5... | collective-permute-start | bytes 1920008 | tf_op jit(solution)/shard_map/ppermute | solution.py:1057
  312.6 19.5 %collective-permute-start.42 = (f32[2,200,400]{2,1,0:T(8,128)S(1)}, f32[2,200,400]{2,1,0:T(8,128)S(1)}, u32[]{:S(2)}, u32[]{:S(2)}) collective-permute-start(f32[2,200,400]{2,1,0:T(8,128)S(1)} %get-tuple-element.603), channel_id=1, source_target_pairs={{0,16},{4,20},{8,24},{12,28},{16,0},{20,4},{24,8},{28,12},{1,17},{... | collective-permute-start | bytes 1920008 | tf_op jit(solution)/shard_map/ppermute | solution.py:1057
  343.1 14.0 %collective-permute-start.44 = (f32[200,400]{1,0:T(8,128)S(1)}, f32[200,400]{1,0:T(8,128)S(1)}, u32[]{:S(2)}, u32[]{:S(2)}) collective-permute-start(f32[200,400]{1,0:T(8,128)S(1)} %get-tuple-element.609), channel_id=1, source_target_pairs={{0,16},{4,20},{8,24},{12,28},{16,0},{20,4},{24,8},{28,12},{1,17},{... | collective-permute-start | bytes 960008 | tf_op jit(solution)/shard_map/ppermute | solution.py:1057
  344.1 12.9 %collective-permute-start.45 = (f32[200,400]{1,0:T(8,128)S(1)}, f32[200,400]{1,0:T(8,128)S(1)}, u32[]{:S(2)}, u32[]{:S(2)}) collective-permute-start(f32[200,400]{1,0:T(8,128)S(1)} %get-tuple-element.611), channel_id=1, source_target_pairs={{0,8},{4,12},{8,0},{12,4},{16,24},{20,28},{24,16},{28,20},{1,9},{5... | collective-permute-start | bytes 960008 | tf_op jit(solution)/shard_map/ppermute | solution.py:1057
  352.9 16.5 %collective-permute-start.56 = (f32[40,896]{1,0:T(8,128)S(1)}, f32[40,896]{1,0:T(8,128)S(1)}, u32[]{:S(2)}, u32[]{:S(2)}) collective-permute-start(f32[40,896]{1,0:T(8,128)S(1)} %get-tuple-element.634.refs_1_), channel_id=1, source_target_pairs={{0,2},{1,3},{2,0},{3,1},{4,6},{5,7},{6,4},{7,5},{8,10},{9,11},{10,... | collective-permute-start | bytes 430088 | tf_op jit(solution)/shard_map/ppermute | solution.py:1057
  357.7 18.3 %collective-permute-start.54 = (f32[200,400]{1,0:T(8,128)S(1)}, f32[200,400]{1,0:T(8,128)S(1)}, u32[]{:S(2)}, u32[]{:S(2)}) collective-permute-start(f32[200,400]{1,0:T(8,128)S(1)} %get-tuple-element.630), channel_id=1, source_target_pairs={{0,1},{1,0},{2,3},{3,2},{4,5},{5,4},{6,7},{7,6},{8,9},{9,8},{10,11... | collective-permute-start | bytes 960008 | tf_op jit(solution)/shard_map/ppermute | solution.py:1057
  360.9 11.8 %collective-permute-start.55 = (f32[80,400]{1,0:T(8,128)S(1)}, f32[80,400]{1,0:T(8,128)S(1)}, u32[]{:S(2)}, u32[]{:S(2)}) collective-permute-start(f32[80,400]{1,0:T(8,128)S(1)} %get-tuple-element.631.refs_1_), channel_id=1, source_target_pairs={{0,2},{1,3},{2,0},{3,1},{4,6},{5,7},{6,4},{7,5},{8,10},{9,11},{10,... | collective-permute-start | bytes 384008 | tf_op jit(solution)/shard_map/ppermute | solution.py:1057
  362.9 14.7 %all-to-all-start.1 = ((f32[8,88,96]{2,1,0:T(8,128)}), f32[8,88,96]{2,1,0:T(8,128)S(1)}, u32[]{:S(2)}, u32[]{:S(2)}) async-start(f32[8,88,96]{2,1,0:T(8,128)} %get-tuple-element.628), calls=%async_computation.1 | async-start | bytes 720896 | tf_op jit(solution)/shard_map/all_to_all | solution.py:1123
  (83 other events, 544.1 us)
